TPU v7x, 32 devices: a whole 2x2x4 slice. The times are simulated.
32 devices in a mesh: groups: 2 (over y), rows: 16 (over z, x, core).
Axes of the slice: x: 2, y: 2, z: 4, core: 2. Of those that a mesh axis runs over, the one named last changes fastest.
Arguments:
- scene_map: bfloat16 [128, 128, 1024], P(('groups', 'rows')), parts along dimension 0, may hold values from -6 to 6
- reduce_kernel: bfloat16 [128, 8, 32], replicated, may hold values from -0.25 to 0.25
- reduce_bias: float32 [32], replicated, may hold values from -3 to 3
- spatial_kernel: bfloat16 [9, 32, 8, 32], replicated, may hold values from -0.1875 to 0.1875
- spatial_bias: float32 [32], replicated, may hold values from -3 to 3
- widen_kernel: bfloat16 [32, 8, 128], replicated, may hold values from -0.5 to 0.5
- widen_bias: float32 [128], replicated, may hold values from -3 to 3
- entry_kernel: bfloat16 [128, 8, 64], replicated, may hold values from -0.25 to 0.25
- entry_bias: float32 [64], replicated, may hold values from -3 to 3
- stride_kernel: bfloat16 [9, 64, 8, 64], replicated, may hold values from -0.125 to 0.125
- stride_bias: float32 [64], replicated, may hold values from -3 to 3
Outputs:
- section_three: bfloat16 [128, 128, 1024], P(('groups', 'rows')), parts along dimension 0
- section_four: bfloat16 [64, 64, 512], P(('groups', 'rows')), parts along dimension 0
There are 2 independent parts, one for each index of `groups`. A program takes and returns all parts, laid end to end along the dimension named above; an argument that names none is the same for every part. Nothing has to cross between parts.
All inputs are finite; a program needn't handle non-finite values.
Results may differ from a plain program's by a relative error of at most 0.0095.
Values may be sent and summed in bfloat16 or wider, within the bound.
No kernel may reach another device: no remote copies, remote signals or barrier semaphores. Data moves between devices by JAX's collectives and lax.ppermute only.
A program may use at most 192 MiB of HBM per device.

v0:
```python
import jax
import jax.numpy as jnp
import numpy as np
from jax import lax
from jax.sharding import PartitionSpec as P

ORIENT = 8


CYCLE_TAPS = [0, 1, 2, 5, 8, 7, 6, 3]


def extended_2(cells, sides, width):
    for axis, dim in sides:
        count = lax.axis_size(axis)
        ends = count - 1
        head = lax.slice_in_dim(cells, 0, width, axis=dim)
        tail = lax.slice_in_dim(cells, cells.shape[dim] - width, cells.shape[dim], axis=dim)
        cells = jnp.concatenate(
            [
                lax.ppermute(tail, axis, [(i, (i + 1) % count) for i in range(ends)]),
                cells,
                lax.ppermute(head, axis, [((i + 1) % count, i) for i in range(ends)]),
            ],
            axis=dim,
        )
    return cells


def passed_along(shard, axis, by):
    count = lax.axis_size(axis)
    pairs = [(i, i + by) for i in range(count) if 0 <= i + by < count]
    return lax.ppermute(shard, axis, pairs)


def turned_taps(turn_index):
    tap_table = np.arange(9)
    for cycle_pos in range(8):
        tap_table[CYCLE_TAPS[cycle_pos]] = CYCLE_TAPS[(cycle_pos - turn_index) % 8]
    return tap_table


def unfold_group(kernel):
    tap_count = kernel.shape[0]
    in_fields, orients, out_fields = (kernel.shape[1], kernel.shape[2], kernel.shape[3])
    turned = []
    for turn_index in range(orients):
        source = kernel[turned_taps(turn_index)] if tap_count == 9 else kernel
        turned.append(jnp.roll(source, turn_index, axis=2))
    stacked = jnp.stack(turned, axis=-1)
    return stacked.reshape(tap_count, in_fields * orients, out_fields * orients)


def bias_row(bias_vec):
    return jnp.repeat(bias_vec, ORIENT)


def pointwise(feature, weight):
    flattened = feature.reshape(-1, feature.shape[-1])
    product = jnp.dot(flattened, weight, preferred_element_type=jnp.float32)
    return product.reshape(feature.shape[:-1] + (weight.shape[-1],))


def convolve(feature, kernel_hwio, strides, padding):
    result = lax.conv_general_dilated(
        feature[None],
        kernel_hwio,
        strides,
        padding,
        dimension_numbers=("NHWC", "HWIO", "NHWC"),
        preferred_element_type=jnp.float32,
    )
    return result[0]


def stencil_rows(core_rows, above_row, below_row, weight):
    kernel_hwio = weight.reshape(3, 3, weight.shape[1], weight.shape[2])
    full_rows = jnp.concatenate([above_row, core_rows, below_row], 0)
    return convolve(full_rows, kernel_hwio, (1, 1), ((0, 0), (1, 1)))


def stride_rows(core_rows, above_row, weight):
    kernel_hwio = weight.reshape(3, 3, weight.shape[1], weight.shape[2])
    padded = jnp.concatenate([above_row, core_rows], 0)
    return convolve(padded, kernel_hwio, (2, 2), ((0, 0), (1, 0)))


def shards(
    scene_map,
    reduce_kernel,
    reduce_bias,
    spatial_kernel,
    spatial_bias,
    widen_kernel,
    widen_bias,
    entry_kernel,
    entry_bias,
    stride_kernel,
    stride_bias,
):
    w_reduce = unfold_group(reduce_kernel[None])[0]
    w_spatial = unfold_group(spatial_kernel)
    w_widen = unfold_group(widen_kernel[None])[0]
    w_entry = unfold_group(entry_kernel[None])[0]
    w_stride = unfold_group(stride_kernel)
    mid_own = jax.nn.relu(pointwise(scene_map, w_reduce) + bias_row(reduce_bias)).astype(
        jnp.bfloat16
    )
    extended = extended_2(mid_own, (("rows", 0),), 1)
    above_row, below_row = (extended[:1], extended[-1:])
    mid_two = jax.nn.relu(
        stencil_rows(mid_own, above_row, below_row, w_spatial) + bias_row(spatial_bias)
    ).astype(jnp.bfloat16)
    section_three = jax.nn.relu(
        scene_map.astype(jnp.float32) + pointwise(mid_two, w_widen) + bias_row(widen_bias)
    ).astype(jnp.bfloat16)
    mid_four = jax.nn.relu(pointwise(section_three, w_entry) + bias_row(entry_bias)).astype(
        jnp.bfloat16
    )
    above_four = passed_along(mid_four[-1:], "rows", 1)
    section_four = jax.nn.relu(
        stride_rows(mid_four, above_four, w_stride) + bias_row(stride_bias)
    ).astype(jnp.bfloat16)
    return (section_three, section_four)


def solution(mesh):
    in_specs = (P(("groups", "rows"), None, None), P(), P(), P(), P(), P(), P(), P(), P(), P(), P())
    out_specs = (P(("groups", "rows"), None, None), P(("groups", "rows"), None, None))
    return jax.shard_map(shards, mesh=mesh, in_specs=in_specs, out_specs=out_specs, check_vma=False)
```

profile of v0, /device:TPU:1, one launch (start us, length us, event | category | flops | bytes accessed | tf_op | source)
XLA Modules:
  0.0 402.7 jit_solution(13693639504847373233)
XLA Ops:
  7.4 11.7 %copy.51 = bf16[1,128,8,32,8]{4,3,2,1,0:T(8,128)(2,1)} copy(bf16[1,128,8,32,8]{1,3,2,4,0:T(8,128)(2,1)S(1)} %constant_dynamic-update-slice_fusion) | data formatting | bytes 1048576 | tf_op jit(solution)/shard_map/stack | solution.py:50
  19.1 12.6 %squeeze_reshape.9 = bf16[1024,256]{1,0:T(8,128)(2,1)S(1)} reshape(bf16[1,128,8,32,8]{4,3,2,1,0:T(8,128)(2,1)} %copy.51) | data formatting | bytes 1048576 | tf_op jit(solution)/shard_map/squeeze;reshape | solution.py:101
  34.5 2.0 collective-permute-start.1
  36.5 4.5 %collective-permute-start = (bf16[1,128,256]{2,1,0:T(8,128)(2,1)}, bf16[1,128,256]{2,1,0:T(8,128)(2,1)}, u32[]{:S(2)}, u32[]{:S(2)}) collective-permute-start(bf16[1,128,256]{2,1,0:T(8,128)(2,1)} %get-tuple-element.8), channel_id=1, source_target_pairs={{0,1},{1,2},{2,3},{3,4},{4,5},{5,6},{6,7},{7,8},{8,9},{9,10},{10,1... | collective-permute-start | bytes 196616 | tf_op jit(solution)/shard_map/ppermute | solution.py:21
  55.9 1.8 gather_fusion.8
  61.0 1.8 gather_fusion.10
  66.6 1.8 gather_fusion.12
  75.6 2.2 slice.473
  77.8 2.7 slice.472
  86.4 6.0 %copy.58 = bf16[1,32,8,128,8]{4,3,2,1,0:T(8,128)(2,1)} copy(bf16[1,32,8,128,8]{3,2,1,4,0:T(8,128)(2,1)S(1)} %constant_dynamic-update-slice_fusion.8) | data formatting | bytes 1048576 | tf_op jit(solution)/shard_map/stack | solution.py:50
  92.4 13.6 %reshape.191 = bf16[256,1024,1]{1,0,2:T(8,128)(2,1)} reshape(bf16[1,32,8,128,8]{4,3,2,1,0:T(8,128)(2,1)} %copy.58) | data formatting | bytes 1048576 | tf_op jit(solution)/shard_map/squeeze;reshape | solution.py:103
  119.2 15.4 %copy.55 = bf16[9,32,8,32,8]{4,3,2,1,0:T(8,128)(2,1)} copy(bf16[9,32,8,32,8]{3,2,1,0,4:T(8,128)(2,1)} %fusion.26) | data formatting | bytes 2359296 | tf_op jit(solution)/shard_map/stack | solution.py:50
  134.6 27.5 %reshape_reshape.6 = bf16[3,3,256,256]{3,2,1,0:T(8,128)(2,1)} reshape(bf16[9,32,8,32,8]{4,3,2,1,0:T(8,128)(2,1)} %copy.55) | data formatting | bytes 2359296 | tf_op jit(solution)/shard_map/reshape;reshape | solution.py:77
  166.4 1.8 fusion.6
  168.3 1.9 fusion.7
  173.8 1.8 fusion.10
  175.7 1.8 fusion.11
  178.5 22.4 %copy.59 = bf16[1,128,8,64,8]{4,3,2,1,0:T(8,128)(2,1)} copy(bf16[1,128,8,64,8]{1,3,2,4,0:T(8,128)(2,1)S(1)} %fusion.44) | data formatting | bytes 2097152 | tf_op jit(solution)/shard_map/stack | solution.py:50
  201.0 24.6 %reshape.192 = bf16[1024,512,1]{1,0,2:T(8,128)(2,1)S(1)} reshape(bf16[1,128,8,64,8]{4,3,2,1,0:T(8,128)(2,1)} %copy.59) | data formatting | bytes 2097152 | tf_op jit(solution)/shard_map/squeeze;reshape | solution.py:104
  230.9 2.4 collective-permute-start.2
  233.3 1.8 fusion.12
  235.1 54.9 %copy.62 = bf16[9,64,8,64,8]{4,3,2,1,0:T(8,128)(2,1)} copy(bf16[9,64,8,64,8]{3,2,1,0,4:T(8,128)(2,1)} %fusion.12) | data formatting | bytes 9437184 | tf_op jit(solution)/shard_map/stack | solution.py:50
  290.0 107.0 %reshape_reshape.7 = bf16[3,3,512,512]{3,2,1,0:T(8,128)(2,1)} reshape(bf16[9,64,8,64,8]{4,3,2,1,0:T(8,128)(2,1)} %copy.62) | data formatting | bytes 9437184 | tf_op jit(solution)/shard_map/reshape;reshape | solution.py:83
  398.3 3.3 convolution_select_fusion.1
  (282 shorter events, 73.7 us)
Async XLA Ops:
  0.6 55.3 %copy-start = (bf16[9,64,8,64]{3,2,1,0:T(8,128)(2,1)S(1)}, bf16[9,64,8,64]{3,2,1,0:T(8,128)(2,1)}, u32[]{:S(2)}) copy-start(bf16[9,64,8,64]{3,2,1,0:T(8,128)(2,1)} %param.52) | copy-start | bytes 1769476
  33.4 7.6 %copy-start.4 = (bf16[32,8,128]{2,1,0:T(8,128)(2,1)S(1)}, bf16[32,8,128]{2,1,0:T(8,128)(2,1)}, u32[]{:S(2)}) copy-start(bf16[32,8,128]{2,1,0:T(8,128)(2,1)} %param.48) | copy-start | bytes 196612
  33.8 12.4 %copy-start.69 = (s32[9]{0:T(128)S(1)}, s32[9]{0:T(128)}, u32[]{:S(2)}) copy-start(s32[9]{0:T(128)} %constant.60) | copy-start | bytes 112
  33.8 12.4 %copy-start.72 = (s32[9]{0:T(128)S(1)}, s32[9]{0:T(128)}, u32[]{:S(2)}) copy-start(s32[9]{0:T(128)} %constant.59) | copy-start | bytes 112
  33.8 12.4 %copy-start.2 = (bf16[9,32,8,32]{3,2,1,0:T(8,128)(2,1)S(1)}, bf16[9,32,8,32]{3,2,1,0:T(8,128)(2,1)}, u32[]{:S(2)}) copy-start(bf16[9,32,8,32]{3,2,1,0:T(8,128)(2,1)} %param.46) | copy-start | bytes 442372
  33.9 12.3 %copy-start.23 = (bf16[4,128,256]{2,1,0:T(8,128)(2,1)}, bf16[4,128,256]{2,1,0:T(8,128)(2,1)S(1)}, u32[]{:S(2)}) copy-start(bf16[4,128,256]{2,1,0:T(8,128)(2,1)S(1)} %maximum_convert_fusion.1) | copy-start | bytes 786436
  34.5 191.2 %collective-permute-start.1 = (bf16[1,128,256]{2,1,0:T(8,128)(2,1)}, bf16[1,128,256]{2,1,0:T(8,128)(2,1)}, u32[]{:S(2)}, u32[]{:S(2)}) collective-permute-start(bf16[1,128,256]{2,1,0:T(8,128)(2,1)} %get-tuple-element.9), channel_id=1, source_target_pairs={{1,0},{2,1},{3,2},{4,3},{5,4},{6,5},{7,6},{8,7},{9,8},{10,9},{11,1... | collective-permute-start | bytes 196616 | tf_op jit(solution)/shard_map/ppermute | solution.py:23
  36.5 189.3 %collective-permute-start = (bf16[1,128,256]{2,1,0:T(8,128)(2,1)}, bf16[1,128,256]{2,1,0:T(8,128)(2,1)}, u32[]{:S(2)}, u32[]{:S(2)}) collective-permute-start(bf16[1,128,256]{2,1,0:T(8,128)(2,1)} %get-tuple-element.8), channel_id=1, source_target_pairs={{0,1},{1,2},{2,3},{3,4},{4,5},{5,6},{6,7},{7,8},{8,9},{9,10},{10,1... | collective-permute-start | bytes 196616 | tf_op jit(solution)/shard_map/ppermute | solution.py:21
  80.5 5.4 %copy-start.30 = (bf16[1,32,8,128,8]{3,2,1,4,0:T(8,128)(2,1)S(1)}, bf16[1,32,8,128,8]{3,2,1,4,0:T(8,128)(2,1)}, u32[]{:S(2)}) copy-start(bf16[1,32,8,128,8]{3,2,1,4,0:T(8,128)(2,1)} %constant_dynamic-update-slice_fusion.15) | copy-start | bytes 1572868
  80.5 5.4 %copy-start.42 = (bf16[1,32,7,128]{3,2,1,0:T(8,128)(2,1)S(1)}, bf16[1,32,7,128]{3,2,1,0:T(8,128)(2,1)}, u32[]{:S(2)}) copy-start(bf16[1,32,7,128]{3,2,1,0:T(8,128)(2,1)} %get-tuple-element.39) | copy-start | bytes 172036
  80.5 5.4 %copy-start.58 = (bf16[1,32,1,128]{3,2,1,0:T(2,128)(2,1)S(1)}, bf16[1,32,1,128]{3,2,1,0:T(2,128)(2,1)}, u32[]{:S(2)}) copy-start(bf16[1,32,1,128]{3,2,1,0:T(2,128)(2,1)} %get-tuple-element.41) | copy-start | bytes 24580
  80.5 5.4 %copy-start.43 = (bf16[1,32,6,128]{3,2,1,0:T(8,128)(2,1)S(1)}, bf16[1,32,6,128]{3,2,1,0:T(8,128)(2,1)}, u32[]{:S(2)}) copy-start(bf16[1,32,6,128]{3,2,1,0:T(8,128)(2,1)} %get-tuple-element.43) | copy-start | bytes 147460
  80.5 5.4 %copy-start.59 = (bf16[1,32,2,128]{3,2,1,0:T(2,128)(2,1)S(1)}, bf16[1,32,2,128]{3,2,1,0:T(2,128)(2,1)}, u32[]{:S(2)}) copy-start(bf16[1,32,2,128]{3,2,1,0:T(2,128)(2,1)} %get-tuple-element.45) | copy-start | bytes 49156
  80.5 5.5 %copy-start.44 = (bf16[1,32,5,128]{3,2,1,0:T(8,128)(2,1)S(1)}, bf16[1,32,5,128]{3,2,1,0:T(8,128)(2,1)}, u32[]{:S(2)}) copy-start(bf16[1,32,5,128]{3,2,1,0:T(8,128)(2,1)} %get-tuple-element.47) | copy-start | bytes 122884
  80.5 5.5 %copy-start.50 = (bf16[1,32,3,128]{3,2,1,0:T(4,128)(2,1)S(1)}, bf16[1,32,3,128]{3,2,1,0:T(4,128)(2,1)}, u32[]{:S(2)}) copy-start(bf16[1,32,3,128]{3,2,1,0:T(4,128)(2,1)} %get-tuple-element.49) | copy-start | bytes 73732
  81.2 4.9 %copy-start.49 = (bf16[1,32,3,128]{3,2,1,0:T(4,128)(2,1)S(1)}, bf16[1,32,3,128]{3,2,1,0:T(4,128)(2,1)}, u32[]{:S(2)}) copy-start(bf16[1,32,3,128]{3,2,1,0:T(4,128)(2,1)} %get-tuple-element.48) | copy-start | bytes 73732
  92.4 16.6 %copy-start.17 = (bf16[9,32,8,32]{3,2,1,0:T(8,128)(2,1)S(1)}, bf16[9,32,8,32]{3,2,1,0:T(8,128)(2,1)}, u32[]{:S(2)}) copy-start(bf16[9,32,8,32]{3,2,1,0:T(8,128)(2,1)} %gather_fusion) | copy-start | bytes 442372
  92.4 17.6 %copy-start.16 = (bf16[9,32,8,32]{3,2,1,0:T(8,128)(2,1)S(1)}, bf16[9,32,8,32]{3,2,1,0:T(8,128)(2,1)}, u32[]{:S(2)}) copy-start(bf16[9,32,8,32]{3,2,1,0:T(8,128)(2,1)} %gather_fusion.2) | copy-start | bytes 442372
  134.6 27.5 %copy-start.65 = (f32[32]{0:T(128)S(1)}, f32[32]{0:T(128)}, u32[]{:S(2)}) copy-start(f32[32]{0:T(128)} %param.47) | copy-start | bytes 388
  134.6 28.2 %copy-start.8 = (bf16[9,64,8,64]{3,2,1,0:T(8,128)(2,1)S(1)}, bf16[9,64,8,64]{3,2,1,0:T(8,128)(2,1)}, u32[]{:S(2)}) copy-start(bf16[9,64,8,64]{3,2,1,0:T(8,128)(2,1)} %gather_fusion.8) | copy-start | bytes 1769476
  201.0 24.6 %copy-start.62 = (f32[64]{0:T(128)S(1)}, f32[64]{0:T(128)}, u32[]{:S(2)}) copy-start(f32[64]{0:T(128)} %param.51) | copy-start | bytes 772
  201.0 24.8 %copy-start.24 = (bf16[4,128,256]{2,1,0:T(8,128)(2,1)S(1)}, bf16[4,128,256]{2,1,0:T(8,128)(2,1)}, u32[]{:S(2)}) copy-start(bf16[4,128,256]{2,1,0:T(8,128)(2,1)} %copy-done.23) | copy-start | bytes 786436
  230.9 166.2 %collective-permute-start.2 = (bf16[1,128,512]{2,1,0:T(8,128)(2,1)S(1)}, bf16[1,128,512]{2,1,0:T(8,128)(2,1)S(1)}, u32[]{:S(2)}, u32[]{:S(2)}) collective-permute-start(bf16[1,128,512]{2,1,0:T(8,128)(2,1)S(1)} %slice.458), channel_id=1, source_target_pairs={{0,1},{1,2},{2,3},{3,4},{4,5},{5,6},{6,7},{7,8},{8,9},{9,10},{10,1... | collective-permute-start | bytes 393224 | tf_op jit(solution)/shard_map/ppermute | solution.py:33
  290.0 107.0 %copy-start.63 = (f32[64]{0:T(128)S(1)}, f32[64]{0:T(128)}, u32[]{:S(2)}) copy-start(f32[64]{0:T(128)} %param.53) | copy-start | bytes 772
  (57 other events, 131.1 us)
where the time goes:
time: 405 us; the launch traced here: 403 us
  local copies, waits for them, and re-layouts  362 us (89%)
  other arithmetic  23.1 us (6%)
  starting transfers between devices  8.82 us (2%)
  matrix products  7.05 us (2%)
    another operation x5, local copies, waits for them, and re-layouts, unfold_group(): stacked = jnp.stack(turned, axis=-1)  110 us
    another operation x1, local copies, waits for them, and re-layouts, stride_rows(): kernel_hwio = weight.reshape(3, 3, weight.shape[1], weight.shape[2])  107 us
    slice x43, local copies, waits for them, and re-layouts, unfold_group(): turned.append(jnp.roll(source, turn_index, axis=2))  30.3 us
    another operation x1, local copies, waits for them, and re-layouts, stencil_rows(): kernel_hwio = weight.reshape(3, 3, weight.shape[1], weight.shape[2])  27.5 us
    another operation x1, local copies, waits for them, and re-layouts, shards(): w_entry = unfold_group(entry_kernel[None])[0]  24.6 us
    gather x16, local copies, waits for them, and re-layouts, unfold_group(): source = kernel[turned_taps(turn_index)] if tap_count == 9 else kernel  20.8 us
    unnamed x30, other arithmetic  18.8 us
    another operation x1, local copies, waits for them, and re-layouts, shards(): w_widen = unfold_group(widen_kernel[None])[0]  13.6 us
  transfers between devices with their start and end apart: 3, of which 0 were waited for; matrix products, arithmetic and copies ran while one was open for 86% of the time, Pallas kernels for 0%

commit v1 on v0

v1 whole, which is shorter than its diff:
```python
import functools

import jax
import jax.numpy as jnp
from jax import lax
from jax.experimental import pallas as pl
from jax.experimental.pallas import tpu as pltpu
from jax.sharding import PartitionSpec as P

ORIENT = 8
CYCLE_TAPS = [0, 1, 2, 5, 8, 7, 6, 3]
BF16, F32 = jnp.bfloat16, jnp.float32
NT = (((1,), (1,)), ((), ()))


def back_tap(tap, turn):
    if tap == 4:
        return 4
    return CYCLE_TAPS[(CYCLE_TAPS.index(tap) - turn) % ORIENT]


def iota(shape, dim):
    return lax.broadcasted_iota(jnp.int32, shape, dim)


def dot(a, b):
    return jnp.dot(a, b, preferred_element_type=F32)


def dot_nt(a, b):
    return lax.dot_general(a, b, NT, preferred_element_type=F32)


def rows_rolled(x, by):
    by %= x.shape[0]
    if by == 0:
        return x
    return jnp.concatenate([x[x.shape[0] - by:], x[:x.shape[0] - by]], 0)


def spread(fields, first, width):
    return jnp.where((iota((fields, width), 1) + first) // ORIENT == iota((fields, width), 0), 1.0, 0.0).astype(BF16)


def turned(blocks, block):
    lane = iota((1, blocks.shape[1]), 1)
    for bit in (1, 2, 4):
        take = jnp.broadcast_to(lane & bit, blocks.shape) != 0
        blocks = jnp.where(take, rows_rolled(blocks, bit * block), blocks)
    return blocks


def bias_lanes(bias, hot):
    first = bias.astype(BF16)
    rest = bias - first.astype(F32)
    second = rest.astype(BF16)
    third = (rest - second.astype(F32)).astype(BF16)
    parts = [dot(jnp.broadcast_to(p, (16,) + p.shape[1:]), hot)[:1] for p in (first, second, third)]
    return parts[0] + parts[1] + parts[2]


def unfold_kernel(kr_ref, ks_ref, kw_ref, ke_ref, kt_ref,
                  wr_ref, ws_ref, ww_ref, we_ref, k2_ref,
                  ks_v, kt_v, flat_w, flat_s, flat_t, sem):
    copy_s = pltpu.make_async_copy(ks_ref, ks_v, sem.at[0])
    copy_t = pltpu.make_async_copy(kt_ref, kt_v, sem.at[1])
    copy_s.start()
    copy_t.start()
    in_f, mid, s4 = kr_ref.shape[2], kr_ref.shape[1], ke_ref.shape[1]
    wide = in_f * ORIENT
    kr = kr_ref[...].reshape(ORIENT * mid, in_f)
    ke = ke_ref[...].reshape(ORIENT * s4, in_f)
    back = lambda x, block: jnp.concatenate([x[(-r) % ORIENT * block:((-r) % ORIENT + 1) * block] for r in range(ORIENT)], 0)
    kr, ke = back(kr, mid), back(ke, s4)
    flat_w[...] = kw_ref[...].astype(F32).reshape(mid * ORIENT, in_f)
    kw = jnp.concatenate([flat_w[pl.ds(u, mid, stride=ORIENT), :] for u in range(ORIENT)], 0).astype(BF16)
    step = 256
    for first in range(0, wide, step):
        hot = spread(in_f, first, step)
        cols = pl.ds(first, step)
        wr_ref[:, cols] = turned(dot(kr, hot), mid).astype(BF16)
        ww_ref[:, cols] = turned(dot(kw, hot), mid).astype(BF16)
        we_ref[:, cols] = turned(dot(ke, hot), s4).astype(BF16)

    lane = iota((1, 128), 1)
    copy_s.wait()
    rows = mid * ORIENT
    for tap in range(9):
        flat_s[pl.ds(tap * rows, rows), :mid] = ks_v[tap].astype(F32).reshape(rows, mid)
    piece = lambda tap, u: flat_s[pl.ds(tap * rows + u % ORIENT, mid, stride=ORIENT), :]
    low = jnp.broadcast_to(lane < mid, (mid, 128))
    half = jnp.broadcast_to(lane < 2 * mid, (mid, 128))
    pairs = {}
    for tap in range(9):
        for u in range(ORIENT):
            pairs[tap, u] = jnp.where(low, piece(tap, u), pltpu.roll(piece(back_tap(tap, 1), u - 1), mid, 1))
    for tap in range(9):
        for u in range(ORIENT):
            quad = jnp.where(half, pairs[tap, u], pltpu.roll(pairs[back_tap(tap, 2), (u - 2) % ORIENT], 2 * mid, 1)).astype(BF16)
            ws_ref[pl.ds(tap * rows + u * mid, mid), :128] = quad
            ahead = back_tap(tap, -4)
            ws_ref[pl.ds(ahead * rows + (u + 4) % ORIENT * mid, mid), 128:] = quad

    copy_t.wait()
    rows_t = s4 * ORIENT
    for tap in range(9):
        flat_t[pl.ds(tap * rows_t, rows_t), :s4] = kt_v[tap].astype(F32).reshape(rows_t, s4)
    piece_t = lambda tap, u: flat_t[pl.ds(tap * rows_t + u % ORIENT, s4, stride=ORIENT), :]
    low_t = jnp.broadcast_to(lane < s4, (s4, 128))
    for tap in range(9):
        for u in range(ORIENT):
            pair = jnp.where(low_t, piece_t(tap, u), pltpu.roll(piece_t(back_tap(tap, 1), u - 1), s4, 1))
            k2_ref[pl.ds(tap * rows_t + u * s4, s4), :] = pair.astype(BF16)


def block_kernel(x_ref, dn_ref, up_ref, wr_ref, ws_ref, ww_ref, we_ref, k2_ref,
                 br_ref, bs_ref, bw_ref, be_ref, bt_ref,
                 three_ref, four_ref,
                 xs, mids, threes, fours, evens, sem):
    place, count = lax.axis_index("rows"), lax.axis_size("rows")
    cols = dn_ref.shape[0] // 2
    own = x_ref.shape[0]
    wide, mid = x_ref.shape[1], wr_ref.shape[0]
    s4 = we_ref.shape[0]
    strips = own // cols
    copies = [
        pltpu.make_async_copy(dn_ref, xs.at[pl.ds(0, 2 * cols)], sem.at[0]),
        pltpu.make_async_copy(x_ref, xs.at[pl.ds(2 * cols, own)], sem.at[1]),
        pltpu.make_async_copy(up_ref, xs.at[pl.ds(2 * cols + own, cols)], sem.at[2]),
    ]
    for copy in copies:
        copy.start()
    tile = lambda fields, width: jnp.where(iota((fields, width), 1) % fields == iota((fields, width), 0), 1.0, 0.0).astype(BF16)
    b_red = bias_lanes(br_ref[...], tile(br_ref.shape[1], mid))
    b_mid = bias_lanes(bs_ref[...], tile(bs_ref.shape[1], mid))
    b_ent = bias_lanes(be_ref[...], tile(be_ref.shape[1], s4))
    b_str = bias_lanes(bt_ref[...], tile(bt_ref.shape[1], s4))
    b_wid = bias_lanes(bw_ref[...], spread(bw_ref.shape[1], 0, wide))
    not_first = jnp.where(place == 0, 0.0, 1.0)
    not_last = jnp.where(place == count - 1, 0.0, 1.0)
    for copy in copies:
        copy.wait()

    col = iota((cols, mid), 0)
    for row in range(strips + 3):
        y = dot_nt(xs[pl.ds(row * cols, cols), :], wr_ref[...]) + b_red
        y = jnp.maximum(y, 0.0)
        if row < 2:
            y = y * not_first
        if row == strips + 2:
            y = y * not_last
        at = pl.ds(row * cols, cols)
        mids[at, :mid] = jnp.where(col == 0, 0.0, pltpu.roll(y, 1, 0)).astype(BF16)
        mids[at, mid:2 * mid] = y.astype(BF16)
        mids[at, 2 * mid:] = jnp.where(col == cols - 1, 0.0, pltpu.roll(y, cols - 1, 0)).astype(BF16)

    for row in range(strips + 1):
        at = pl.ds(row * cols, cols)
        acc = b_mid
        for dy in range(3):
            acc = acc + dot(mids[pl.ds((row + dy) * cols, cols), :], ws_ref[pl.ds(dy * 3 * mid, 3 * mid), :])
        two = jnp.maximum(acc, 0.0).astype(BF16)
        for first in range(0, wide, 256):
            part = slice(first, first + 256)
            z = xs[pl.ds((row + 1) * cols, cols), part].astype(F32) + dot(two, ww_ref[:, part]) + b_wid[:, part]
            threes[at, part] = jnp.maximum(z, 0.0).astype(BF16)
        f = jnp.maximum(dot_nt(threes[at, :], we_ref[...]) + b_ent, 0.0)
        if row == 0:
            f = f * not_first
        for g in range(s4 // 128):
            fours[g, at, :] = f[:, g * 128:(g + 1) * 128]
    out = pltpu.make_async_copy(threes.at[pl.ds(cols, own)], three_ref, sem.at[3])
    out.start()

    half = cols // 2
    col = iota((half, 128), 0)
    for row in range(strips + 1):
        at = pl.ds(row * half, half)
        for g in range(s4 // 128):
            even = fours[g, pl.ds(row * cols, half, stride=2), :]
            odd = fours[g, pl.ds(row * cols + 1, half, stride=2), :]
            evens[at, pl.ds(g * 128, 128)] = jnp.where(col == 0, 0.0, pltpu.roll(odd, 1, 0)).astype(BF16)
            evens[at, pl.ds(s4 + g * 128, 128)] = even.astype(BF16)
            evens[at, pl.ds(2 * s4 + g * 128, 128)] = odd.astype(BF16)

    def filter_tile(tap, pair):
        halves = []
        for j in (2 * pair, 2 * pair + 1):
            source = back_tap(tap, 2 * j)
            halves.append(rows_rolled(k2_ref[pl.ds(source * s4, s4), :], 128 * j))
        return jnp.concatenate(halves, 1)

    results = []
    for pair in range(s4 // 256):
        acc = b_str[:, pair * 256:(pair + 1) * 256]
        for tap in range(9):
            dy, dx = divmod(tap, 3)
            lhs = jnp.concatenate(
                [evens[pl.ds((2 * q + dy) * half, half), dx * s4:(dx + 1) * s4] for q in range(strips // 2)], 0)
            acc = acc + dot(lhs, filter_tile(tap, pair))
        results.append(jnp.maximum(acc, 0.0).astype(BF16))
    result = jnp.concatenate(results, 1)
    fields = s4 // ORIENT
    a, b = iota((s4, s4), 0), iota((s4, s4), 1)
    order = jnp.where(b == (a % fields) * ORIENT + a // fields, 1.0, 0.0).astype(BF16)
    four_ref[...] = dot(result, order).astype(BF16)
    out.wait()


def shards(scene_map, reduce_kernel, reduce_bias, spatial_kernel, spatial_bias, widen_kernel, widen_bias,
           entry_kernel, entry_bias, stride_kernel, stride_bias):
    count = lax.axis_size("rows")
    down = lax.ppermute(scene_map[-2:], "rows", [(i, i + 1) for i in range(count - 1)])
    up = lax.ppermute(scene_map[:1], "rows", [(i + 1, i) for i in range(count - 1)])

    strips, cols, wide = scene_map.shape
    mid_f, s4_f = reduce_kernel.shape[2], entry_kernel.shape[2]
    mid, s4 = mid_f * ORIENT, s4_f * ORIENT
    any_spec = pl.BlockSpec(memory_space=pl.ANY)
    vmem = pl.BlockSpec(memory_space=pltpu.VMEM)
    dma = pltpu.SemaphoreType.DMA
    filters = pl.pallas_call(
        unfold_kernel,
        out_shape=[
            pltpu.VMEM((mid, wide), BF16),
            pltpu.VMEM((9 * mid, mid), BF16),
            pltpu.VMEM((mid, wide), BF16),
            pltpu.VMEM((s4, wide), BF16),
            pltpu.VMEM((9 * s4, 128), BF16),
        ],
        in_specs=[vmem, any_spec, vmem, vmem, any_spec],
        out_specs=[vmem] * 5,
        scratch_shapes=[
            pltpu.VMEM(spatial_kernel.shape, BF16),
            pltpu.VMEM(stride_kernel.shape, BF16),
            pltpu.VMEM((mid, wide // ORIENT), F32),
            pltpu.VMEM((9 * mid, 128), F32),
            pltpu.VMEM((9 * s4, 128), F32),
            dma((2,)),
        ],
        compiler_params=pltpu.CompilerParams(vmem_limit_bytes=24 << 20),
        name="unfold",
    )(reduce_kernel.transpose(1, 2, 0), spatial_kernel, widen_kernel, entry_kernel.transpose(1, 2, 0), stride_kernel)

    flat = lambda x: x.reshape(-1, wide)
    three, four = pl.pallas_call(
        block_kernel,
        out_shape=[
            jax.ShapeDtypeStruct((strips * cols, wide), BF16),
            jax.ShapeDtypeStruct((strips // 2 * (cols // 2), s4), BF16),
        ],
        in_specs=[any_spec] * 3 + [vmem] * 10,
        out_specs=[any_spec, vmem],
        scratch_shapes=[
            pltpu.VMEM(((strips + 3) * cols, wide), BF16),
            pltpu.VMEM(((strips + 3) * cols, 3 * mid), BF16),
            pltpu.VMEM(((strips + 1) * cols, wide), BF16),
            pltpu.VMEM((s4 // 128, (strips + 1) * cols, 128), F32),
            pltpu.VMEM(((strips + 1) * (cols // 2), 3 * s4), BF16),
            dma((4,)),
        ],
        compiler_params=pltpu.CompilerParams(vmem_limit_bytes=32 << 20),
        name="block",
    )(flat(scene_map), flat(down), flat(up), *filters,
      reduce_bias[None], spatial_bias[None], widen_bias[None], entry_bias[None], stride_bias[None])
    return three.reshape(strips, cols, wide), four.reshape(strips // 2, cols // 2, s4)


def solution(mesh):
    rows = P(("groups", "rows"), None, None)
    return jax.shard_map(shards, mesh=mesh, in_specs=(rows,) + (P(),) * 10, out_specs=(rows, rows), check_vma=False)
```

time: 405 us -> 24.5 us (0.06)
  the two profiles are of different devices: /device:TPU:1 before, /device:TPU:25 now
where the time goes in v1:
time: 24.5 us; the launch traced here: 24.3 us
  Pallas kernels  10.7 us (44%)
  starting transfers between devices  5.73 us (23%)
  local copies, waits for them, and re-layouts  3.57 us (15%)
  waiting for transfers between devices  3.46 us (14%)
  between operations  0.81 us (3%)
    pallas_call x1, Pallas kernels, shards(): pl.pallas_call(block_kernel, out_shape=[jax.ShapeDtypeStruct((strips * co...  7.99 us
    ppermute x1, starting transfers between devices, shards(): lax.ppermute(scene_map[-2:], 'rows', [(i, i + 1) for i in range(count - 1)])  3.81 us
    ppermute x1, waiting for transfers between devices, shards(): lax.ppermute(scene_map[:1], 'rows', [(i + 1, i) for i in range(count - 1)])  3.46 us
    pallas_call x1, Pallas kernels, shards(): pl.pallas_call(unfold_kernel, out_shape=[pltpu.VMEM((mid, wide), BF16), p...  2.7 us
    unnamed x22, local copies, waits for them, and re-layouts  2.38 us
    ppermute x1, starting transfers between devices, shards(): lax.ppermute(scene_map[:1], 'rows', [(i + 1, i) for i in range(count - 1)])  1.92 us
    slice x1, local copies, waits for them, and re-layouts, shards(): scene_map[-2:]  1.17 us
  transfers between devices with their start and end apart: 2, of which 1 were waited for; matrix products, arithmetic and copies ran while one was open for 0% of the time, Pallas kernels for 11%

profile of v1, /device:TPU:25, one launch (start us, length us, event | category | flops | bytes accessed | tf_op | source)
XLA Modules:
  0.0 24.3 jit_solution(5897123663889352558)
XLA Ops:
  0.6 0.0 copy-start
  0.6 0.0 copy-start.3
  0.7 0.0 copy-start.5
  0.7 0.0 copy-start.4
  0.7 1.2 %slice.6 = bf16[2,128,1024]{2,1,0:T(8,128)(2,1)S(1)} slice(bf16[4,128,1024]{2,1,0:T(8,128)(2,1)} %param.11), slice={[2:4], [0:128], [0:1024]} | slice | bytes 1048576 | tf_op jit(solution)/shard_map/slice | solution.py:213
  1.8 0.0 copy-start.6
  1.9 0.0 copy-start.7
  1.9 0.0 copy-start.8
  1.9 0.0 copy-start.9
  1.9 0.0 copy-start.10
  1.9 3.8 %collective-permute-start = (bf16[2,128,1024]{2,1,0:T(8,128)(2,1)S(1)}, bf16[2,128,1024]{2,1,0:T(8,128)(2,1)S(1)}, u32[]{:S(2)}, u32[]{:S(2)}) collective-permute-start(bf16[2,128,1024]{2,1,0:T(8,128)(2,1)S(1)} %slice.6), channel_id=1, source_target_pairs={{0,1},{1,2},{2,3},{3,4},{4,5},{5,6},{6,7},{7,8},{8,9},{9,10},{10,1... | collective-permute-start | bytes 1572872 | tf_op jit(solution)/shard_map/ppermute | solution.py:213
  5.7 0.0 copy-done
  5.8 1.9 %collective-permute-start.1 = (bf16[1,128,1024]{2,1,0:T(8,128)(2,1)S(1)}, bf16[1,128,1024]{2,1,0:T(8,128)(2,1)S(1)}, u32[]{:S(2)}, u32[]{:S(2)}) collective-permute-start(bf16[1,128,1024]{2,1,0:T(8,128)(2,1)S(1)} %slice.7), channel_id=1, source_target_pairs={{1,0},{2,1},{3,2},{4,3},{5,4},{6,5},{7,6},{8,7},{9,8},{10,9},{11,1... | collective-permute-start | bytes 786440 | tf_op jit(solution)/shard_map/ppermute | solution.py:214
  7.7 0.0 copy-done.3
  7.7 0.0 copy-done.5
  7.7 0.0 copy-done.4
  7.7 0.0 copy-start.1
  7.7 1.3 %copy-done.1 = bf16[9,64,8,64]{3,2,1,0:T(8,128)(2,1)S(1)} copy-done((bf16[9,64,8,64]{3,2,1,0:T(8,128)(2,1)S(1)}, bf16[9,64,8,64]{3,2,1,0:T(8,128)(2,1)}, u32[]{:S(2)}) %copy-start.1) | copy-done | bytes 589848
  9.0 1.1 %copy-done.2 = bf16[9,32,8,32]{3,2,1,0:T(8,128)(2,1)S(1)} copy-done((bf16[9,32,8,32]{3,2,1,0:T(8,128)(2,1)S(1)}, bf16[9,32,8,32]{3,2,1,0:T(8,128)(2,1)}, u32[]{:S(2)}) %copy-start.2) | copy-done | bytes 147480
  10.1 2.7 %unfold.1 = (bf16[256,1024]{1,0:T(8,128)(2,1)S(1)}, bf16[2304,256]{1,0:T(8,128)(2,1)S(1)}, bf16[256,1024]{1,0:T(8,128)(2,1)S(1)}, bf16[512,1024]{1,0:T(8,128)(2,1)S(1)}, bf16[4608,128]{1,0:T(8,128)(2,1)S(1)}) custom-call(bf16[8,32,128]{2,1,0:T(8,128)(2,1)S(1)} %bitcast.16, bf16[9,32,8,32]{3,2,1,0:T(8,128)(2,1)S(1)} %copy-done.2, ...), custom_call_target="tpu_custom_call" | custom-call | tf_op jit(solution)/shard_map/unfold/pallas_call | solution.py:222
  12.8 3.5 %collective-permute-done.1 = bf16[1,128,1024]{2,1,0:T(8,128)(2,1)S(1)} collective-permute-done((bf16[1,128,1024]{2,1,0:T(8,128)(2,1)S(1)}, bf16[1,128,1024]{2,1,0:T(8,128)(2,1)S(1)}, u32[]{:S(2)}, u32[]{:S(2)}) %collective-permute-start.1) | collective-permute-done | bytes 262176 | tf_op jit(solution)/shard_map/ppermute | solution.py:214
  16.2 0.0 collective-permute-done
  16.2 0.0 copy-done.6
  16.3 8.0 %block.1 = (bf16[512,1024]{1,0:T(8,128)(2,1)}, bf16[128,512]{1,0:T(8,128)(2,1)}) custom-call(bf16[512,1024]{1,0:T(8,128)(2,1)S(1)} %bitcast.12, bf16[256,1024]{1,0:T(8,128)(2,1)S(1)} %bitcast.13, bf16[128,1024]{1,0:T(8,128)(2,1)S(1)} %bitcast.14, bf16[256,1024]{1,0:T(8,128)(2,1)S(1)} %get-tuple-element.9.wr_ref, ...), custom_call_target="tpu_custom_call" | custom-call | tf_op jit(solution)/shard_map/block/pallas_call | solution.py:246
  (6 shorter events, 0.0 us)
Async XLA Ops:
  0.6 5.1 %copy-start = (bf16[4,128,1024]{2,1,0:T(8,128)(2,1)S(1)}, bf16[4,128,1024]{2,1,0:T(8,128)(2,1)}, u32[]{:S(2)}) copy-start(bf16[4,128,1024]{2,1,0:T(8,128)(2,1)} %param.11) | copy-start | bytes 3145732
  0.6 7.1 %copy-start.3 = (bf16[128,8,64]{0,2,1:T(8,128)(2,1)S(1)}, bf16[128,8,64]{0,2,1:T(8,128)(2,1)}, u32[]{:S(2)}) copy-start(bf16[128,8,64]{0,2,1:T(8,128)(2,1)} %param.18) | copy-start | bytes 393220
  0.7 7.1 %copy-start.5 = (bf16[32,8,128]{2,1,0:T(8,128)(2,1)S(1)}, bf16[32,8,128]{2,1,0:T(8,128)(2,1)}, u32[]{:S(2)}) copy-start(bf16[32,8,128]{2,1,0:T(8,128)(2,1)} %kw_ref.1) | copy-start | bytes 196612
  0.7 7.1 %copy-start.4 = (bf16[128,8,32]{0,2,1:T(8,128)(2,1)S(1)}, bf16[128,8,32]{0,2,1:T(8,128)(2,1)}, u32[]{:S(2)}) copy-start(bf16[128,8,32]{0,2,1:T(8,128)(2,1)} %param.12) | copy-start | bytes 196612
  1.8 14.4 %copy-start.6 = (f32[32]{0:T(128)S(1)}, f32[32]{0:T(128)}, u32[]{:S(2)}) copy-start(f32[32]{0:T(128)} %param.13) | copy-start | bytes 388
  1.9 14.4 %copy-start.7 = (f32[32]{0:T(128)S(1)}, f32[32]{0:T(128)}, u32[]{:S(2)}) copy-start(f32[32]{0:T(128)} %param.15) | copy-start | bytes 388
  1.9 14.4 %copy-start.8 = (f32[128]{0:T(128)S(1)}, f32[128]{0:T(128)}, u32[]{:S(2)}) copy-start(f32[128]{0:T(128)} %param.17) | copy-start | bytes 1540
  1.9 14.4 %copy-start.9 = (f32[64]{0:T(128)S(1)}, f32[64]{0:T(128)}, u32[]{:S(2)}) copy-start(f32[64]{0:T(128)} %param.19) | copy-start | bytes 772
  1.9 14.4 %copy-start.10 = (f32[64]{0:T(128)S(1)}, f32[64]{0:T(128)}, u32[]{:S(2)}) copy-start(f32[64]{0:T(128)} %param.21) | copy-start | bytes 772
  1.9 14.3 %collective-permute-start = (bf16[2,128,1024]{2,1,0:T(8,128)(2,1)S(1)}, bf16[2,128,1024]{2,1,0:T(8,128)(2,1)S(1)}, u32[]{:S(2)}, u32[]{:S(2)}) collective-permute-start(bf16[2,128,1024]{2,1,0:T(8,128)(2,1)S(1)} %slice.6), channel_id=1, source_target_pairs={{0,1},{1,2},{2,3},{3,4},{4,5},{5,6},{6,7},{7,8},{8,9},{9,10},{10,1... | collective-permute-start | bytes 1572872 | tf_op jit(solution)/shard_map/ppermute | solution.py:213
  5.8 10.5 %collective-permute-start.1 = (bf16[1,128,1024]{2,1,0:T(8,128)(2,1)S(1)}, bf16[1,128,1024]{2,1,0:T(8,128)(2,1)S(1)}, u32[]{:S(2)}, u32[]{:S(2)}) collective-permute-start(bf16[1,128,1024]{2,1,0:T(8,128)(2,1)S(1)} %slice.7), channel_id=1, source_target_pairs={{1,0},{2,1},{3,2},{4,3},{5,4},{6,5},{7,6},{8,7},{9,8},{10,9},{11,1... | collective-permute-start | bytes 786440 | tf_op jit(solution)/shard_map/ppermute | solution.py:214
  7.7 1.3 %copy-start.1 = (bf16[9,64,8,64]{3,2,1,0:T(8,128)(2,1)S(1)}, bf16[9,64,8,64]{3,2,1,0:T(8,128)(2,1)}, u32[]{:S(2)}) copy-start(bf16[9,64,8,64]{3,2,1,0:T(8,128)(2,1)} %kt_ref.1) | copy-start | bytes 1769476
  9.0 1.1 %copy-start.2 = (bf16[9,32,8,32]{3,2,1,0:T(8,128)(2,1)S(1)}, bf16[9,32,8,32]{3,2,1,0:T(8,128)(2,1)}, u32[]{:S(2)}) copy-start(bf16[9,32,8,32]{3,2,1,0:T(8,128)(2,1)} %ks_ref.1) | copy-start | bytes 442372

commit v2 on v1

v2 whole, which is shorter than its diff:
```python
import functools

import jax
import jax.numpy as jnp
from jax import lax
from jax.experimental import pallas as pl
from jax.experimental.pallas import tpu as pltpu
from jax.sharding import PartitionSpec as P

ORIENT = 8
CYCLE_TAPS = [0, 1, 2, 5, 8, 7, 6, 3]
BF16, F32 = jnp.bfloat16, jnp.float32
NT = (((1,), (1,)), ((), ()))


def back_tap(tap, turn):
    if tap == 4:
        return 4
    return CYCLE_TAPS[(CYCLE_TAPS.index(tap) - turn) % ORIENT]


def iota(shape, dim):
    return lax.broadcasted_iota(jnp.int32, shape, dim)


def dot(a, b):
    return jnp.dot(a, b, preferred_element_type=F32)


def dot_nt(a, b):
    return lax.dot_general(a, b, NT, preferred_element_type=F32)


def rows_rolled(x, by):
    by %= x.shape[0]
    if by == 0:
        return x
    return jnp.concatenate([x[x.shape[0] - by:], x[:x.shape[0] - by]], 0)


def spread(fields, first, width):
    return jnp.where((iota((fields, width), 1) + first) // ORIENT == iota((fields, width), 0), 1.0, 0.0).astype(BF16)


def turned(blocks, block):
    lane = iota((1, blocks.shape[1]), 1)
    for bit in (1, 2, 4):
        take = jnp.broadcast_to(lane & bit, blocks.shape) != 0
        blocks = jnp.where(take, rows_rolled(blocks, bit * block), blocks)
    return blocks


def bias_lanes(bias, hot):
    first = bias.astype(BF16)
    rest = bias - first.astype(F32)
    second = rest.astype(BF16)
    third = (rest - second.astype(F32)).astype(BF16)
    parts = [dot(jnp.broadcast_to(p, (16,) + p.shape[1:]), hot)[:1] for p in (first, second, third)]
    return parts[0] + parts[1] + parts[2]


def shifted(y, cols):
    col = iota(y.shape, 0)
    left = jnp.where(col == 0, 0.0, pltpu.roll(y, 1, 0))
    right = jnp.where(col == cols - 1, 0.0, pltpu.roll(y, cols - 1, 0))
    return jnp.concatenate([left, y, right], 1).astype(BF16)


def tile_hot(fields, width):
    return jnp.where(iota((fields, width), 1) % fields == iota((fields, width), 0), 1.0, 0.0).astype(BF16)


def fetched(pairs, sem, first=0):
    copies = [pltpu.make_async_copy(source, target, sem.at[first + n]) for n, (source, target) in enumerate(pairs)]
    for copy in copies:
        copy.start()
    return copies


def reduce_kernel_body(x_ref, kr_hbm, br_hbm, xs_ref, wr_ref, bias_ref, mids_ref, down_ref, up_ref, kr_ref, br_ref, sem):
    cols = up_ref.shape[0]
    strips = x_ref.shape[0] // cols
    small = fetched([(kr_hbm, kr_ref), (br_hbm, br_ref)], sem, strips)
    copies = []
    for row in range(strips):
        at = pl.ds(row * cols, cols)
        copies.append(pltpu.make_async_copy(x_ref.at[at], xs_ref.at[at], sem.at[row]))
        copies[-1].start()
    in_f, mid_f = kr_ref.shape[2], kr_ref.shape[1]
    wide, mid = in_f * ORIENT, mid_f * ORIENT
    for copy in small:
        copy.wait()
    kr = kr_ref[...].reshape(mid, in_f)
    kr = jnp.concatenate([kr[(-r) % ORIENT * mid_f:((-r) % ORIENT + 1) * mid_f] for r in range(ORIENT)], 0)
    for first in range(0, wide, 256):
        wr_ref[:, pl.ds(first, 256)] = turned(dot(kr, spread(in_f, first, 256)), mid_f).astype(BF16)
    bias = bias_lanes(br_ref[...], tile_hot(mid_f, mid))
    bias_ref[...] = bias
    for copy in copies:
        copy.wait()
    y = jnp.maximum(dot_nt(xs_ref[...], wr_ref[...]) + bias, 0.0)
    for row in range(strips):
        part = y[row * cols:(row + 1) * cols]
        mids_ref[pl.ds(row * cols, cols), :] = shifted(part, cols)
        if row == 0:
            up_ref[...] = part.astype(BF16)
        if row == strips - 2:
            down_ref[:, wide:] = part.astype(BF16)
    down_ref[:, :wide] = xs_ref[pl.ds((strips - 1) * cols, cols), :]


def strip_block(windows, x, ws_ref, ww_ref, we_ref, b_mid, b_wid, b_ent, threes):
    acc = b_mid
    depth = windows[0].shape[1]
    for dy in range(3):
        acc = acc + dot(windows[dy], ws_ref[pl.ds(dy * depth, depth), :])
    two = jnp.maximum(acc, 0.0).astype(BF16)
    for first in range(0, ww_ref.shape[1], 256):
        part = slice(first, first + 256)
        z = x(part).astype(F32) + dot(two, ww_ref[:, part]) + b_wid[:, part]
        threes[:, part] = jnp.maximum(z, 0.0).astype(BF16)
    return jnp.maximum(dot_nt(threes[...], we_ref[...]) + b_ent, 0.0)


def thirds(fours, f, strip, slot, cols, phases):
    half = cols // 2
    groups = f.shape[1] // 128
    for g in range(groups):
        fours[g, pl.ds(strip * cols, cols), :] = f[strip * cols:(strip + 1) * cols, g * 128:(g + 1) * 128]
    col = iota((half, 128), 0)
    for g in range(groups):
        even = fours[g, pl.ds(strip * cols, half, stride=2), :]
        odd = fours[g, pl.ds(strip * cols + 1, half, stride=2), :]
        moved = jnp.where(col == 0, 0.0, pltpu.roll(odd, 1, 0))
        for n, value in enumerate((moved, even, odd)):
            phases[pl.ds(slot * half, half), pl.ds((n * groups + g) * 128, 128)] = value.astype(BF16)


def inner_kernel(xs_ref, mids_ref, ks_hbm, kw_hbm, ke_hbm, kt_hbm, bs_hbm, bw_hbm, be_hbm, bt_hbm,
                 three_ref, ws_ref, ww_ref, we_ref, k2_ref, order_ref, b_mid_ref, b_wid_ref, b_ent_ref, b_str_ref, phases_ref,
                 ks_v, kw_ref, ke_ref, kt_v, bs_ref, bw_ref, be_ref, bt_ref, flat_w, flat_s, flat_t, threes, fours, sem):
    small = fetched([(ke_hbm, ke_ref), (kw_hbm, kw_ref), (bs_hbm, bs_ref), (bw_hbm, bw_ref), (be_hbm, be_ref), (bt_hbm, bt_ref)], sem, 1)
    large = fetched([(ks_hbm, ks_v), (kt_hbm, kt_v)], sem, 7)
    in_f, s4_f, mid_f = ke_ref.shape[2], ke_ref.shape[1], kw_ref.shape[0]
    wide, s4, mid = in_f * ORIENT, s4_f * ORIENT, mid_f * ORIENT
    cols = phases_ref.shape[0]
    strips = xs_ref.shape[0] // cols
    a, b = iota((s4, s4), 0), iota((s4, s4), 1)
    order_ref[...] = jnp.where(b == (a % s4_f) * ORIENT + a // s4_f, 1.0, 0.0).astype(BF16)
    for copy in small:
        copy.wait()
    ke = ke_ref[...].reshape(s4, in_f)
    ke = jnp.concatenate([ke[(-r) % ORIENT * s4_f:((-r) % ORIENT + 1) * s4_f] for r in range(ORIENT)], 0)
    flat_w[...] = kw_ref[...].astype(F32).reshape(mid, in_f)
    kw = jnp.concatenate([flat_w[pl.ds(u, mid_f, stride=ORIENT), :] for u in range(ORIENT)], 0).astype(BF16)
    for first in range(0, wide, 256):
        hot = spread(in_f, first, 256)
        cut = pl.ds(first, 256)
        ww_ref[:, cut] = turned(dot(kw, hot), mid_f).astype(BF16)
        we_ref[:, cut] = turned(dot(ke, hot), s4_f).astype(BF16)
    b_mid_ref[...] = bias_lanes(bs_ref[...], tile_hot(mid_f, mid))
    b_ent_ref[...] = bias_lanes(be_ref[...], tile_hot(s4_f, s4))
    b_str_ref[...] = bias_lanes(bt_ref[...], tile_hot(s4_f, s4))
    b_wid_ref[...] = bias_lanes(bw_ref[...], spread(in_f, 0, wide))

    lane = iota((1, 128), 1)
    large[0].wait()
    for tap in range(9):
        flat_s[pl.ds(tap * mid, mid), :mid_f] = ks_v[tap].astype(F32).reshape(mid, mid_f)
    piece = lambda tap, u: flat_s[pl.ds(tap * mid + u % ORIENT, mid_f, stride=ORIENT), :]
    low = jnp.broadcast_to(lane < mid_f, (mid_f, 128))
    half = jnp.broadcast_to(lane < 2 * mid_f, (mid_f, 128))
    pairs = {}
    for tap in range(9):
        for u in range(ORIENT):
            pairs[tap, u] = jnp.where(low, piece(tap, u), pltpu.roll(piece(back_tap(tap, 1), u - 1), mid_f, 1))
    for tap in range(9):
        for u in range(ORIENT):
            quad = jnp.where(half, pairs[tap, u], pltpu.roll(pairs[back_tap(tap, 2), (u - 2) % ORIENT], 2 * mid_f, 1)).astype(BF16)
            ws_ref[pl.ds(tap * mid + u * mid_f, mid_f), :128] = quad
            ahead = back_tap(tap, -4)
            ws_ref[pl.ds(ahead * mid + (u + 4) % ORIENT * mid_f, mid_f), 128:] = quad

    large[1].wait()
    for tap in range(9):
        flat_t[pl.ds(tap * s4, s4), :s4_f] = kt_v[tap].astype(F32).reshape(s4, s4_f)
    piece_t = lambda tap, u: flat_t[pl.ds(tap * s4 + u % ORIENT, s4_f, stride=ORIENT), :]
    low_t = jnp.broadcast_to(lane < s4_f, (s4_f, 128))
    for tap in range(9):
        for u in range(ORIENT):
            pair = jnp.where(low_t, piece_t(tap, u), pltpu.roll(piece_t(back_tap(tap, 1), u - 1), s4_f, 1))
            k2_ref[pl.ds(tap * s4 + u * s4_f, s4_f), :] = pair.astype(BF16)

    inner = strips - 2
    windows = [mids_ref[pl.ds(dy * cols, inner * cols), :] for dy in range(3)]
    f = strip_block(windows, lambda part: xs_ref[pl.ds(cols, inner * cols), part], ws_ref, ww_ref, we_ref,
                    b_mid_ref[...], b_wid_ref[...], b_ent_ref[...], threes)
    out = pltpu.make_async_copy(threes, three_ref.at[pl.ds(cols, inner * cols)], sem.at[0])
    out.start()
    for strip in range(inner):
        thirds(fours, f, strip, strip, cols, phases_ref)
    out.wait()


def edge_kernel(down_ref, up_ref, xs_ref, wr_ref, bias_ref, mids_ref, ws_ref, ww_ref, we_ref, k2_ref, order_ref,
                b_mid_ref, b_wid_ref, b_ent_ref, b_str_ref, inner_ref, kept_ref,
                three_ref, four_ref, xe, threes, fours, phases, sem):
    place, count = lax.axis_index("rows"), lax.axis_size("rows")
    cols = up_ref.shape[0]
    half = cols // 2
    strips = xs_ref.shape[0] // cols
    wide, mid, s4 = xs_ref.shape[1], wr_ref.shape[0], we_ref.shape[0]
    not_first = jnp.where(place == 0, 0.0, 1.0)
    not_last = jnp.where(place == count - 1, 0.0, 1.0)
    strip_of = lambda row: mids_ref[pl.ds(row * cols, cols), :]
    xe[pl.ds(0, cols), :] = down_ref[:, :wide]
    xe[pl.ds(cols, cols), :] = xs_ref[pl.ds(0, cols), :]
    xe[pl.ds(2 * cols, cols), :] = xs_ref[pl.ds((strips - 1) * cols, cols), :]
    above_two = shifted(down_ref[:, wide:].astype(F32) * not_first, cols)
    y = jnp.maximum(dot_nt(down_ref[:, :wide], wr_ref[...]) + bias_ref[...], 0.0) * not_first
    above = shifted(y, cols)
    below = shifted(up_ref[...].astype(F32) * not_last, cols)
    last = strips - 1
    windows = [
        jnp.concatenate([above_two, above, strip_of(last - 1)], 0),
        jnp.concatenate([above, strip_of(0), strip_of(last)], 0),
        jnp.concatenate([strip_of(0), strip_of(1), below], 0),
    ]
    f = strip_block(windows, lambda part: xe[:, part], ws_ref, ww_ref, we_ref,
                    b_mid_ref[...], b_wid_ref[...], b_ent_ref[...], threes)
    outs = [
        pltpu.make_async_copy(threes.at[pl.ds(cols, cols)], three_ref.at[pl.ds(0, cols)], sem.at[0]),
        pltpu.make_async_copy(threes.at[pl.ds(2 * cols, cols)], three_ref.at[pl.ds(last * cols, cols)], sem.at[1]),
    ]
    for out in outs:
        out.start()
    f = jnp.concatenate([f[:cols] * not_first, f[cols:]], 0)
    for strip in range(3):
        thirds(fours, f, strip, strip, cols, phases)

    def rows_of(row, dx):
        cut = slice(dx * s4, (dx + 1) * s4)
        if row < 1:
            return phases[pl.ds((row + 1) * half, half), cut]
        if row == last:
            return phases[pl.ds(2 * half, half), cut]
        return inner_ref[pl.ds((row - 1) * half, half), cut]

    def filter_tile(tap, pair):
        halves = []
        for j in (2 * pair, 2 * pair + 1):
            source = back_tap(tap, 2 * j)
            halves.append(rows_rolled(k2_ref[pl.ds(source * s4, s4), :], 128 * j))
        return jnp.concatenate(halves, 1)

    lhs = []
    for tap in range(9):
        dy, dx = divmod(tap, 3)
        lhs.append(jnp.concatenate([rows_of(2 * q + dy - 1, dx) for q in range(strips // 2)], 0))
    results = []
    for pair in range(s4 // 256):
        acc = b_str_ref[:, pair * 256:(pair + 1) * 256]
        for tap in range(9):
            acc = acc + dot(lhs[tap], filter_tile(tap, pair))
        results.append(jnp.maximum(acc, 0.0).astype(BF16))
    four_ref[...] = dot(jnp.concatenate(results, 1), order_ref[...]).astype(BF16)
    for out in outs:
        out.wait()


def shards(scene_map, reduce_kernel, reduce_bias, spatial_kernel, spatial_bias, widen_kernel, widen_bias,
           entry_kernel, entry_bias, stride_kernel, stride_bias):
    count = lax.axis_size("rows")
    strips, cols, wide = scene_map.shape
    mid_f, s4_f = reduce_kernel.shape[2], entry_kernel.shape[2]
    mid, s4 = mid_f * ORIENT, s4_f * ORIENT
    own, half = strips * cols, cols // 2
    hbm = pl.BlockSpec(memory_space=pl.ANY)
    vmem = pl.BlockSpec(memory_space=pltpu.VMEM)
    dma = pltpu.SemaphoreType.DMA
    limit = lambda mib: pltpu.CompilerParams(vmem_limit_bytes=mib << 20)

    pinned = lambda *arrays: [pltpu.with_memory_space_constraint(a, pltpu.HBM) for a in arrays]
    xs, w_reduce, b_reduce, mids, down, up = pl.pallas_call(
        reduce_kernel_body,
        out_shape=[
            pltpu.VMEM((own, wide), BF16),
            pltpu.VMEM((mid, wide), BF16),
            pltpu.VMEM((1, mid), F32),
            pltpu.VMEM((own, 3 * mid), BF16),
            pltpu.VMEM((cols, wide + mid), BF16),
            pltpu.VMEM((cols, mid), BF16),
        ],
        in_specs=[hbm] * 3,
        out_specs=[vmem] * 6,
        scratch_shapes=[
            pltpu.VMEM((ORIENT, mid_f, wide // ORIENT), BF16),
            pltpu.VMEM((1, mid_f), F32),
            dma((strips + 2,)),
        ],
        compiler_params=limit(16),
        name="reduce",
    )(*pinned(scene_map.reshape(own, wide), reduce_kernel.transpose(1, 2, 0), reduce_bias[None]))
    down = lax.ppermute(down, "rows", [(i, i + 1) for i in range(count - 1)])
    up = lax.ppermute(up, "rows", [(i + 1, i) for i in range(count - 1)])

    three, *kept, phases = pl.pallas_call(
        inner_kernel,
        out_shape=[
            jax.ShapeDtypeStruct((own, wide), BF16),
            pltpu.VMEM((9 * mid, mid), BF16),
            pltpu.VMEM((mid, wide), BF16),
            pltpu.VMEM((s4, wide), BF16),
            pltpu.VMEM((9 * s4, 128), BF16),
            pltpu.VMEM((s4, s4), BF16),
            pltpu.VMEM((1, mid), F32),
            pltpu.VMEM((1, wide), F32),
            pltpu.VMEM((1, s4), F32),
            pltpu.VMEM((1, s4), F32),
            pltpu.VMEM(((strips - 2) * half, 3 * s4), BF16),
        ],
        in_specs=[vmem] * 2 + [hbm] * 8,
        out_specs=[hbm] + [vmem] * 10,
        scratch_shapes=[
            pltpu.VMEM(spatial_kernel.shape, BF16),
            pltpu.VMEM(widen_kernel.shape, BF16),
            pltpu.VMEM((ORIENT, s4_f, wide // ORIENT), BF16),
            pltpu.VMEM(stride_kernel.shape, BF16),
            pltpu.VMEM((1, mid_f), F32),
            pltpu.VMEM((1, wide // ORIENT), F32),
            pltpu.VMEM((1, s4_f), F32),
            pltpu.VMEM((1, s4_f), F32),
            pltpu.VMEM((mid, wide // ORIENT), F32),
            pltpu.VMEM((9 * mid, 128), F32),
            pltpu.VMEM((9 * s4, 128), F32),
            pltpu.VMEM(((strips - 2) * cols, wide), BF16),
            pltpu.VMEM((s4 // 128, (strips - 2) * cols, 128), F32),
            dma((9,)),
        ],
        compiler_params=limit(28),
        name="inner",
    )(xs, mids, *pinned(spatial_kernel, widen_kernel, entry_kernel.transpose(1, 2, 0), stride_kernel,
                         spatial_bias[None], widen_bias[None], entry_bias[None], stride_bias[None]))

    operands = [down, up, xs, w_reduce, b_reduce, mids, *kept, phases, three]
    three, four = pl.pallas_call(
        edge_kernel,
        out_shape=[
            jax.ShapeDtypeStruct((own, wide), BF16),
            jax.ShapeDtypeStruct((strips // 2 * half, s4), BF16),
        ],
        in_specs=[vmem] * (len(operands) - 1) + [hbm],
        out_specs=[hbm, vmem],
        input_output_aliases={len(operands) - 1: 0},
        scratch_shapes=[
            pltpu.VMEM((3 * cols, wide), BF16),
            pltpu.VMEM((3 * cols, wide), BF16),
            pltpu.VMEM((s4 // 128, 3 * cols, 128), F32),
            pltpu.VMEM((3 * half, 3 * s4), BF16),
            dma((2,)),
        ],
        compiler_params=limit(28),
        name="edge",
    )(*operands)
    return three.reshape(strips, cols, wide), four.reshape(strips // 2, half, s4)


def solution(mesh):
    rows = P(("groups", "rows"), None, None)
    return jax.shard_map(shards, mesh=mesh, in_specs=(rows,) + (P(),) * 10, out_specs=(rows, rows), check_vma=False)
```

time: 24.5 us -> 18.2 us (0.74)
  the two profiles are of different devices: /device:TPU:25 before, /device:TPU:1 now
where the time goes in v2:
time: 18.2 us; the launch traced here: 17.9 us
  Pallas kernels  10.8 us (59%)
  starting transfers between devices  6.43 us (35%)
  between operations  0.68 us (4%)
    pallas_call x1, Pallas kernels, shards(): pl.pallas_call(inner_kernel, out_shape=[jax.ShapeDtypeStruct((own, wide),...  5.03 us
    ppermute x1, starting transfers between devices, shards(): down = lax.ppermute(down, 'rows', [(i, i + 1) for i in range(count - 1)])  4.51 us
    pallas_call x1, Pallas kernels, shards(): pl.pallas_call(edge_kernel, out_shape=[jax.ShapeDtypeStruct((own, wide),...  3.95 us
    ppermute x1, starting transfers between devices, shards(): up = lax.ppermute(up, 'rows', [(i + 1, i) for i in range(count - 1)])  1.92 us
    pallas_call x1, Pallas kernels, shards(): pl.pallas_call(reduce_kernel_body, out_shape=[pltpu.VMEM((own, wide), BF1...  1.84 us
  transfers between devices with their start and end apart: 2, of which 0 were waited for; matrix products, arithmetic and copies ran while one was open for 0% of the time, Pallas kernels for 28%

profile of v2, /device:TPU:1, one launch (start us, length us, event | category | flops | bytes accessed | tf_op | source)
XLA Modules:
  0.0 17.9 jit_solution(16252886777128144927)
XLA Ops:
  0.6 1.8 %reduce.1 = (bf16[512,1024]{1,0:T(8,128)(2,1)S(1)}, bf16[256,1024]{1,0:T(8,128)(2,1)S(1)}, f32[1,256]{1,0:T(1,128)S(1)}, bf16[512,768]{1,0:T(8,128)(2,1)S(1)}, b...) custom-call(bf16[512,1024]{1,0:T(8,128)(2,1)} %bitcast.10, bf16[8,32,128]{2,1,0:T(8,128)(2,1)} %bitcast.13, ...), custom_call_target="tpu_custom_call" | custom-call | tf_op jit(solution)/shard_map/reduce/pallas_call | solution.py:284
  2.5 4.5 %collective-permute-start = (bf16[128,1280]{1,0:T(8,128)(2,1)S(1)}, bf16[128,1280]{1,0:T(8,128)(2,1)S(1)}, u32[]{:S(2)}, u32[]{:S(2)}) collective-permute-start(bf16[128,1280]{1,0:T(8,128)(2,1)S(1)} %get-tuple-element.21), channel_id=1, source_target_pairs={{0,1},{1,2},{2,3},{3,4},{4,5},{5,6},{6,7},{7,8},{8,9},{9,10},{10,1... | collective-permute-start | bytes 983048 | tf_op jit(solution)/shard_map/ppermute | solution.py:304
  7.0 1.9 %collective-permute-start.1 = (bf16[128,256]{1,0:T(8,128)(2,1)S(1)}, bf16[128,256]{1,0:T(8,128)(2,1)S(1)}, u32[]{:S(2)}, u32[]{:S(2)}) collective-permute-start(bf16[128,256]{1,0:T(8,128)(2,1)S(1)} %get-tuple-element.22), channel_id=1, source_target_pairs={{1,0},{2,1},{3,2},{4,3},{5,4},{6,5},{7,6},{8,7},{9,8},{10,9},{11,1... | collective-permute-start | bytes 196616 | tf_op jit(solution)/shard_map/ppermute | solution.py:305
  8.9 5.0 %inner.1 = (bf16[512,1024]{1,0:T(8,128)(2,1)}, bf16[2304,256]{1,0:T(8,128)(2,1)S(1)}, bf16[256,1024]{1,0:T(8,128)(2,1)S(1)}, bf16[512,1024]{1,0:T(8,128)(2,1)S(1...) custom-call(bf16[512,1024]{1,0:T(8,128)(2,1)S(1)} %get-tuple-element, ...), custom_call_target="tpu_custom_call" | custom-call | tf_op jit(solution)/shard_map/inner/pallas_call | solution.py:307
  14.0 0.0 collective-permute-done.1.up_ref
  14.0 0.0 collective-permute-done.down_ref
  14.0 4.0 %edge.1 = (bf16[512,1024]{1,0:T(8,128)(2,1)}, bf16[128,512]{1,0:T(8,128)(2,1)}) custom-call(bf16[128,1280]{1,0:T(8,128)(2,1)S(1)} %collective-permute-done.down_ref, bf16[128,256]{1,0:T(8,128)(2,1)S(1)} %collective-permute-done.1.up_ref, bf16[512,1024]{1,0:T(8,128)(2,1)S(1)} %get-tuple-element.23.xs_ref, ...), custom_call_target="tpu_custom_call", output_to_operand_aliasing={{0}: (16, {})} | custom-call | tf_op jit(solution)/shard_map/edge/pallas_call | solution.py:346
Async XLA Ops:
  2.5 11.5 %collective-permute-start = (bf16[128,1280]{1,0:T(8,128)(2,1)S(1)}, bf16[128,1280]{1,0:T(8,128)(2,1)S(1)}, u32[]{:S(2)}, u32[]{:S(2)}) collective-permute-start(bf16[128,1280]{1,0:T(8,128)(2,1)S(1)} %get-tuple-element.21), channel_id=1, source_target_pairs={{0,1},{1,2},{2,3},{3,4},{4,5},{5,6},{6,7},{7,8},{8,9},{9,10},{10,1... | collective-permute-start | bytes 983048 | tf_op jit(solution)/shard_map/ppermute | solution.py:304
  7.0 7.0 %collective-permute-start.1 = (bf16[128,256]{1,0:T(8,128)(2,1)S(1)}, bf16[128,256]{1,0:T(8,128)(2,1)S(1)}, u32[]{:S(2)}, u32[]{:S(2)}) collective-permute-start(bf16[128,256]{1,0:T(8,128)(2,1)S(1)} %get-tuple-element.22), channel_id=1, source_target_pairs={{1,0},{2,1},{3,2},{4,3},{5,4},{6,5},{7,6},{8,7},{9,8},{10,9},{11,1... | collective-permute-start | bytes 196616 | tf_op jit(solution)/shard_map/ppermute | solution.py:305

commit v3 on v2

v3 whole, which is shorter than its diff:
```python
import functools

import jax
import jax.numpy as jnp
from jax import lax
from jax.experimental import pallas as pl
from jax.experimental.pallas import tpu as pltpu
from jax.sharding import PartitionSpec as P

ORIENT = 8
BLOCK = 128
CYCLE_TAPS = [0, 1, 2, 5, 8, 7, 6, 3]
BF16, F32 = jnp.bfloat16, jnp.float32
NT = (((1,), (1,)), ((), ()))


def back_tap(tap, turn):
    if tap == 4:
        return 4
    return CYCLE_TAPS[(CYCLE_TAPS.index(tap) - turn) % ORIENT]


def iota(shape, dim):
    return lax.broadcasted_iota(jnp.int32, shape, dim)


def dot(a, b):
    return jnp.dot(a, b, preferred_element_type=F32)


def dot_nt(a, b):
    return lax.dot_general(a, b, NT, preferred_element_type=F32)


def rows_rolled(x, by):
    by %= x.shape[0]
    if by == 0:
        return x
    return jnp.concatenate([x[x.shape[0] - by:], x[:x.shape[0] - by]], 0)


def spread(fields, first, width):
    lead = iota((fields, width), 1) + first - ORIENT * iota((fields, width), 0)
    return jnp.where(lead & -ORIENT == 0, 1.0, 0.0).astype(BF16)


def turned(blocks, block):
    lane = iota((1, blocks.shape[1]), 1)
    for bit in (1, 2, 4):
        take = jnp.broadcast_to(lane & bit, blocks.shape) != 0
        blocks = jnp.where(take, rows_rolled(blocks, bit * block), blocks)
    return blocks


def unfold_in(kernel, fields, store):
    inputs = kernel.shape[1]
    base = jnp.concatenate([kernel[(-r) % ORIENT * fields:((-r) % ORIENT + 1) * fields] for r in range(ORIENT)], 0)
    base, other = base.T, rows_rolled(base, fields).T
    for first in range(0, inputs * ORIENT, 128):
        lead = iota((128, inputs), 0) + first - ORIENT * iota((128, inputs), 1)
        hot = jnp.where(lead & -ORIENT == 0, 1.0, 0.0).astype(BF16)
        row = iota((128, fields * ORIENT), 0)
        block = jnp.where(row & 1 != 0, dot(hot, other), dot(hot, base))
        for bit in (2, 4):
            block = jnp.where(row & bit != 0, pltpu.roll(block, bit * fields, 1), block)
        store(pl.ds(first, 128), block.astype(BF16))


def bias_lanes(bias, hot):
    first = bias.astype(BF16)
    rest = bias - first.astype(F32)
    second = rest.astype(BF16)
    third = (rest - second.astype(F32)).astype(BF16)
    parts = [dot(jnp.broadcast_to(p, (16,) + p.shape[1:]), hot)[:1] for p in (first, second, third)]
    return parts[0] + parts[1] + parts[2]


def fetched(pairs, sem, first=0):
    copies = [pltpu.make_async_copy(source, target, sem.at[first + n]) for n, (source, target) in enumerate(pairs)]
    for copy in copies:
        copy.start()
    return copies


def shifted(y, cols):
    col = iota(y.shape, 0)
    left = jnp.where(col == 0, 0.0, pltpu.roll(y, 1, 0))
    right = jnp.where(col == cols - 1, 0.0, pltpu.roll(y, cols - 1, 0))
    return jnp.concatenate([left, y, right], 1).astype(BF16)


def tile_hot(fields, width):
    return jnp.where((iota((fields, width), 1) - iota((fields, width), 0)) & (fields - 1) == 0, 1.0, 0.0).astype(BF16)


def fetched(pairs, sem, first=0):
    copies = [pltpu.make_async_copy(source, target, sem.at[first + n]) for n, (source, target) in enumerate(pairs)]
    for copy in copies:
        copy.start()
    return copies


def load_kernel(x_hbm, kr_hbm, br_hbm, bs_hbm, bw_hbm, be_hbm, bt_hbm,
                xs_ref, last_ref, wr_ref, b_red_ref, b_mid_ref, b_wid_ref, b_ent_ref, b_str_ref, order_ref,
                kr_ref, br_ref, bs_ref, bw_ref, be_ref, bt_ref, sem):
    cols = last_ref.shape[0]
    own = x_hbm.shape[0]
    small = fetched([(kr_hbm, kr_ref), (br_hbm, br_ref), (bs_hbm, bs_ref), (bw_hbm, bw_ref), (be_hbm, be_ref), (bt_hbm, bt_ref)], sem)
    large = fetched([(x_hbm.at[pl.ds(own - cols, cols)], last_ref), (x_hbm, xs_ref)], sem, 6)
    in_f, mid_f, s4_f = kr_ref.shape[2], kr_ref.shape[1], be_ref.shape[1]
    wide, mid, s4 = in_f * ORIENT, mid_f * ORIENT, s4_f * ORIENT
    shift = s4_f.bit_length() - 1
    a, b = iota((s4, s4), 0), iota((s4, s4), 1)
    order_ref[...] = jnp.where(b == (a & (s4_f - 1)) * ORIENT + (a >> shift), 1.0, 0.0).astype(BF16)
    for copy in small:
        copy.wait()
    def keep(at, block):
        wr_ref[at, :] = block
    unfold_in(kr_ref[...].reshape(mid, in_f), mid_f, keep)
    hot_mid, hot_s4 = tile_hot(mid_f, mid), tile_hot(s4_f, s4)
    b_red_ref[...] = bias_lanes(br_ref[...], hot_mid)
    b_mid_ref[...] = bias_lanes(bs_ref[...], hot_mid)
    b_ent_ref[...] = bias_lanes(be_ref[...], hot_s4)
    b_str_ref[...] = bias_lanes(bt_ref[...], hot_s4)
    b_wid_ref[...] = bias_lanes(bw_ref[...], spread(in_f, 0, wide))
    for copy in large:
        copy.wait()


def reducing(xs_ref, wr_ref, bias_ref, mids_ref, first_ref, second_ref):
    cols = first_ref.shape[0]
    strips = xs_ref.shape[0] // cols
    even = lax.axis_index("groups") % 2 == 0
    y = jnp.maximum(dot(xs_ref[...], wr_ref[...]) + bias_ref[...], 0.0)
    parts = [y[row * cols:(row + 1) * cols] for row in range(strips)]
    first_ref[...] = jnp.where(even, parts[strips - 2], parts[0]).astype(BF16)
    second_ref[...] = jnp.where(even, parts[0], parts[strips - 2]).astype(BF16)
    for row, part in enumerate(parts):
        mids_ref[pl.ds(row * cols, cols), :] = shifted(part, cols)


def strip_block(windows, x, ws_ref, ww_ref, b_mid, b_wid, threes):
    depth = windows[0].shape[1]
    twos = []
    for m in range(0, threes.shape[0], BLOCK):
        acc = b_mid
        for dy in range(3):
            acc = acc + dot(windows[dy][m:m + BLOCK], ws_ref[pl.ds(dy * depth, depth), :])
        twos.append(jnp.maximum(acc, 0.0).astype(BF16))
    for m, two in enumerate(twos):
        at = pl.ds(m * BLOCK, BLOCK)
        for first in range(0, ww_ref.shape[1], 256):
            part = slice(first, first + 256)
            z = x(at, part).astype(F32) + dot(two, ww_ref[:, part]) + b_wid[:, part]
            threes[at, part] = jnp.maximum(z, 0.0).astype(BF16)


def entry_part(threes, we_ref, b_ent, row, first):
    cut = slice(first, first + 256)
    return jnp.maximum(dot(threes[pl.ds(row, BLOCK), :], we_ref[:, cut]) + b_ent[:, cut], 0.0)


def thirds(fours, threes, we_ref, b_ent, scale, strip, slot, cols, phases):
    half = cols // 2
    s4 = we_ref.shape[1]
    for first in range(0, s4, 256):
        f = entry_part(threes, we_ref, b_ent, strip * cols, first)
        if scale is not None:
            f = f * scale
        for g in range(2):
            fours[first // 128 + g, pl.ds(strip * cols, cols), :] = f[:, g * 128:(g + 1) * 128]
    col = iota((half, 128), 0)
    for g in range(s4 // 128):
        even = fours[g, pl.ds(strip * cols, half, stride=2), :]
        odd = fours[g, pl.ds(strip * cols + 1, half, stride=2), :]
        moved = jnp.where(col == 0, 0.0, pltpu.roll(odd, 1, 0))
        for n, value in enumerate((moved, even, odd)):
            phases[pl.ds(slot * half, half), pl.ds(n * s4 + g * 128, 128)] = value.astype(BF16)


def inner_kernel(xs_ref, mids_ref, b_mid_ref, b_wid_ref, b_ent_ref, ks_hbm, kw_hbm, ke_hbm, kt_hbm,
                 three_ref, ws_ref, ww_ref, we_ref, k2_ref, phases_ref,
                 ks_v, kw_ref, ke_ref, kt_v, flat_w, flat_s, flat_t, threes, fours, sem):
    copies = fetched([(kw_hbm, kw_ref), (ke_hbm, ke_ref), (ks_hbm, ks_v), (kt_hbm, kt_v)], sem, 1)
    in_f, s4_f, mid_f = ke_ref.shape[2], ke_ref.shape[1], kw_ref.shape[0]
    wide, s4, mid = in_f * ORIENT, s4_f * ORIENT, mid_f * ORIENT
    cols = phases_ref.shape[0]
    strips = xs_ref.shape[0] // cols
    copies[0].wait()
    flat_w[...] = kw_ref[...].astype(F32).reshape(mid, in_f)
    kw = jnp.concatenate([flat_w[pl.ds(u, mid_f, stride=ORIENT), :] for u in range(ORIENT)], 0).astype(BF16)
    for first in range(0, wide, 256):
        ww_ref[:, pl.ds(first, 256)] = turned(dot(kw, spread(in_f, first, 256)), mid_f).astype(BF16)
    copies[1].wait()
    def keep(at, block):
        we_ref[at, :] = block
    unfold_in(ke_ref[...].reshape(s4, in_f), s4_f, keep)

    lane = iota((1, 128), 1)
    copies[2].wait()
    for tap in range(9):
        flat_s[pl.ds(tap * mid, mid), :mid_f] = ks_v[tap].astype(F32).reshape(mid, mid_f)
    piece = lambda tap, u: flat_s[pl.ds(tap * mid + u % ORIENT, mid_f, stride=ORIENT), :]
    low = jnp.broadcast_to(lane < mid_f, (mid_f, 128))
    half = jnp.broadcast_to(lane < 2 * mid_f, (mid_f, 128))
    pairs = {}
    for tap in range(9):
        for u in range(ORIENT):
            pairs[tap, u] = jnp.where(low, piece(tap, u), pltpu.roll(piece(back_tap(tap, 1), u - 1), mid_f, 1))
    for tap in range(9):
        for u in range(ORIENT):
            quad = jnp.where(half, pairs[tap, u], pltpu.roll(pairs[back_tap(tap, 2), (u - 2) % ORIENT], 2 * mid_f, 1)).astype(BF16)
            ws_ref[pl.ds(tap * mid + u * mid_f, mid_f), :128] = quad
            ahead = back_tap(tap, -4)
            ws_ref[pl.ds(ahead * mid + (u + 4) % ORIENT * mid_f, mid_f), 128:] = quad

    copies[3].wait()
    for tap in range(9):
        flat_t[pl.ds(tap * s4, s4), :s4_f] = kt_v[tap].astype(F32).reshape(s4, s4_f)
    piece_t = lambda tap, u: flat_t[pl.ds(tap * s4 + u % ORIENT, s4_f, stride=ORIENT), :]
    low_t = jnp.broadcast_to(lane < s4_f, (s4_f, 128))
    for tap in range(9):
        for u in range(ORIENT):
            pair = jnp.where(low_t, piece_t(tap, u), pltpu.roll(piece_t(back_tap(tap, 1), u - 1), s4_f, 1))
            k2_ref[pl.ds(tap * s4 + u * s4_f, s4_f), :] = pair.astype(BF16)

    inner = strips - 2
    windows = [mids_ref[pl.ds(dy * cols, inner * cols), :] for dy in range(3)]
    strip_block(windows, lambda at, part: xs_ref[pl.ds(cols + at.start, at.size), part], ws_ref, ww_ref,
                b_mid_ref[...], b_wid_ref[...], threes)
    out = pltpu.make_async_copy(threes, three_ref.at[pl.ds(cols, inner * cols)], sem.at[0])
    out.start()
    for strip in range(inner):
        thirds(fours, threes, we_ref, b_ent_ref[...], None, strip, strip, cols, phases_ref)
    out.wait()


def edge_kernel(last_ref, first_ref, second_ref, xs_ref, wr_ref, bias_ref, b_mid_ref, b_wid_ref, b_ent_ref, b_str_ref, order_ref,
                mids_ref, ws_ref, ww_ref, we_ref, k2_ref, inner_ref, kept_ref,
                three_ref, four_ref, xe, threes, fours, phases, sem):
    place, count = lax.axis_index("rows"), lax.axis_size("rows")
    even = lax.axis_index("groups") % 2 == 0
    cols = first_ref.shape[0]
    half = cols // 2
    strips = xs_ref.shape[0] // cols
    wide, mid, s4 = xs_ref.shape[1], wr_ref.shape[1], we_ref.shape[1]
    not_first = jnp.where(place == 0, 0.0, 1.0)
    not_last = jnp.where(place == count - 1, 0.0, 1.0)
    strip_of = lambda row: mids_ref[pl.ds(row * cols, cols), :]
    xe[pl.ds(0, cols), :] = last_ref[...]
    xe[pl.ds(cols, cols), :] = xs_ref[pl.ds(0, cols), :]
    xe[pl.ds(2 * cols, cols), :] = xs_ref[pl.ds((strips - 1) * cols, cols), :]
    got = [first_ref[...].astype(F32), second_ref[...].astype(F32)]
    above_two = shifted(jnp.where(even, got[0], got[1]) * not_first, cols)
    y = jnp.maximum(dot(last_ref[...], wr_ref[...]) + bias_ref[...], 0.0) * not_first
    above = shifted(y, cols)
    below = shifted(jnp.where(even, got[1], got[0]) * not_last, cols)
    last = strips - 1
    windows = [
        jnp.concatenate([above_two, above, strip_of(last - 1)], 0),
        jnp.concatenate([above, strip_of(0), strip_of(last)], 0),
        jnp.concatenate([strip_of(0), strip_of(1), below], 0),
    ]
    strip_block(windows, lambda at, part: xe[at, part], ws_ref, ww_ref, b_mid_ref[...], b_wid_ref[...], threes)
    outs = [
        pltpu.make_async_copy(threes.at[pl.ds(cols, cols)], three_ref.at[pl.ds(0, cols)], sem.at[0]),
        pltpu.make_async_copy(threes.at[pl.ds(2 * cols, cols)], three_ref.at[pl.ds(last * cols, cols)], sem.at[1]),
    ]
    for out in outs:
        out.start()
    for strip in range(3):
        thirds(fours, threes, we_ref, b_ent_ref[...], None if strip else not_first, strip, strip, cols, phases)

    def rows_of(row, dx):
        cut = slice(dx * s4, (dx + 1) * s4)
        if row < 1:
            return phases[pl.ds((row + 1) * half, half), cut]
        if row == last:
            return phases[pl.ds(2 * half, half), cut]
        return inner_ref[pl.ds((row - 1) * half, half), cut]

    def filter_tile(tap, pair):
        halves = []
        for j in (2 * pair, 2 * pair + 1):
            source = back_tap(tap, 2 * j)
            halves.append(rows_rolled(k2_ref[pl.ds(source * s4, s4), :], 128 * j))
        return jnp.concatenate(halves, 1)

    lhs = []
    for tap in range(9):
        dy, dx = divmod(tap, 3)
        lhs.append(jnp.concatenate([rows_of(2 * q + dy - 1, dx) for q in range(strips // 2)], 0))
    results = []
    for pair in range(s4 // 256):
        acc = b_str_ref[:, pair * 256:(pair + 1) * 256]
        for tap in range(9):
            acc = acc + dot(lhs[tap], filter_tile(tap, pair))
        results.append(jnp.maximum(acc, 0.0).astype(BF16))
    four_ref[...] = dot(jnp.concatenate(results, 1), order_ref[...]).astype(BF16)
    for out in outs:
        out.wait()


def loops(groups, count):
    at = lambda group, row: group * count + row
    pairs = []
    for group in range(groups):
        step = 1 if group % 2 == 0 else -1
        for row in range(count):
            if 0 <= row + step < count:
                pairs.append((at(group, row), at(group, row + step)))
            elif group ^ 1 < groups:
                pairs.append((at(group, row), at(group ^ 1, row)))
    return pairs, [(b, a) for a, b in pairs]


def shards(scene_map, reduce_kernel, reduce_bias, spatial_kernel, spatial_bias, widen_kernel, widen_bias,
           entry_kernel, entry_bias, stride_kernel, stride_bias):
    count = lax.axis_size("rows")
    strips, cols, wide = scene_map.shape
    mid_f, s4_f = reduce_kernel.shape[2], entry_kernel.shape[2]
    mid, s4 = mid_f * ORIENT, s4_f * ORIENT
    own, half = strips * cols, cols // 2
    hbm = pl.BlockSpec(memory_space=pl.ANY)
    vmem = pl.BlockSpec(memory_space=pltpu.VMEM)
    dma = pltpu.SemaphoreType.DMA
    limit = lambda mib: pltpu.CompilerParams(vmem_limit_bytes=mib << 20)

    pinned = lambda *arrays: [pltpu.with_memory_space_constraint(a, pltpu.HBM) for a in arrays]
    xs, last, *known = pl.pallas_call(
        load_kernel,
        out_shape=[
            pltpu.VMEM((own, wide), BF16),
            pltpu.VMEM((cols, wide), BF16),
            pltpu.VMEM((wide, mid), BF16),
            pltpu.VMEM((1, mid), F32),
            pltpu.VMEM((1, mid), F32),
            pltpu.VMEM((1, wide), F32),
            pltpu.VMEM((1, s4), F32),
            pltpu.VMEM((1, s4), F32),
            pltpu.VMEM((s4, s4), BF16),
        ],
        in_specs=[hbm] * 7,
        out_specs=[vmem] * 9,
        scratch_shapes=[
            pltpu.VMEM((ORIENT, mid_f, wide // ORIENT), BF16),
            pltpu.VMEM((1, mid_f), F32),
            pltpu.VMEM((1, mid_f), F32),
            pltpu.VMEM((1, wide // ORIENT), F32),
            pltpu.VMEM((1, s4_f), F32),
            pltpu.VMEM((1, s4_f), F32),
            dma((8,)),
        ],
        compiler_params=limit(16),
        name="load",
    )(*pinned(scene_map.reshape(own, wide), reduce_kernel.transpose(1, 2, 0), reduce_bias[None],
              spatial_bias[None], widen_bias[None], entry_bias[None], stride_bias[None]))
    w_reduce, b_reduce, b_mid, b_wid, b_ent = known[:5]
    last = lax.ppermute(last, "rows", [(i, (i + 1) % count) for i in range(count)])
    mids, first, second = pl.pallas_call(
        reducing,
        out_shape=[
            pltpu.VMEM((own, 3 * mid), BF16),
            pltpu.VMEM((cols, mid), BF16),
            pltpu.VMEM((cols, mid), BF16),
        ],
        in_specs=[vmem] * 3,
        out_specs=[vmem] * 3,
        compiler_params=limit(16),
        name="reduce",
    )(xs, w_reduce, b_reduce)
    there, back = loops(lax.axis_size("groups"), count)
    first = lax.ppermute(first, ("groups", "rows"), there)
    second = lax.ppermute(second, ("groups", "rows"), back)

    three, *kept, phases = pl.pallas_call(
        inner_kernel,
        out_shape=[
            jax.ShapeDtypeStruct((own, wide), BF16),
            pltpu.VMEM((9 * mid, mid), BF16),
            pltpu.VMEM((mid, wide), BF16),
            pltpu.VMEM((wide, s4), BF16),
            pltpu.VMEM((9 * s4, 128), BF16),
            pltpu.VMEM(((strips - 2) * half, 3 * s4), BF16),
        ],
        in_specs=[vmem] * 5 + [hbm] * 4,
        out_specs=[hbm] + [vmem] * 5,
        scratch_shapes=[
            pltpu.VMEM(spatial_kernel.shape, BF16),
            pltpu.VMEM(widen_kernel.shape, BF16),
            pltpu.VMEM((ORIENT, s4_f, wide // ORIENT), BF16),
            pltpu.VMEM(stride_kernel.shape, BF16),
            pltpu.VMEM((mid, wide // ORIENT), F32),
            pltpu.VMEM((9 * mid, 128), F32),
            pltpu.VMEM((9 * s4, 128), F32),
            pltpu.VMEM(((strips - 2) * cols, wide), BF16),
            pltpu.VMEM((s4 // 128, (strips - 2) * cols, 128), F32),
            dma((5,)),
        ],
        compiler_params=limit(28),
        name="inner",
    )(xs, mids, b_mid, b_wid, b_ent, *pinned(spatial_kernel, widen_kernel, entry_kernel.transpose(1, 2, 0), stride_kernel))

    operands = [last, first, second, xs, *known, mids, *kept, phases, three]
    three, four = pl.pallas_call(
        edge_kernel,
        out_shape=[
            jax.ShapeDtypeStruct((own, wide), BF16),
            jax.ShapeDtypeStruct((strips // 2 * half, s4), BF16),
        ],
        in_specs=[vmem] * (len(operands) - 1) + [hbm],
        out_specs=[hbm, vmem],
        input_output_aliases={len(operands) - 1: 0},
        scratch_shapes=[
            pltpu.VMEM((3 * cols, wide), BF16),
            pltpu.VMEM((3 * cols, wide), BF16),
            pltpu.VMEM((s4 // 128, 3 * cols, 128), F32),
            pltpu.VMEM((3 * half, 3 * s4), BF16),
            dma((2,)),
        ],
        compiler_params=limit(28),
        name="edge",
    )(*operands)
    return three.reshape(strips, cols, wide), four.reshape(strips // 2, half, s4)


def solution(mesh):
    rows = P(("groups", "rows"), None, None)
    return jax.shard_map(shards, mesh=mesh, in_specs=(rows,) + (P(),) * 10, out_specs=(rows, rows), check_vma=False)
```

time: 18.2 us -> 15.5 us (0.85)
  starting transfers between devices: 6.43 us -> 3.22 us
  waiting for transfers between devices: 0.01 us -> 1.27 us
  Pallas kernels: 10.8 us -> 10.1 us
    ppermute x2 -> x3, starting transfers between devices: 6.43 us -> 3.22 us  [the longest x1 2.65 us: shards(): lax.ppermute(last, 'rows', [(i, (i + 1) % count) for i in range(count)])]
    ppermute x2 -> x3, waiting for transfers between devices: 0.01 us -> 1.27 us  [the longest x1 1.26 us: shards(): second = lax.ppermute(second, ('groups', 'rows'), back)]
    pallas_call x1, Pallas kernels: 3.95 us -> 3.26 us  [shards(): pl.pallas_call(edge_kernel, out_shape=[jax.ShapeDtypeStruct((own, wide),...]
    pallas_call x1, Pallas kernels: 5.03 us -> 4.62 us  [shards(): pl.pallas_call(inner_kernel, out_shape=[jax.ShapeDtypeStruct((own, wide),...]
    pallas_call x1 -> x2, Pallas kernels: 1.84 us -> 2.22 us  [the longest x1 1.75 us: shards(): pl.pallas_call(load_kernel, out_shape=[pltpu.VMEM((own, wide), BF16), plt...]
  transfers between devices with their start and end apart: 2 -> 3, of which waited for: 0 -> 1; matrix products, arithmetic and copies ran while one was open for 0% -> 0% of each run, Pallas kernels for 28% -> 33%
where the time goes in v3:
time: 15.5 us; the launch traced here: 15.3 us
  Pallas kernels  10.1 us (65%)
  starting transfers between devices  3.22 us (21%)
  waiting for transfers between devices  1.27 us (8%)
  between operations  0.67 us (4%)
    pallas_call x1, Pallas kernels, shards(): pl.pallas_call(inner_kernel, out_shape=[jax.ShapeDtypeStruct((own, wide),...  4.62 us
    pallas_call x1, Pallas kernels, shards(): pl.pallas_call(edge_kernel, out_shape=[jax.ShapeDtypeStruct((own, wide),...  3.26 us
    ppermute x1, starting transfers between devices, shards(): lax.ppermute(last, 'rows', [(i, (i + 1) % count) for i in range(count)])  2.65 us
    pallas_call x1, Pallas kernels, shards(): pl.pallas_call(load_kernel, out_shape=[pltpu.VMEM((own, wide), BF16), plt...  1.75 us
    ppermute x1, waiting for transfers between devices, shards(): second = lax.ppermute(second, ('groups', 'rows'), back)  1.26 us
    ppermute x1, starting transfers between devices, shards(): second = lax.ppermute(second, ('groups', 'rows'), back)  0.5 us
    pallas_call x1, Pallas kernels, shards(): pl.pallas_call(reducing, out_shape=[pltpu.VMEM((own, 3 * mid), BF16), plt...  0.47 us
  transfers between devices with their start and end apart: 3, of which 1 were waited for; matrix products, arithmetic and copies ran while one was open for 0% of the time, Pallas kernels for 33%

profile of v3, /device:TPU:1, one launch (start us, length us, event | category | flops | bytes accessed | tf_op | source)
XLA Modules:
  0.0 15.3 jit_solution(9750334157214030084)
XLA Ops:
  0.6 1.7 %load.1 = (bf16[512,1024]{1,0:T(8,128)(2,1)S(1)}, bf16[128,1024]{1,0:T(8,128)(2,1)S(1)}, bf16[1024,256]{1,0:T(8,128)(2,1)S(1)}, f32[1,256]{1,0:T(1,128)S(1)}, f3...) custom-call(bf16[512,1024]{1,0:T(8,128)(2,1)} %bitcast.10, ...), custom_call_target="tpu_custom_call" | custom-call | tf_op jit(solution)/shard_map/load/pallas_call | solution.py:330
  2.4 2.7 %collective-permute-start = (bf16[128,1024]{1,0:T(8,128)(2,1)S(1)}, bf16[128,1024]{1,0:T(8,128)(2,1)S(1)}, u32[]{:S(2)}, u32[]{:S(2)}) collective-permute-start(bf16[128,1024]{1,0:T(8,128)(2,1)S(1)} %get-tuple-element.22), channel_id=1, source_target_pairs={{0,1},{1,2},{2,3},{3,4},{4,5},{5,6},{6,7},{7,8},{8,9},{9,10},{10,1... | collective-permute-start | bytes 786440 | tf_op jit(solution)/shard_map/ppermute | solution.py:359
  5.0 0.5 %reduce.1 = (bf16[512,768]{1,0:T(8,128)(2,1)S(1)}, bf16[128,256]{1,0:T(8,128)(2,1)S(1)}, bf16[128,256]{1,0:T(8,128)(2,1)S(1)}) custom-call(bf16[512,1024]{1,0:T(8,128)(2,1)S(1)} %get-tuple-element.23.xs_ref, bf16[1024,256]{1,0:T(8,128)(2,1)S(1)} %get-tuple-element.24.wr_ref, f32[1,256]{1,0:T(1,128)S(1)} %get-tuple-element.25.bias_ref), custom_call_target="tpu_custom_call" | custom-call | tf_op jit(solution)/shard_map/reduce/pallas_call | solution.py:360
  5.5 0.1 collective-permute-start.1
  5.6 0.5 %collective-permute-start.2 = (bf16[128,256]{1,0:T(8,128)(2,1)S(1)}, bf16[128,256]{1,0:T(8,128)(2,1)S(1)}, u32[]{:S(2)}, u32[]{:S(2)}) collective-permute-start(bf16[128,256]{1,0:T(8,128)(2,1)S(1)} %get-tuple-element.27), channel_id=1, source_target_pairs={{1,0},{2,1},{3,2},{4,3},{5,4},{6,5},{7,6},{8,7},{9,8},{10,9},{11,1... | collective-permute-start | bytes 196616 | tf_op jit(solution)/shard_map/ppermute | solution.py:374
  6.1 4.6 %inner.1 = (bf16[512,1024]{1,0:T(8,128)(2,1)}, bf16[2304,256]{1,0:T(8,128)(2,1)S(1)}, bf16[256,1024]{1,0:T(8,128)(2,1)S(1)}, bf16[1024,512]{1,0:T(8,128)(2,1)S(1...) custom-call(bf16[512,1024]{1,0:T(8,128)(2,1)S(1)} %get-tuple-element.23.xs_ref, ...), custom_call_target="tpu_custom_call" | custom-call | tf_op jit(solution)/shard_map/inner/pallas_call | solution.py:376
  10.7 0.0 collective-permute-done.1.first_ref
  10.7 1.3 %collective-permute-done.2.second_ref = bf16[128,256]{1,0:T(8,128)(2,1)S(1)} collective-permute-done((bf16[128,256]{1,0:T(8,128)(2,1)S(1)}, bf16[128,256]{1,0:T(8,128)(2,1)S(1)}, u32[]{:S(2)}, u32[]{:S(2)}) %collective-permute-start.2) | collective-permute-done | bytes 65568 | tf_op jit(solution)/shard_map/ppermute | solution.py:374
  12.0 0.0 collective-permute-done.last_ref
  12.0 3.3 %edge.1 = (bf16[512,1024]{1,0:T(8,128)(2,1)}, bf16[128,512]{1,0:T(8,128)(2,1)}) custom-call(bf16[128,1024]{1,0:T(8,128)(2,1)S(1)} %collective-permute-done.last_ref, bf16[128,256]{1,0:T(8,128)(2,1)S(1)} %collective-permute-done.1.first_ref, bf16[128,256]{1,0:T(8,128)(2,1)S(1)} %collective-permute-done.2.second_ref, ...), custom_call_target="tpu_custom_call", output_to_operand_aliasing={{0}: (17, {})} | custom-call | tf_op jit(solution)/shard_map/edge/pallas_call | solution.py:405
Async XLA Ops:
  2.4 9.6 %collective-permute-start = (bf16[128,1024]{1,0:T(8,128)(2,1)S(1)}, bf16[128,1024]{1,0:T(8,128)(2,1)S(1)}, u32[]{:S(2)}, u32[]{:S(2)}) collective-permute-start(bf16[128,1024]{1,0:T(8,128)(2,1)S(1)} %get-tuple-element.22), channel_id=1, source_target_pairs={{0,1},{1,2},{2,3},{3,4},{4,5},{5,6},{6,7},{7,8},{8,9},{9,10},{10,1... | collective-permute-start | bytes 786440 | tf_op jit(solution)/shard_map/ppermute | solution.py:359
  5.5 5.2 %collective-permute-start.1 = (bf16[128,256]{1,0:T(8,128)(2,1)S(1)}, bf16[128,256]{1,0:T(8,128)(2,1)S(1)}, u32[]{:S(2)}, u32[]{:S(2)}) collective-permute-start(bf16[128,256]{1,0:T(8,128)(2,1)S(1)} %get-tuple-element.26), channel_id=1, source_target_pairs={{0,1},{1,2},{2,3},{3,4},{4,5},{5,6},{6,7},{7,8},{8,9},{9,10},{10,1... | collective-permute-start | bytes 196616 | tf_op jit(solution)/shard_map/ppermute | solution.py:373
  5.6 6.4 %collective-permute-start.2 = (bf16[128,256]{1,0:T(8,128)(2,1)S(1)}, bf16[128,256]{1,0:T(8,128)(2,1)S(1)}, u32[]{:S(2)}, u32[]{:S(2)}) collective-permute-start(bf16[128,256]{1,0:T(8,128)(2,1)S(1)} %get-tuple-element.27), channel_id=1, source_target_pairs={{1,0},{2,1},{3,2},{4,3},{5,4},{6,5},{7,6},{8,7},{9,8},{10,9},{11,1... | collective-permute-start | bytes 196616 | tf_op jit(solution)/shard_map/ppermute | solution.py:374

commit v4 on v3

v4 whole, which is shorter than its diff:
```python
import functools

import jax
import jax.numpy as jnp
from jax import lax
from jax.experimental import pallas as pl
from jax.experimental.pallas import tpu as pltpu
from jax.sharding import PartitionSpec as P

ORIENT = 8
BLOCK = 128
CYCLE_TAPS = [0, 1, 2, 5, 8, 7, 6, 3]
BF16, F32 = jnp.bfloat16, jnp.float32
NT = (((1,), (1,)), ((), ()))


def back_tap(tap, turn):
    if tap == 4:
        return 4
    return CYCLE_TAPS[(CYCLE_TAPS.index(tap) - turn) % ORIENT]


def iota(shape, dim):
    return lax.broadcasted_iota(jnp.int32, shape, dim)


def dot(a, b):
    return jnp.dot(a, b, preferred_element_type=F32)


def dot_nt(a, b):
    return lax.dot_general(a, b, NT, preferred_element_type=F32)


def rows_rolled(x, by):
    by %= x.shape[0]
    if by == 0:
        return x
    return jnp.concatenate([x[x.shape[0] - by:], x[:x.shape[0] - by]], 0)


def spread(fields, first, width):
    lead = iota((fields, width), 1) + first - ORIENT * iota((fields, width), 0)
    return jnp.where(lead & -ORIENT == 0, 1.0, 0.0).astype(BF16)


def turned(blocks, block):
    lane = iota((1, blocks.shape[1]), 1)
    for bit in (1, 2, 4):
        take = jnp.broadcast_to(lane & bit, blocks.shape) != 0
        blocks = jnp.where(take, rows_rolled(blocks, bit * block), blocks)
    return blocks


def unfold_in(kernel, fields, store):
    inputs = kernel.shape[1]
    base = jnp.concatenate([kernel[(-r) % ORIENT * fields:((-r) % ORIENT + 1) * fields] for r in range(ORIENT)], 0)
    base, other = base.T, rows_rolled(base, fields).T
    for first in range(0, inputs * ORIENT, 128):
        lead = iota((128, inputs), 0) + first - ORIENT * iota((128, inputs), 1)
        hot = jnp.where(lead & -ORIENT == 0, 1.0, 0.0).astype(BF16)
        row = iota((128, fields * ORIENT), 0)
        block = jnp.where(row & 1 != 0, dot(hot, other), dot(hot, base))
        for bit in (2, 4):
            block = jnp.where(row & bit != 0, pltpu.roll(block, bit * fields, 1), block)
        store(pl.ds(first, 128), block.astype(BF16))


def bias_lanes(bias, hot):
    first = bias.astype(BF16)
    rest = bias - first.astype(F32)
    second = rest.astype(BF16)
    third = (rest - second.astype(F32)).astype(BF16)
    parts = [dot(jnp.broadcast_to(p, (16,) + p.shape[1:]), hot)[:1] for p in (first, second, third)]
    return parts[0] + parts[1] + parts[2]


def fetched(pairs, sem, first=0):
    copies = [pltpu.make_async_copy(source, target, sem.at[first + n]) for n, (source, target) in enumerate(pairs)]
    for copy in copies:
        copy.start()
    return copies


def shifted(y, cols):
    col = iota(y.shape, 0)
    left = jnp.where(col == 0, 0.0, pltpu.roll(y, 1, 0))
    right = jnp.where(col == cols - 1, 0.0, pltpu.roll(y, cols - 1, 0))
    return jnp.concatenate([left, y, right], 1).astype(BF16)


def tile_hot(fields, width):
    return jnp.where((iota((fields, width), 1) - iota((fields, width), 0)) & (fields - 1) == 0, 1.0, 0.0).astype(BF16)


def fetched(pairs, sem, first=0):
    copies = [pltpu.make_async_copy(source, target, sem.at[first + n]) for n, (source, target) in enumerate(pairs)]
    for copy in copies:
        copy.start()
    return copies


def load_kernel(x_hbm, br_hbm, bs_hbm, bw_hbm, be_hbm, bt_hbm,
                last_ref, b_red_ref, b_mid_ref, b_wid_ref, b_ent_ref, b_str_ref, order_ref,
                br_ref, bs_ref, bw_ref, be_ref, bt_ref, sem):
    cols, wide = last_ref.shape
    large = fetched([(x_hbm.at[pl.ds(x_hbm.shape[0] - cols, cols)], last_ref)], sem)
    small = fetched([(br_hbm, br_ref), (bs_hbm, bs_ref), (bw_hbm, bw_ref), (be_hbm, be_ref), (bt_hbm, bt_ref)], sem, 1)
    in_f, mid_f, s4_f = wide // ORIENT, br_ref.shape[1], be_ref.shape[1]
    mid, s4 = mid_f * ORIENT, s4_f * ORIENT
    shift = s4_f.bit_length() - 1
    a, b = iota((s4, s4), 0), iota((s4, s4), 1)
    order_ref[...] = jnp.where(b == (a & (s4_f - 1)) * ORIENT + (a >> shift), 1.0, 0.0).astype(BF16)
    hot_mid, hot_s4, hot_wide = tile_hot(mid_f, mid), tile_hot(s4_f, s4), spread(in_f, 0, wide)
    for copy in small:
        copy.wait()
    b_red_ref[...] = bias_lanes(br_ref[...], hot_mid)
    b_mid_ref[...] = bias_lanes(bs_ref[...], hot_mid)
    b_ent_ref[...] = bias_lanes(be_ref[...], hot_s4)
    b_str_ref[...] = bias_lanes(bt_ref[...], hot_s4)
    b_wid_ref[...] = bias_lanes(bw_ref[...], hot_wide)
    large[0].wait()


def reducing(xs_ref, kr_ref, bias_ref, wr_ref, mids_ref, first_ref, second_ref):
    cols = first_ref.shape[0]
    strips = xs_ref.shape[0] // cols
    even = lax.axis_index("rows") % 2 == 0
    _, mid_f, in_f = kr_ref.shape
    def keep(at, block):
        wr_ref[at, :] = block
    unfold_in(kr_ref[...].reshape(mid_f * ORIENT, in_f), mid_f, keep)
    y = jnp.maximum(dot(xs_ref[...], wr_ref[...]) + bias_ref[...], 0.0)
    parts = [y[row * cols:(row + 1) * cols] for row in range(strips)]
    first_ref[...] = jnp.where(even, parts[strips - 2], parts[0]).astype(BF16)
    second_ref[...] = jnp.where(even, parts[0], parts[strips - 2]).astype(BF16)
    for row, part in enumerate(parts):
        mids_ref[pl.ds(row * cols, cols), :] = shifted(part, cols)


def strip_blocks(jobs, ws_ref, ww_ref, b_mid, b_wid, threes):
    twos = []
    for windows, _, _ in jobs:
        depth = windows[0].shape[1]
        acc = b_mid
        for dy in range(3):
            acc = acc + dot(windows[dy], ws_ref[pl.ds(dy * depth, depth), :])
        twos.append(jnp.maximum(acc, 0.0).astype(BF16))
    for two, (_, x, at) in zip(twos, jobs):
        for first in range(0, ww_ref.shape[1], 256):
            part = slice(first, first + 256)
            z = x(part).astype(F32) + dot(two, ww_ref[:, part]) + b_wid[:, part]
            threes[at, part] = jnp.maximum(z, 0.0).astype(BF16)


def entry_part(threes, we_ref, b_ent, at, first):
    cut = slice(first, first + 256)
    return jnp.maximum(dot(threes[at, :], we_ref[:, cut]) + b_ent[:, cut], 0.0)


def thirds(fours, threes, we_ref, b_ent, scales, cols, phases):
    half = cols // 2
    s4 = we_ref.shape[1]
    for first in range(0, s4, 256):
        for strip, scale in enumerate(scales):
            f = entry_part(threes, we_ref, b_ent, pl.ds(strip * cols, cols), first)
            if scale is not None:
                f = f * scale
            for g in range(2):
                fours[first // 128 + g, pl.ds(strip * cols, cols), :] = f[:, g * 128:(g + 1) * 128]
    col = iota((half, 128), 0)
    for strip in range(len(scales)):
        for g in range(s4 // 128):
            even = fours[g, pl.ds(strip * cols, half, stride=2), :]
            odd = fours[g, pl.ds(strip * cols + 1, half, stride=2), :]
            moved = jnp.where(col == 0, 0.0, pltpu.roll(odd, 1, 0))
            for n, value in enumerate((moved, even, odd)):
                phases[pl.ds(strip * half, half), pl.ds(n * s4 + g * 128, 128)] = value.astype(BF16)


def inner_kernel(xs_ref, mids_ref, b_mid_ref, b_wid_ref, b_ent_ref, ks_v, kw_ref, ke_ref, kt_v,
                 three_ref, ws_ref, ww_ref, we_ref, k2_ref, phases_ref,
                 flat_w, flat_s, flat_t, threes, fours, sem):
    in_f, s4_f, mid_f = ke_ref.shape[2], ke_ref.shape[1], kw_ref.shape[0]
    wide, s4, mid = in_f * ORIENT, s4_f * ORIENT, mid_f * ORIENT
    cols = phases_ref.shape[0]
    strips = xs_ref.shape[0] // cols
    flat_w[...] = kw_ref[...].astype(F32).reshape(mid, in_f)
    kw = jnp.concatenate([flat_w[pl.ds(u, mid_f, stride=ORIENT), :] for u in range(ORIENT)], 0).astype(BF16)
    for first in range(0, wide, 256):
        ww_ref[:, pl.ds(first, 256)] = turned(dot(kw, spread(in_f, first, 256)), mid_f).astype(BF16)
    def keep(at, block):
        we_ref[at, :] = block
    unfold_in(ke_ref[...].reshape(s4, in_f), s4_f, keep)

    lane = iota((1, 128), 1)
    for tap in range(9):
        flat_s[pl.ds(tap * mid, mid), :mid_f] = ks_v[tap].astype(F32).reshape(mid, mid_f)
    piece = lambda tap, u: flat_s[pl.ds(tap * mid + u % ORIENT, mid_f, stride=ORIENT), :]
    low = jnp.broadcast_to(lane < mid_f, (mid_f, 128))
    half = jnp.broadcast_to(lane < 2 * mid_f, (mid_f, 128))
    pairs = {}
    for tap in range(9):
        for u in range(ORIENT):
            pairs[tap, u] = jnp.where(low, piece(tap, u), pltpu.roll(piece(back_tap(tap, 1), u - 1), mid_f, 1))
    for tap in range(9):
        for u in range(ORIENT):
            quad = jnp.where(half, pairs[tap, u], pltpu.roll(pairs[back_tap(tap, 2), (u - 2) % ORIENT], 2 * mid_f, 1)).astype(BF16)
            ws_ref[pl.ds(tap * mid + u * mid_f, mid_f), :128] = quad
            ahead = back_tap(tap, -4)
            ws_ref[pl.ds(ahead * mid + (u + 4) % ORIENT * mid_f, mid_f), 128:] = quad

    for tap in range(9):
        flat_t[pl.ds(tap * s4, s4), :s4_f] = kt_v[tap].astype(F32).reshape(s4, s4_f)
    piece_t = lambda tap, u: flat_t[pl.ds(tap * s4 + u % ORIENT, s4_f, stride=ORIENT), :]
    low_t = jnp.broadcast_to(lane < s4_f, (s4_f, 128))
    for tap in range(9):
        for u in range(ORIENT):
            pair = jnp.where(low_t, piece_t(tap, u), pltpu.roll(piece_t(back_tap(tap, 1), u - 1), s4_f, 1))
            k2_ref[pl.ds(tap * s4 + u * s4_f, s4_f), :] = pair.astype(BF16)

    inner = strips - 2
    strip_of = lambda row: mids_ref[pl.ds(row * cols, cols), :]
    jobs = [([strip_of(row + dy) for dy in range(3)], lambda part, row=row: xs_ref[pl.ds((row + 1) * cols, cols), part],
             pl.ds(row * cols, cols)) for row in range(inner)]
    strip_blocks(jobs, ws_ref, ww_ref, b_mid_ref[...], b_wid_ref[...], threes)
    out = pltpu.make_async_copy(threes, three_ref.at[pl.ds(cols, inner * cols)], sem.at[0])
    out.start()
    thirds(fours, threes, we_ref, b_ent_ref[...], [None] * inner, cols, phases_ref)
    out.wait()


def edge_kernel(last_ref, first_ref, second_ref, xs_ref, wr_ref, bias_ref, b_mid_ref, b_wid_ref, b_ent_ref, b_str_ref, order_ref,
                mids_ref, ws_ref, ww_ref, we_ref, k2_ref, inner_ref, kept_ref,
                three_ref, four_ref, halo, threes, fours, phases, sem):
    place, count = lax.axis_index("rows"), lax.axis_size("rows")
    even = lax.axis_index("rows") % 2 == 0
    cols = first_ref.shape[0]
    half = cols // 2
    strips = xs_ref.shape[0] // cols
    wide, mid, s4 = xs_ref.shape[1], wr_ref.shape[1], we_ref.shape[1]
    not_first = jnp.where(place == 0, 0.0, 1.0)
    not_last = jnp.where(place == count - 1, 0.0, 1.0)
    strip_of = lambda row: mids_ref[pl.ds(row * cols, cols), :]
    got = [first_ref[...].astype(F32), second_ref[...].astype(F32)]
    last = strips - 1
    b_mid, b_wid, b_ent = b_mid_ref[...], b_wid_ref[...], b_ent_ref[...]
    halo[0] = shifted(jnp.where(even, got[1], got[0]) * not_first, cols)
    halo[2] = shifted(jnp.where(even, got[0], got[1]) * not_last, cols)
    halo[1] = shifted(jnp.maximum(dot(last_ref[...], wr_ref[...]) + bias_ref[...], 0.0) * not_first, cols)
    below = [strip_of(0), strip_of(1)] if last > 1 else [strip_of(0), halo[2]]
    jobs = [
        ([halo[0], halo[1], strip_of(0)], lambda part: last_ref[:, part], pl.ds(0, cols)),
        ([halo[1], *below], lambda part: xs_ref[pl.ds(0, cols), part], pl.ds(cols, cols)),
        ([strip_of(last - 1), strip_of(last), halo[2]], lambda part: xs_ref[pl.ds(last * cols, cols), part], pl.ds(2 * cols, cols)),
    ]
    strip_blocks(jobs, ws_ref, ww_ref, b_mid, b_wid, threes)
    outs = [
        pltpu.make_async_copy(threes.at[pl.ds(cols, cols)], three_ref.at[pl.ds(0, cols)], sem.at[0]),
        pltpu.make_async_copy(threes.at[pl.ds(2 * cols, cols)], three_ref.at[pl.ds(last * cols, cols)], sem.at[1]),
    ]
    for out in outs:
        out.start()
    thirds(fours, threes, we_ref, b_ent, [not_first, None, None], cols, phases)

    def rows_of(row, dx):
        cut = slice(dx * s4, (dx + 1) * s4)
        if row < 1:
            return phases[pl.ds((row + 1) * half, half), cut]
        if row == last:
            return phases[pl.ds(2 * half, half), cut]
        return inner_ref[pl.ds((row - 1) * half, half), cut]

    def filter_tile(tap, pair):
        halves = []
        for j in (2 * pair, 2 * pair + 1):
            source = back_tap(tap, 2 * j)
            halves.append(rows_rolled(k2_ref[pl.ds(source * s4, s4), :], 128 * j))
        return jnp.concatenate(halves, 1)

    lhs = []
    for tap in range(9):
        dy, dx = divmod(tap, 3)
        lhs.append(jnp.concatenate([rows_of(2 * q + dy - 1, dx) for q in range(strips // 2)], 0))
    results = []
    for pair in range(s4 // 256):
        acc = b_str_ref[:, pair * 256:(pair + 1) * 256]
        for tap in range(9):
            acc = acc + dot(lhs[tap], filter_tile(tap, pair))
        results.append(jnp.maximum(acc, 0.0).astype(BF16))
    four_ref[...] = dot(jnp.concatenate(results, 1), order_ref[...]).astype(BF16)
    for out in outs:
        out.wait()


def swaps(groups, count):
    near, far = [], []
    for group in range(groups):
        for row in range(count):
            me = group * count + row
            if row ^ 1 < count:
                near.append((me, group * count + (row ^ 1)))
            other = row - 1 if row % 2 == 0 else row + 1
            if 0 <= other < count:
                far.append((me, group * count + other))
            elif group ^ 1 < groups:
                far.append((me, (group ^ 1) * count + row))
    return near, far


def shards(scene_map, reduce_kernel, reduce_bias, spatial_kernel, spatial_bias, widen_kernel, widen_bias,
           entry_kernel, entry_bias, stride_kernel, stride_bias):
    count = lax.axis_size("rows")
    strips, cols, wide = scene_map.shape
    mid_f, s4_f = reduce_kernel.shape[2], entry_kernel.shape[2]
    mid, s4 = mid_f * ORIENT, s4_f * ORIENT
    own, half = strips * cols, cols // 2
    hbm = pl.BlockSpec(memory_space=pl.ANY)
    vmem = pl.BlockSpec(memory_space=pltpu.VMEM)
    dma = pltpu.SemaphoreType.DMA
    limit = lambda mib: pltpu.CompilerParams(vmem_limit_bytes=mib << 20)

    pinned = lambda *arrays: [pltpu.with_memory_space_constraint(a, pltpu.HBM) for a in arrays]
    scene = scene_map.reshape(own, wide)
    work = lambda flops: pl.CostEstimate(flops=flops, transcendentals=0, bytes_accessed=1 << 22)
    last, b_reduce, *known = pl.pallas_call(
        load_kernel,
        out_shape=[
            pltpu.VMEM((cols, wide), BF16),
            pltpu.VMEM((1, mid), F32),
            pltpu.VMEM((1, mid), F32),
            pltpu.VMEM((1, wide), F32),
            pltpu.VMEM((1, s4), F32),
            pltpu.VMEM((1, s4), F32),
            pltpu.VMEM((s4, s4), BF16),
        ],
        in_specs=[hbm] * 6,
        out_specs=[vmem] * 7,
        scratch_shapes=[
            pltpu.VMEM((1, mid_f), F32),
            pltpu.VMEM((1, mid_f), F32),
            pltpu.VMEM((1, wide // ORIENT), F32),
            pltpu.VMEM((1, s4_f), F32),
            pltpu.VMEM((1, s4_f), F32),
            dma((6,)),
        ],
        cost_estimate=work(2 * 10**9),
        compiler_params=limit(16),
        name="load",
    )(*pinned(scene, reduce_bias[None], spatial_bias[None], widen_bias[None], entry_bias[None], stride_bias[None]))
    b_mid, b_wid, b_ent = known[:3]
    last = lax.ppermute(last, "rows", [(i, (i + 1) % count) for i in range(count)])
    w_reduce, mids, first, second = pl.pallas_call(
        reducing,
        out_shape=[
            pltpu.VMEM((wide, mid), BF16),
            pltpu.VMEM((own, 3 * mid), BF16),
            pltpu.VMEM((cols, mid), BF16),
            pltpu.VMEM((cols, mid), BF16),
        ],
        in_specs=[vmem] * 3,
        out_specs=[vmem] * 4,
        cost_estimate=work(2 * 10**9),
        compiler_params=limit(16),
        name="reduce",
    )(scene, reduce_kernel.transpose(1, 2, 0), b_reduce)
    near, far = swaps(lax.axis_size("groups"), count)
    first = lax.ppermute(first, ("groups", "rows"), near)
    second = lax.ppermute(second, ("groups", "rows"), far)

    three, *kept, phases = pl.pallas_call(
        inner_kernel,
        out_shape=[
            jax.ShapeDtypeStruct((own, wide), BF16),
            pltpu.VMEM((9 * mid, mid), BF16),
            pltpu.VMEM((mid, wide), BF16),
            pltpu.VMEM((wide, s4), BF16),
            pltpu.VMEM((9 * s4, 128), BF16),
            pltpu.VMEM(((strips - 2) * half, 3 * s4), BF16),
        ],
        in_specs=[vmem] * 9,
        out_specs=[hbm] + [vmem] * 5,
        scratch_shapes=[
            pltpu.VMEM((mid, wide // ORIENT), F32),
            pltpu.VMEM((9 * mid, 128), F32),
            pltpu.VMEM((9 * s4, 128), F32),
            pltpu.VMEM(((strips - 2) * cols, wide), BF16),
            pltpu.VMEM((s4 // 128, (strips - 2) * cols, 128), F32),
            dma((1,)),
        ],
        compiler_params=limit(28),
        name="inner",
    )(scene, mids, b_mid, b_wid, b_ent, spatial_kernel, widen_kernel, entry_kernel.transpose(1, 2, 0), stride_kernel)

    operands = [last, first, second, scene, w_reduce, b_reduce, *known, mids, *kept, phases, three]
    three, four = pl.pallas_call(
        edge_kernel,
        out_shape=[
            jax.ShapeDtypeStruct((own, wide), BF16),
            jax.ShapeDtypeStruct((strips // 2 * half, s4), BF16),
        ],
        in_specs=[vmem] * (len(operands) - 1) + [hbm],
        out_specs=[hbm, vmem],
        input_output_aliases={len(operands) - 1: 0},
        scratch_shapes=[
            pltpu.VMEM((3, cols, 3 * mid), BF16),
            pltpu.VMEM((3 * cols, wide), BF16),
            pltpu.VMEM((s4 // 128, 3 * cols, 128), F32),
            pltpu.VMEM((3 * half, 3 * s4), BF16),
            dma((2,)),
        ],
        compiler_params=limit(28),
        name="edge",
    )(*operands)
    return three.reshape(strips, cols, wide), four.reshape(strips // 2, half, s4)


def solution(mesh):
    rows = P(("groups", "rows"), None, None)
    return jax.shard_map(shards, mesh=mesh, in_specs=(rows,) + (P(),) * 10, out_specs=(rows, rows), check_vma=False)
```

time: 15.5 us -> 14.9 us (0.961)
  Pallas kernels: 10.1 us -> 8.93 us
  starting transfers between devices: 3.22 us -> 4.38 us
  waiting for transfers between devices: 1.27 us -> 0.7 us
    ppermute x2, starting transfers between devices: 0.57 us -> 1.72 us  [the longest x1 1.65 us: shards(): second = lax.ppermute(second, ('groups', 'rows'), far)]
    pallas_call x1, Pallas kernels: 4.62 us -> 3.49 us  [shards(): pl.pallas_call(inner_kernel, out_shape=[jax.ShapeDtypeStruct((own, wide),...]
    ppermute x2, waiting for transfers between devices: 1.27 us -> 0.7 us  [the longest x1 0.69 us: shards(): second = lax.ppermute(second, ('groups', 'rows'), far)]
  transfers between devices with their start and end apart: 3 -> 3, of which waited for: 1 -> 1; matrix products, arithmetic and copies ran while one was open for 0% -> 0% of each run, Pallas kernels for 33% -> 30%
where the time goes in v4:
time: 14.9 us; the launch traced here: 14.8 us
  Pallas kernels  8.93 us (60%)
  starting transfers between devices  4.38 us (29%)
  between operations  0.72 us (5%)
  waiting for transfers between devices  0.7 us (5%)
    pallas_call x1, Pallas kernels, shards(): pl.pallas_call(inner_kernel, out_shape=[jax.ShapeDtypeStruct((own, wide),...  3.49 us
    pallas_call x1, Pallas kernels, shards(): pl.pallas_call(edge_kernel, out_shape=[jax.ShapeDtypeStruct((own, wide),...  3.25 us
    ppermute x1, starting transfers between devices, shards(): lax.ppermute(last, 'rows', [(i, (i + 1) % count) for i in range(count)])  2.65 us
    ppermute x1, starting transfers between devices, shards(): second = lax.ppermute(second, ('groups', 'rows'), far)  1.65 us
    pallas_call x1, Pallas kernels, shards(): pl.pallas_call(load_kernel, out_shape=[pltpu.VMEM((cols, wide), BF16), pl...  1.24 us
    pallas_call x1, Pallas kernels, shards(): pl.pallas_call(reducing, out_shape=[pltpu.VMEM((wide, mid), BF16), pltpu....  0.96 us
    ppermute x1, waiting for transfers between devices, shards(): second = lax.ppermute(second, ('groups', 'rows'), far)  0.69 us
  transfers between devices with their start and end apart: 3, of which 1 were waited for; matrix products, arithmetic and copies ran while one was open for 0% of the time, Pallas kernels for 30%

profile of v4, /device:TPU:1, one launch (start us, length us, event | category | flops | bytes accessed | tf_op | source)
XLA Modules:
  0.0 14.8 jit_solution(11746173803591394515)
XLA Ops:
  0.6 0.0 copy-start
  0.6 0.0 copy-start.5
  0.7 1.2 %load.1 = (bf16[128,1024]{1,0:T(8,128)(2,1)S(1)}, f32[1,256]{1,0:T(1,128)S(1)}, f32[1,256]{1,0:T(1,128)S(1)}, f32[1,1024]{1,0:T(1,128)S(1)}, f32[1,512]{1,0:T(1,...) custom-call(bf16[512,1024]{1,0:T(8,128)(2,1)} %bitcast.10, f32[1,32]{1,0:T(1,128)} %bitcast.18, ...), custom_call_target="tpu_custom_call" | custom-call | flops 2000000000 | bytes 4194304 | tf_op jit(solution)/shard_map/load/pallas_call | solution.py:326
  1.9 2.7 %collective-permute-start = (bf16[128,1024]{1,0:T(8,128)(2,1)S(1)}, bf16[128,1024]{1,0:T(8,128)(2,1)S(1)}, u32[]{:S(2)}, u32[]{:S(2)}) collective-permute-start(bf16[128,1024]{1,0:T(8,128)(2,1)S(1)} %get-tuple-element.21), channel_id=1, source_target_pairs={{0,1},{1,2},{2,3},{3,4},{4,5},{5,6},{6,7},{7,8},{8,9},{9,10},{10,1... | collective-permute-start | bytes 786440 | tf_op jit(solution)/shard_map/ppermute | solution.py:352
  4.6 0.0 copy-done
  4.6 0.0 copy-done.5
  4.6 0.0 copy-start.1
  4.6 0.0 copy-start.2
  4.6 0.0 copy-start.3
  4.6 0.0 copy-start.4
  4.6 1.0 %reduce.1 = (bf16[1024,256]{1,0:T(8,128)(2,1)S(1)}, bf16[512,768]{1,0:T(8,128)(2,1)S(1)}, bf16[128,256]{1,0:T(8,128)(2,1)S(1)}, bf16[128,256]{1,0:T(8,128)(2,1)S(1)}) custom-call(bf16[512,1024]{1,0:T(8,128)(2,1)S(1)} %bitcast.11, bf16[8,32,128]{2,1,0:T(8,128)(2,1)S(1)} %bitcast.15, f32[1,256]{1,0:T(1,128)S(1)} %get-tuple-element.22.bias_ref), custom_call_target="tpu_custom_call" | custom-call | flops 2000000000 | bytes 4194304 | tf_op jit(solution)/shard_map/reduce/pallas_call | solution.py:353
  5.6 0.1 collective-permute-start.1
  5.6 1.7 %collective-permute-start.2 = (bf16[128,256]{1,0:T(8,128)(2,1)S(1)}, bf16[128,256]{1,0:T(8,128)(2,1)S(1)}, u32[]{:S(2)}, u32[]{:S(2)}) collective-permute-start(bf16[128,256]{1,0:T(8,128)(2,1)S(1)} %get-tuple-element.24), channel_id=1, source_target_pairs={{0,16},{1,2},{2,1},{3,4},{4,3},{5,6},{6,5},{7,8},{8,7},{9,10},{10,... | collective-permute-start | bytes 196616 | tf_op jit(solution)/shard_map/ppermute | solution.py:369
  7.3 0.0 copy-done.1
  7.3 0.0 copy-done.2
  7.3 0.0 copy-done.3
  7.3 0.0 copy-done.4
  7.3 3.5 %inner.1 = (bf16[512,1024]{1,0:T(8,128)(2,1)}, bf16[2304,256]{1,0:T(8,128)(2,1)S(1)}, bf16[256,1024]{1,0:T(8,128)(2,1)S(1)}, bf16[1024,512]{1,0:T(8,128)(2,1)S(1...) custom-call(bf16[512,1024]{1,0:T(8,128)(2,1)S(1)} %bitcast.12, ...), custom_call_target="tpu_custom_call" | custom-call | tf_op jit(solution)/shard_map/inner/pallas_call | solution.py:371
  10.8 0.0 collective-permute-done.1.first_ref
  10.8 0.7 %collective-permute-done.2.second_ref = bf16[128,256]{1,0:T(8,128)(2,1)S(1)} collective-permute-done((bf16[128,256]{1,0:T(8,128)(2,1)S(1)}, bf16[128,256]{1,0:T(8,128)(2,1)S(1)}, u32[]{:S(2)}, u32[]{:S(2)}) %collective-permute-start.2) | collective-permute-done | bytes 65568 | tf_op jit(solution)/shard_map/ppermute | solution.py:369
  11.5 0.0 collective-permute-done.last_ref
  11.5 3.2 %edge.1 = (bf16[512,1024]{1,0:T(8,128)(2,1)}, bf16[128,512]{1,0:T(8,128)(2,1)}) custom-call(bf16[128,1024]{1,0:T(8,128)(2,1)S(1)} %collective-permute-done.last_ref, bf16[128,256]{1,0:T(8,128)(2,1)S(1)} %collective-permute-done.1.first_ref, bf16[128,256]{1,0:T(8,128)(2,1)S(1)} %collective-permute-done.2.second_ref, ...), custom_call_target="tpu_custom_call", output_to_operand_aliasing={{0}: (17, {})} | custom-call | tf_op jit(solution)/shard_map/edge/pallas_call | solution.py:396
Async XLA Ops:
  0.6 3.9 %copy-start = (bf16[4,128,1024]{2,1,0:T(8,128)(2,1)S(1)}, bf16[4,128,1024]{2,1,0:T(8,128)(2,1)}, u32[]{:S(2)}) copy-start(bf16[4,128,1024]{2,1,0:T(8,128)(2,1)} %param.11) | copy-start | bytes 3145732
  0.6 3.9 %copy-start.5 = (bf16[128,8,32]{0,2,1:T(8,128)(2,1)S(1)}, bf16[128,8,32]{0,2,1:T(8,128)(2,1)}, u32[]{:S(2)}) copy-start(bf16[128,8,32]{0,2,1:T(8,128)(2,1)} %param.12) | copy-start | bytes 196612
  1.9 9.6 %collective-permute-start = (bf16[128,1024]{1,0:T(8,128)(2,1)S(1)}, bf16[128,1024]{1,0:T(8,128)(2,1)S(1)}, u32[]{:S(2)}, u32[]{:S(2)}) collective-permute-start(bf16[128,1024]{1,0:T(8,128)(2,1)S(1)} %get-tuple-element.21), channel_id=1, source_target_pairs={{0,1},{1,2},{2,3},{3,4},{4,5},{5,6},{6,7},{7,8},{8,9},{9,10},{10,1... | collective-permute-start | bytes 786440 | tf_op jit(solution)/shard_map/ppermute | solution.py:352
  4.6 2.7 %copy-start.1 = (bf16[9,64,8,64]{3,2,1,0:T(8,128)(2,1)S(1)}, bf16[9,64,8,64]{3,2,1,0:T(8,128)(2,1)}, u32[]{:S(2)}) copy-start(bf16[9,64,8,64]{3,2,1,0:T(8,128)(2,1)} %kt_v.1) | copy-start | bytes 1769476
  4.6 2.7 %copy-start.2 = (bf16[9,32,8,32]{3,2,1,0:T(8,128)(2,1)S(1)}, bf16[9,32,8,32]{3,2,1,0:T(8,128)(2,1)}, u32[]{:S(2)}) copy-start(bf16[9,32,8,32]{3,2,1,0:T(8,128)(2,1)} %ks_v.1) | copy-start | bytes 442372
  4.6 2.7 %copy-start.3 = (bf16[128,8,64]{0,2,1:T(8,128)(2,1)S(1)}, bf16[128,8,64]{0,2,1:T(8,128)(2,1)}, u32[]{:S(2)}) copy-start(bf16[128,8,64]{0,2,1:T(8,128)(2,1)} %param.18) | copy-start | bytes 393220
  4.6 2.7 %copy-start.4 = (bf16[32,8,128]{2,1,0:T(8,128)(2,1)S(1)}, bf16[32,8,128]{2,1,0:T(8,128)(2,1)}, u32[]{:S(2)}) copy-start(bf16[32,8,128]{2,1,0:T(8,128)(2,1)} %kw_ref.1) | copy-start | bytes 196612
  5.6 5.2 %collective-permute-start.1 = (bf16[128,256]{1,0:T(8,128)(2,1)S(1)}, bf16[128,256]{1,0:T(8,128)(2,1)S(1)}, u32[]{:S(2)}, u32[]{:S(2)}) collective-permute-start(bf16[128,256]{1,0:T(8,128)(2,1)S(1)} %get-tuple-element.23), channel_id=1, source_target_pairs={{0,1},{1,0},{2,3},{3,2},{4,5},{5,4},{6,7},{7,6},{8,9},{9,8},{10,11... | collective-permute-start | bytes 196616 | tf_op jit(solution)/shard_map/ppermute | solution.py:368
  5.6 5.9 %collective-permute-start.2 = (bf16[128,256]{1,0:T(8,128)(2,1)S(1)}, bf16[128,256]{1,0:T(8,128)(2,1)S(1)}, u32[]{:S(2)}, u32[]{:S(2)}) collective-permute-start(bf16[128,256]{1,0:T(8,128)(2,1)S(1)} %get-tuple-element.24), channel_id=1, source_target_pairs={{0,16},{1,2},{2,1},{3,4},{4,3},{5,6},{6,5},{7,8},{8,7},{9,10},{10,... | collective-permute-start | bytes 196616 | tf_op jit(solution)/shard_map/ppermute | solution.py:369

commit v5 on v4

--- a/solution.py
+++ b/solution.py
@@ -100,29 +100,16 @@
     return copies
 
 
-def load_kernel(x_hbm, br_hbm, bs_hbm, bw_hbm, be_hbm, bt_hbm,
-                last_ref, b_red_ref, b_mid_ref, b_wid_ref, b_ent_ref, b_str_ref, order_ref,
-                br_ref, bs_ref, bw_ref, be_ref, bt_ref, sem):
-    cols, wide = last_ref.shape
-    large = fetched([(x_hbm.at[pl.ds(x_hbm.shape[0] - cols, cols)], last_ref)], sem)
-    small = fetched([(br_hbm, br_ref), (bs_hbm, bs_ref), (bw_hbm, bw_ref), (be_hbm, be_ref), (bt_hbm, bt_ref)], sem, 1)
-    in_f, mid_f, s4_f = wide // ORIENT, br_ref.shape[1], be_ref.shape[1]
-    mid, s4 = mid_f * ORIENT, s4_f * ORIENT
-    shift = s4_f.bit_length() - 1
-    a, b = iota((s4, s4), 0), iota((s4, s4), 1)
-    order_ref[...] = jnp.where(b == (a & (s4_f - 1)) * ORIENT + (a >> shift), 1.0, 0.0).astype(BF16)
-    hot_mid, hot_s4, hot_wide = tile_hot(mid_f, mid), tile_hot(s4_f, s4), spread(in_f, 0, wide)
-    for copy in small:
+def load_kernel(x_hbm, last_ref, sem):
+    cols = last_ref.shape[0]
+    cut, parts = cols // 4, []
+    for n in range(4):
+        parts.append((x_hbm.at[pl.ds(x_hbm.shape[0] - cols + n * cut, cut)], last_ref.at[pl.ds(n * cut, cut)]))
+    for copy in fetched(parts, sem):
         copy.wait()
-    b_red_ref[...] = bias_lanes(br_ref[...], hot_mid)
-    b_mid_ref[...] = bias_lanes(bs_ref[...], hot_mid)
-    b_ent_ref[...] = bias_lanes(be_ref[...], hot_s4)
-    b_str_ref[...] = bias_lanes(bt_ref[...], hot_s4)
-    b_wid_ref[...] = bias_lanes(bw_ref[...], hot_wide)
-    large[0].wait()
-
-
-def reducing(xs_ref, kr_ref, bias_ref, wr_ref, mids_ref, first_ref, second_ref):
+
+
+def reducing(xs_ref, kr_ref, br_ref, wr_ref, bias_ref, mids_ref, first_ref, second_ref):
     cols = first_ref.shape[0]
     strips = xs_ref.shape[0] // cols
     even = lax.axis_index("rows") % 2 == 0
@@ -130,21 +117,27 @@
     def keep(at, block):
         wr_ref[at, :] = block
     unfold_in(kr_ref[...].reshape(mid_f * ORIENT, in_f), mid_f, keep)
-    y = jnp.maximum(dot(xs_ref[...], wr_ref[...]) + bias_ref[...], 0.0)
+    bias = bias_lanes(br_ref[...], tile_hot(mid_f, mid_f * ORIENT))
+    bias_ref[...] = bias
+    y = jnp.maximum(dot(xs_ref[...], wr_ref[...]) + bias, 0.0)
     parts = [y[row * cols:(row + 1) * cols] for row in range(strips)]
-    first_ref[...] = jnp.where(even, parts[strips - 2], parts[0]).astype(BF16)
-    second_ref[...] = jnp.where(even, parts[0], parts[strips - 2]).astype(BF16)
+    first_ref[...] = jnp.where(even, parts[0], parts[strips - 2]).astype(BF16)
+    second_ref[...] = jnp.where(even, parts[strips - 2], parts[0]).astype(BF16)
     for row, part in enumerate(parts):
         mids_ref[pl.ds(row * cols, cols), :] = shifted(part, cols)
 
 
-def strip_blocks(jobs, ws_ref, ww_ref, b_mid, b_wid, threes):
+def column_sum(windows, ws_ref, acc):
+    for dy, window in windows.items():
+        depth = window.shape[1]
+        acc = acc + dot(window, ws_ref[pl.ds(dy * depth, depth), :])
+    return acc
+
+
+def strip_blocks(jobs, ws_ref, ww_ref, b_wid, threes):
     twos = []
-    for windows, _, _ in jobs:
-        depth = windows[0].shape[1]
-        acc = b_mid
-        for dy in range(3):
-            acc = acc + dot(windows[dy], ws_ref[pl.ds(dy * depth, depth), :])
+    for (windows, start), _, _ in jobs:
+        acc = column_sum(windows, ws_ref, start)
         twos.append(jnp.maximum(acc, 0.0).astype(BF16))
     for two, (_, x, at) in zip(twos, jobs):
         for first in range(0, ww_ref.shape[1], 256):
@@ -178,8 +171,8 @@
                 phases[pl.ds(strip * half, half), pl.ds(n * s4 + g * 128, 128)] = value.astype(BF16)
 
 
-def inner_kernel(xs_ref, mids_ref, b_mid_ref, b_wid_ref, b_ent_ref, ks_v, kw_ref, ke_ref, kt_v,
-                 three_ref, ws_ref, ww_ref, we_ref, k2_ref, phases_ref,
+def inner_kernel(xs_ref, mids_ref, bs_ref, bw_ref, be_ref, bt_ref, ks_v, kw_ref, ke_ref, kt_v,
+                 three_ref, ws_ref, ww_ref, we_ref, k2_ref, b_mid_ref, b_wid_ref, b_ent_ref, b_str_ref, order_ref, begun_ref, phases_ref,
                  flat_w, flat_s, flat_t, threes, fours, sem):
     in_f, s4_f, mid_f = ke_ref.shape[2], ke_ref.shape[1], kw_ref.shape[0]
     wide, s4, mid = in_f * ORIENT, s4_f * ORIENT, mid_f * ORIENT
@@ -187,8 +180,17 @@
     strips = xs_ref.shape[0] // cols
     flat_w[...] = kw_ref[...].astype(F32).reshape(mid, in_f)
     kw = jnp.concatenate([flat_w[pl.ds(u, mid_f, stride=ORIENT), :] for u in range(ORIENT)], 0).astype(BF16)
+    shift = s4_f.bit_length() - 1
+    a, b = iota((s4, s4), 0), iota((s4, s4), 1)
+    order_ref[...] = jnp.where(b == (a & (s4_f - 1)) * ORIENT + (a >> shift), 1.0, 0.0).astype(BF16)
+    hot_s4 = tile_hot(s4_f, s4)
+    b_mid_ref[...] = bias_lanes(bs_ref[...], tile_hot(mid_f, mid))
+    b_ent_ref[...] = bias_lanes(be_ref[...], hot_s4)
+    b_str_ref[...] = bias_lanes(bt_ref[...], hot_s4)
     for first in range(0, wide, 256):
-        ww_ref[:, pl.ds(first, 256)] = turned(dot(kw, spread(in_f, first, 256)), mid_f).astype(BF16)
+        hot = spread(in_f, first, 256)
+        ww_ref[:, pl.ds(first, 256)] = turned(dot(kw, hot), mid_f).astype(BF16)
+        b_wid_ref[:, pl.ds(first, 256)] = bias_lanes(bw_ref[...], hot)
     def keep(at, block):
         we_ref[at, :] = block
     unfold_in(ke_ref[...].reshape(s4, in_f), s4_f, keep)
@@ -221,17 +223,20 @@
 
     inner = strips - 2
     strip_of = lambda row: mids_ref[pl.ds(row * cols, cols), :]
-    jobs = [([strip_of(row + dy) for dy in range(3)], lambda part, row=row: xs_ref[pl.ds((row + 1) * cols, cols), part],
+    b_mid = b_mid_ref[...]
+    jobs = [(({dy: strip_of(row + dy) for dy in range(3)}, b_mid), lambda part, row=row: xs_ref[pl.ds((row + 1) * cols, cols), part],
              pl.ds(row * cols, cols)) for row in range(inner)]
-    strip_blocks(jobs, ws_ref, ww_ref, b_mid_ref[...], b_wid_ref[...], threes)
+    strip_blocks(jobs, ws_ref, ww_ref, b_wid_ref[...], threes)
     out = pltpu.make_async_copy(threes, three_ref.at[pl.ds(cols, inner * cols)], sem.at[0])
     out.start()
+    begun_ref[0] = column_sum({1: strip_of(0), 2: strip_of(1)}, ws_ref, b_mid)
+    begun_ref[1] = column_sum({0: strip_of(inner), 1: strip_of(inner + 1)}, ws_ref, b_mid)
     thirds(fours, threes, we_ref, b_ent_ref[...], [None] * inner, cols, phases_ref)
     out.wait()
 
 
-def edge_kernel(last_ref, first_ref, second_ref, xs_ref, wr_ref, bias_ref, b_mid_ref, b_wid_ref, b_ent_ref, b_str_ref, order_ref,
-                mids_ref, ws_ref, ww_ref, we_ref, k2_ref, inner_ref, kept_ref,
+def edge_kernel(last_ref, first_ref, second_ref, xs_ref, wr_ref, bias_ref, mids_ref, ws_ref, ww_ref, we_ref, k2_ref,
+                b_mid_ref, b_wid_ref, b_ent_ref, b_str_ref, order_ref, begun_ref, inner_ref, kept_ref,
                 three_ref, four_ref, halo, threes, fours, phases, sem):
     place, count = lax.axis_index("rows"), lax.axis_size("rows")
     even = lax.axis_index("rows") % 2 == 0
@@ -245,16 +250,15 @@
     got = [first_ref[...].astype(F32), second_ref[...].astype(F32)]
     last = strips - 1
     b_mid, b_wid, b_ent = b_mid_ref[...], b_wid_ref[...], b_ent_ref[...]
-    halo[0] = shifted(jnp.where(even, got[1], got[0]) * not_first, cols)
-    halo[2] = shifted(jnp.where(even, got[0], got[1]) * not_last, cols)
+    halo[0] = shifted(jnp.where(even, got[0], got[1]) * not_first, cols)
+    halo[2] = shifted(jnp.where(even, got[1], got[0]) * not_last, cols)
     halo[1] = shifted(jnp.maximum(dot(last_ref[...], wr_ref[...]) + bias_ref[...], 0.0) * not_first, cols)
-    below = [strip_of(0), strip_of(1)] if last > 1 else [strip_of(0), halo[2]]
     jobs = [
-        ([halo[0], halo[1], strip_of(0)], lambda part: last_ref[:, part], pl.ds(0, cols)),
-        ([halo[1], *below], lambda part: xs_ref[pl.ds(0, cols), part], pl.ds(cols, cols)),
-        ([strip_of(last - 1), strip_of(last), halo[2]], lambda part: xs_ref[pl.ds(last * cols, cols), part], pl.ds(2 * cols, cols)),
+        (({0: halo[0], 1: halo[1], 2: strip_of(0)}, b_mid), lambda part: last_ref[:, part], pl.ds(0, cols)),
+        (({0: halo[1]}, begun_ref[0]), lambda part: xs_ref[pl.ds(0, cols), part], pl.ds(cols, cols)),
+        (({2: halo[2]}, begun_ref[1]), lambda part: xs_ref[pl.ds(last * cols, cols), part], pl.ds(2 * cols, cols)),
     ]
-    strip_blocks(jobs, ws_ref, ww_ref, b_mid, b_wid, threes)
+    strip_blocks(jobs, ws_ref, ww_ref, b_wid, threes)
     outs = [
         pltpu.make_async_copy(threes.at[pl.ds(cols, cols)], three_ref.at[pl.ds(0, cols)], sem.at[0]),
         pltpu.make_async_copy(threes.at[pl.ds(2 * cols, cols)], three_ref.at[pl.ds(last * cols, cols)], sem.at[1]),
@@ -323,50 +327,35 @@
     pinned = lambda *arrays: [pltpu.with_memory_space_constraint(a, pltpu.HBM) for a in arrays]
     scene = scene_map.reshape(own, wide)
     work = lambda flops: pl.CostEstimate(flops=flops, transcendentals=0, bytes_accessed=1 << 22)
-    last, b_reduce, *known = pl.pallas_call(
+    last = pl.pallas_call(
         load_kernel,
-        out_shape=[
-            pltpu.VMEM((cols, wide), BF16),
-            pltpu.VMEM((1, mid), F32),
-            pltpu.VMEM((1, mid), F32),
-            pltpu.VMEM((1, wide), F32),
-            pltpu.VMEM((1, s4), F32),
-            pltpu.VMEM((1, s4), F32),
-            pltpu.VMEM((s4, s4), BF16),
-        ],
-        in_specs=[hbm] * 6,
-        out_specs=[vmem] * 7,
-        scratch_shapes=[
-            pltpu.VMEM((1, mid_f), F32),
-            pltpu.VMEM((1, mid_f), F32),
-            pltpu.VMEM((1, wide // ORIENT), F32),
-            pltpu.VMEM((1, s4_f), F32),
-            pltpu.VMEM((1, s4_f), F32),
-            dma((6,)),
-        ],
+        out_shape=pltpu.VMEM((cols, wide), BF16),
+        in_specs=[hbm],
+        out_specs=vmem,
+        scratch_shapes=[dma((4,))],
         cost_estimate=work(2 * 10**9),
         compiler_params=limit(16),
         name="load",
-    )(*pinned(scene, reduce_bias[None], spatial_bias[None], widen_bias[None], entry_bias[None], stride_bias[None]))
-    b_mid, b_wid, b_ent = known[:3]
+    )(*pinned(scene))
     last = lax.ppermute(last, "rows", [(i, (i + 1) % count) for i in range(count)])
-    w_reduce, mids, first, second = pl.pallas_call(
+    w_reduce, b_reduce, mids, first, second = pl.pallas_call(
         reducing,
         out_shape=[
             pltpu.VMEM((wide, mid), BF16),
+            pltpu.VMEM((1, mid), F32),
             pltpu.VMEM((own, 3 * mid), BF16),
             pltpu.VMEM((cols, mid), BF16),
             pltpu.VMEM((cols, mid), BF16),
         ],
         in_specs=[vmem] * 3,
-        out_specs=[vmem] * 4,
+        out_specs=[vmem] * 5,
         cost_estimate=work(2 * 10**9),
         compiler_params=limit(16),
         name="reduce",
-    )(scene, reduce_kernel.transpose(1, 2, 0), b_reduce)
+    )(scene, reduce_kernel.transpose(1, 2, 0), reduce_bias[None])
     near, far = swaps(lax.axis_size("groups"), count)
-    first = lax.ppermute(first, ("groups", "rows"), near)
-    second = lax.ppermute(second, ("groups", "rows"), far)
+    first = lax.ppermute(first, ("groups", "rows"), far)
+    second = lax.ppermute(second, ("groups", "rows"), near)
 
     three, *kept, phases = pl.pallas_call(
         inner_kernel,
@@ -376,10 +365,16 @@
             pltpu.VMEM((mid, wide), BF16),
             pltpu.VMEM((wide, s4), BF16),
             pltpu.VMEM((9 * s4, 128), BF16),
+            pltpu.VMEM((1, mid), F32),
+            pltpu.VMEM((1, wide), F32),
+            pltpu.VMEM((1, s4), F32),
+            pltpu.VMEM((1, s4), F32),
+            pltpu.VMEM((s4, s4), BF16),
+            pltpu.VMEM((2, cols, mid), F32),
             pltpu.VMEM(((strips - 2) * half, 3 * s4), BF16),
         ],
-        in_specs=[vmem] * 9,
-        out_specs=[hbm] + [vmem] * 5,
+        in_specs=[vmem] * 10,
+        out_specs=[hbm] + [vmem] * 11,
         scratch_shapes=[
             pltpu.VMEM((mid, wide // ORIENT), F32),
             pltpu.VMEM((9 * mid, 128), F32),
@@ -390,9 +385,9 @@
         ],
         compiler_params=limit(28),
         name="inner",
-    )(scene, mids, b_mid, b_wid, b_ent, spatial_kernel, widen_kernel, entry_kernel.transpose(1, 2, 0), stride_kernel)
-
-    operands = [last, first, second, scene, w_reduce, b_reduce, *known, mids, *kept, phases, three]
+    )(scene, mids, spatial_bias[None], widen_bias[None], entry_bias[None], stride_bias[None], spatial_kernel, widen_kernel, entry_kernel.transpose(1, 2, 0), stride_kernel)
+
+    operands = [last, first, second, scene, w_reduce, b_reduce, mids, *kept, phases, three]
     three, four = pl.pallas_call(
         edge_kernel,
         out_shape=[

time: 14.9 us -> 14.6 us (0.980)
  starting transfers between devices: 4.38 us -> 3.33 us
  Pallas kernels: 8.93 us -> 9.76 us
  waiting for transfers between devices: 0.7 us -> 0.44 us
    pallas_call x1, Pallas kernels: 3.49 us -> 4.71 us  [shards(): pl.pallas_call(inner_kernel, out_shape=[jax.ShapeDtypeStruct((own, wide),...]
    ppermute x2, starting transfers between devices: 1.72 us -> 0.68 us  [the longest x1 0.43 us: shards(): second = lax.ppermute(second, ('groups', 'rows'), near)]
    ppermute x2, waiting for transfers between devices: 0.7 us -> 0.44 us  [the longest x1 0.44 us: shards(): first = lax.ppermute(first, ('groups', 'rows'), far)]
    pallas_call x1, Pallas kernels: 3.25 us -> 3.04 us  [shards(): pl.pallas_call(edge_kernel, out_shape=[jax.ShapeDtypeStruct((own, wide),...]
    pallas_call x1, Pallas kernels: 1.24 us -> 1.06 us  [shards(): pl.pallas_call(load_kernel, out_shape=pltpu.VMEM((cols, wide), BF16), in_...]
  transfers between devices with their start and end apart: 3 -> 3, of which waited for: 1 -> 1; matrix products, arithmetic and copies ran while one was open for 0% -> 0% of each run, Pallas kernels for 30% -> 39%
where the time goes in v5:
time: 14.6 us; the launch traced here: 14.4 us
  Pallas kernels  9.76 us (67%)
  starting transfers between devices  3.33 us (23%)
  between operations  0.78 us (5%)
  waiting for transfers between devices  0.44 us (3%)
    pallas_call x1, Pallas kernels, shards(): pl.pallas_call(inner_kernel, out_shape=[jax.ShapeDtypeStruct((own, wide),...  4.71 us
    pallas_call x1, Pallas kernels, shards(): pl.pallas_call(edge_kernel, out_shape=[jax.ShapeDtypeStruct((own, wide),...  3.04 us
    ppermute x1, starting transfers between devices, shards(): lax.ppermute(last, 'rows', [(i, (i + 1) % count) for i in range(count)])  2.65 us
    pallas_call x1, Pallas kernels, shards(): pl.pallas_call(load_kernel, out_shape=pltpu.VMEM((cols, wide), BF16), in_...  1.06 us
    pallas_call x1, Pallas kernels, shards(): pl.pallas_call(reducing, out_shape=[pltpu.VMEM((wide, mid), BF16), pltpu....  0.95 us
    ppermute x1, waiting for transfers between devices, shards(): first = lax.ppermute(first, ('groups', 'rows'), far)  0.44 us
    ppermute x1, starting transfers between devices, shards(): second = lax.ppermute(second, ('groups', 'rows'), near)  0.43 us
  transfers between devices with their start and end apart: 3, of which 1 were waited for; matrix products, arithmetic and copies ran while one was open for 0% of the time, Pallas kernels for 39%

profile of v5, /device:TPU:1, one launch (start us, length us, event | category | flops | bytes accessed | tf_op | source)
XLA Modules:
  0.0 14.4 jit_solution(8516188611591495488)
XLA Ops:
  0.6 0.0 copy-start
  0.6 0.0 copy-start.9
  0.6 0.0 copy-start.10
  0.7 1.1 %load.1 = bf16[128,1024]{1,0:T(8,128)(2,1)S(1)} custom-call(bf16[512,1024]{1,0:T(8,128)(2,1)} %bitcast.10), custom_call_target="tpu_custom_call" | custom-call | flops 2000000000 | bytes 4194304 | tf_op jit(solution)/shard_map/load/pallas_call | solution.py:330
  1.7 2.7 %collective-permute-start = (bf16[128,1024]{1,0:T(8,128)(2,1)S(1)}, bf16[128,1024]{1,0:T(8,128)(2,1)S(1)}, u32[]{:S(2)}, u32[]{:S(2)}) collective-permute-start(bf16[128,1024]{1,0:T(8,128)(2,1)S(1)} %load.1), channel_id=1, source_target_pairs={{0,1},{1,2},{2,3},{3,4},{4,5},{5,6},{6,7},{7,8},{8,9},{9,10},{10,1... | collective-permute-start | bytes 786440 | tf_op jit(solution)/shard_map/ppermute | solution.py:340
  4.4 0.0 copy-done
  4.4 0.0 copy-done.9
  4.4 0.0 copy-start.2
  4.4 0.0 copy-start.3
  4.4 0.0 copy-start.4
  4.4 0.0 copy-start.5
  4.4 0.0 copy-start.6
  4.5 0.0 copy-start.7
  4.5 0.0 copy-start.8
  4.5 1.0 %reduce.1 = (bf16[1024,256]{1,0:T(8,128)(2,1)S(1)}, f32[1,256]{1,0:T(1,128)S(1)}, bf16[512,768]{1,0:T(8,128)(2,1)S(1)}, bf16[128,256]{1,0:T(8,128)(2,1)S(1)}, bf16[128,256]{1,0:T(8,128)(2,1)S(1)}) custom-call(bf16[512,1024]{1,0:T(8,128)(2,1)S(1)} %bitcast.11, bf16[8,32,128]{2,1,0:T(8,128)(2,1)S(1)} %bitcast.19, f32[1,32]{1,0:T(1,128)S(1)} %bitcast.20), custom_call_target="tpu_custom_call" | custom-call | flops 2000000000 | bytes 4194304 | tf_op jit(solution)/shard_map/reduce/pallas_call | solution.py:341
  5.4 0.2 %collective-permute-start.1 = (bf16[128,256]{1,0:T(8,128)(2,1)S(1)}, bf16[128,256]{1,0:T(8,128)(2,1)S(1)}, u32[]{:S(2)}, u32[]{:S(2)}) collective-permute-start(bf16[128,256]{1,0:T(8,128)(2,1)S(1)} %get-tuple-element.21), channel_id=1, source_target_pairs={{0,16},{1,2},{2,1},{3,4},{4,3},{5,6},{6,5},{7,8},{8,7},{9,10},{10,... | collective-permute-start | bytes 196616 | tf_op jit(solution)/shard_map/ppermute | solution.py:357
  5.7 0.4 %collective-permute-start.2 = (bf16[128,256]{1,0:T(8,128)(2,1)S(1)}, bf16[128,256]{1,0:T(8,128)(2,1)S(1)}, u32[]{:S(2)}, u32[]{:S(2)}) collective-permute-start(bf16[128,256]{1,0:T(8,128)(2,1)S(1)} %get-tuple-element.22), channel_id=1, source_target_pairs={{0,1},{1,0},{2,3},{3,2},{4,5},{5,4},{6,7},{7,6},{8,9},{9,8},{10,11... | collective-permute-start | bytes 196616 | tf_op jit(solution)/shard_map/ppermute | solution.py:358
  6.1 0.0 copy-done.2
  6.1 0.0 copy-done.4
  6.2 4.7 %inner.1 = (bf16[512,1024]{1,0:T(8,128)(2,1)}, bf16[2304,256]{1,0:T(8,128)(2,1)S(1)}, bf16[256,1024]{1,0:T(8,128)(2,1)S(1)}, bf16[1024,512]{1,0:T(8,128)(2,1)S(1...) custom-call(bf16[512,1024]{1,0:T(8,128)(2,1)S(1)} %bitcast.12, ...), custom_call_target="tpu_custom_call" | custom-call | tf_op jit(solution)/shard_map/inner/pallas_call | solution.py:360
  10.9 0.4 %collective-permute-done.1.first_ref = bf16[128,256]{1,0:T(8,128)(2,1)S(1)} collective-permute-done((bf16[128,256]{1,0:T(8,128)(2,1)S(1)}, bf16[128,256]{1,0:T(8,128)(2,1)S(1)}, u32[]{:S(2)}, u32[]{:S(2)}) %collective-permute-start.1) | collective-permute-done | bytes 65568 | tf_op jit(solution)/shard_map/ppermute | solution.py:357
  11.3 0.0 collective-permute-done.2.second_ref
  11.3 0.0 collective-permute-done.last_ref
  11.3 3.0 %edge.1 = (bf16[512,1024]{1,0:T(8,128)(2,1)}, bf16[128,512]{1,0:T(8,128)(2,1)}) custom-call(bf16[128,1024]{1,0:T(8,128)(2,1)S(1)} %collective-permute-done.last_ref, bf16[128,256]{1,0:T(8,128)(2,1)S(1)} %collective-permute-done.1.first_ref, bf16[128,256]{1,0:T(8,128)(2,1)S(1)} %collective-permute-done.2.second_ref, ...), custom_call_target="tpu_custom_call", output_to_operand_aliasing={{0}: (18, {})} | custom-call | tf_op jit(solution)/shard_map/edge/pallas_call | solution.py:391
  (8 shorter events, 0.0 us)
Async XLA Ops:
  0.6 3.8 %copy-start = (bf16[4,128,1024]{2,1,0:T(8,128)(2,1)S(1)}, bf16[4,128,1024]{2,1,0:T(8,128)(2,1)}, u32[]{:S(2)}) copy-start(bf16[4,128,1024]{2,1,0:T(8,128)(2,1)} %param.11) | copy-start | bytes 3145732
  0.6 3.7 %copy-start.9 = (bf16[128,8,32]{0,2,1:T(8,128)(2,1)S(1)}, bf16[128,8,32]{0,2,1:T(8,128)(2,1)}, u32[]{:S(2)}) copy-start(bf16[128,8,32]{0,2,1:T(8,128)(2,1)} %param.12) | copy-start | bytes 196612
  0.6 3.7 %copy-start.10 = (f32[32]{0:T(128)S(1)}, f32[32]{0:T(128)}, u32[]{:S(2)}) copy-start(f32[32]{0:T(128)} %param.13) | copy-start | bytes 388
  1.7 9.6 %collective-permute-start = (bf16[128,1024]{1,0:T(8,128)(2,1)S(1)}, bf16[128,1024]{1,0:T(8,128)(2,1)S(1)}, u32[]{:S(2)}, u32[]{:S(2)}) collective-permute-start(bf16[128,1024]{1,0:T(8,128)(2,1)S(1)} %load.1), channel_id=1, source_target_pairs={{0,1},{1,2},{2,3},{3,4},{4,5},{5,6},{6,7},{7,8},{8,9},{9,10},{10,1... | collective-permute-start | bytes 786440 | tf_op jit(solution)/shard_map/ppermute | solution.py:340
  4.4 1.7 %copy-start.1 = (bf16[9,64,8,64]{3,2,1,0:T(8,128)(2,1)S(1)}, bf16[9,64,8,64]{3,2,1,0:T(8,128)(2,1)}, u32[]{:S(2)}) copy-start(bf16[9,64,8,64]{3,2,1,0:T(8,128)(2,1)} %kt_v.1) | copy-start | bytes 1769476
  4.4 1.7 %copy-start.2 = (bf16[9,32,8,32]{3,2,1,0:T(8,128)(2,1)S(1)}, bf16[9,32,8,32]{3,2,1,0:T(8,128)(2,1)}, u32[]{:S(2)}) copy-start(bf16[9,32,8,32]{3,2,1,0:T(8,128)(2,1)} %ks_v.1) | copy-start | bytes 442372
  4.4 1.7 %copy-start.3 = (bf16[128,8,64]{0,2,1:T(8,128)(2,1)S(1)}, bf16[128,8,64]{0,2,1:T(8,128)(2,1)}, u32[]{:S(2)}) copy-start(bf16[128,8,64]{0,2,1:T(8,128)(2,1)} %param.18) | copy-start | bytes 393220
  4.4 1.7 %copy-start.4 = (bf16[32,8,128]{2,1,0:T(8,128)(2,1)S(1)}, bf16[32,8,128]{2,1,0:T(8,128)(2,1)}, u32[]{:S(2)}) copy-start(bf16[32,8,128]{2,1,0:T(8,128)(2,1)} %kw_ref.1) | copy-start | bytes 196612
  4.4 1.7 %copy-start.5 = (f32[32]{0:T(128)S(1)}, f32[32]{0:T(128)}, u32[]{:S(2)}) copy-start(f32[32]{0:T(128)} %param.15) | copy-start | bytes 388
  4.4 1.7 %copy-start.6 = (f32[128]{0:T(128)S(1)}, f32[128]{0:T(128)}, u32[]{:S(2)}) copy-start(f32[128]{0:T(128)} %param.17) | copy-start | bytes 1540
  4.5 1.7 %copy-start.7 = (f32[64]{0:T(128)S(1)}, f32[64]{0:T(128)}, u32[]{:S(2)}) copy-start(f32[64]{0:T(128)} %param.19) | copy-start | bytes 772
  4.5 1.7 %copy-start.8 = (f32[64]{0:T(128)S(1)}, f32[64]{0:T(128)}, u32[]{:S(2)}) copy-start(f32[64]{0:T(128)} %param.21) | copy-start | bytes 772
  5.4 5.9 %collective-permute-start.1 = (bf16[128,256]{1,0:T(8,128)(2,1)S(1)}, bf16[128,256]{1,0:T(8,128)(2,1)S(1)}, u32[]{:S(2)}, u32[]{:S(2)}) collective-permute-start(bf16[128,256]{1,0:T(8,128)(2,1)S(1)} %get-tuple-element.21), channel_id=1, source_target_pairs={{0,16},{1,2},{2,1},{3,4},{4,3},{5,6},{6,5},{7,8},{8,7},{9,10},{10,... | collective-permute-start | bytes 196616 | tf_op jit(solution)/shard_map/ppermute | solution.py:357
  5.7 5.6 %collective-permute-start.2 = (bf16[128,256]{1,0:T(8,128)(2,1)S(1)}, bf16[128,256]{1,0:T(8,128)(2,1)S(1)}, u32[]{:S(2)}, u32[]{:S(2)}) collective-permute-start(bf16[128,256]{1,0:T(8,128)(2,1)S(1)} %get-tuple-element.22), channel_id=1, source_target_pairs={{0,1},{1,0},{2,3},{3,2},{4,5},{5,4},{6,7},{7,6},{8,9},{9,8},{10,11... | collective-permute-start | bytes 196616 | tf_op jit(solution)/shard_map/ppermute | solution.py:358

commit v6 on v5

--- a/solution.py
+++ b/solution.py
@@ -102,11 +102,9 @@
 
 def load_kernel(x_hbm, last_ref, sem):
     cols = last_ref.shape[0]
-    cut, parts = cols // 4, []
-    for n in range(4):
-        parts.append((x_hbm.at[pl.ds(x_hbm.shape[0] - cols + n * cut, cut)], last_ref.at[pl.ds(n * cut, cut)]))
-    for copy in fetched(parts, sem):
-        copy.wait()
+    copy = pltpu.make_async_copy(x_hbm.at[pl.ds(x_hbm.shape[0] - cols, cols)], last_ref, sem)
+    copy.start()
+    copy.wait()
 
 
 def reducing(xs_ref, kr_ref, br_ref, wr_ref, bias_ref, mids_ref, first_ref, second_ref):
@@ -127,17 +125,13 @@
         mids_ref[pl.ds(row * cols, cols), :] = shifted(part, cols)
 
 
-def column_sum(windows, ws_ref, acc):
-    for dy, window in windows.items():
-        depth = window.shape[1]
-        acc = acc + dot(window, ws_ref[pl.ds(dy * depth, depth), :])
-    return acc
-
-
-def strip_blocks(jobs, ws_ref, ww_ref, b_wid, threes):
+def strip_blocks(jobs, ws_ref, ww_ref, b_mid, b_wid, threes):
     twos = []
-    for (windows, start), _, _ in jobs:
-        acc = column_sum(windows, ws_ref, start)
+    for windows, _, _ in jobs:
+        depth = windows[0].shape[1]
+        acc = b_mid
+        for dy in range(3):
+            acc = acc + dot(windows[dy], ws_ref[pl.ds(dy * depth, depth), :])
         twos.append(jnp.maximum(acc, 0.0).astype(BF16))
     for two, (_, x, at) in zip(twos, jobs):
         for first in range(0, ww_ref.shape[1], 256):
@@ -172,7 +166,7 @@
 
 
 def inner_kernel(xs_ref, mids_ref, bs_ref, bw_ref, be_ref, bt_ref, ks_v, kw_ref, ke_ref, kt_v,
-                 three_ref, ws_ref, ww_ref, we_ref, k2_ref, b_mid_ref, b_wid_ref, b_ent_ref, b_str_ref, order_ref, begun_ref, phases_ref,
+                 three_ref, ws_ref, ww_ref, we_ref, k2_ref, b_mid_ref, b_wid_ref, b_ent_ref, b_str_ref, order_ref, phases_ref,
                  flat_w, flat_s, flat_t, threes, fours, sem):
     in_f, s4_f, mid_f = ke_ref.shape[2], ke_ref.shape[1], kw_ref.shape[0]
     wide, s4, mid = in_f * ORIENT, s4_f * ORIENT, mid_f * ORIENT
@@ -223,21 +217,18 @@
 
     inner = strips - 2
     strip_of = lambda row: mids_ref[pl.ds(row * cols, cols), :]
-    b_mid = b_mid_ref[...]
-    jobs = [(({dy: strip_of(row + dy) for dy in range(3)}, b_mid), lambda part, row=row: xs_ref[pl.ds((row + 1) * cols, cols), part],
+    jobs = [([strip_of(row + dy) for dy in range(3)], lambda part, row=row: xs_ref[pl.ds((row + 1) * cols, cols), part],
              pl.ds(row * cols, cols)) for row in range(inner)]
-    strip_blocks(jobs, ws_ref, ww_ref, b_wid_ref[...], threes)
+    strip_blocks(jobs, ws_ref, ww_ref, b_mid_ref[...], b_wid_ref[...], threes)
     out = pltpu.make_async_copy(threes, three_ref.at[pl.ds(cols, inner * cols)], sem.at[0])
     out.start()
-    begun_ref[0] = column_sum({1: strip_of(0), 2: strip_of(1)}, ws_ref, b_mid)
-    begun_ref[1] = column_sum({0: strip_of(inner), 1: strip_of(inner + 1)}, ws_ref, b_mid)
     thirds(fours, threes, we_ref, b_ent_ref[...], [None] * inner, cols, phases_ref)
     out.wait()
 
 
-def edge_kernel(last_ref, first_ref, second_ref, xs_ref, wr_ref, bias_ref, mids_ref, ws_ref, ww_ref, we_ref, k2_ref,
-                b_mid_ref, b_wid_ref, b_ent_ref, b_str_ref, order_ref, begun_ref, inner_ref, kept_ref,
-                three_ref, four_ref, halo, threes, fours, phases, sem):
+def edge_kernel(last_ref, beside_ref, first_ref, second_ref, xs_ref, wr_ref, bias_ref, mids_ref, ws_ref, ww_ref, we_ref, k2_ref,
+                b_mid_ref, b_wid_ref, b_ent_ref, b_str_ref, order_ref, inner_ref, kept_ref,
+                three_ref, four_ref, halo, line, threes, fours, phases, sem):
     place, count = lax.axis_index("rows"), lax.axis_size("rows")
     even = lax.axis_index("rows") % 2 == 0
     cols = first_ref.shape[0]
@@ -247,18 +238,20 @@
     not_first = jnp.where(place == 0, 0.0, 1.0)
     not_last = jnp.where(place == count - 1, 0.0, 1.0)
     strip_of = lambda row: mids_ref[pl.ds(row * cols, cols), :]
+    line[...] = jnp.where(even, last_ref[...], beside_ref[...])
     got = [first_ref[...].astype(F32), second_ref[...].astype(F32)]
     last = strips - 1
     b_mid, b_wid, b_ent = b_mid_ref[...], b_wid_ref[...], b_ent_ref[...]
     halo[0] = shifted(jnp.where(even, got[0], got[1]) * not_first, cols)
     halo[2] = shifted(jnp.where(even, got[1], got[0]) * not_last, cols)
-    halo[1] = shifted(jnp.maximum(dot(last_ref[...], wr_ref[...]) + bias_ref[...], 0.0) * not_first, cols)
+    halo[1] = shifted(jnp.maximum(dot(line[...], wr_ref[...]) + bias_ref[...], 0.0) * not_first, cols)
+    below = [strip_of(0), strip_of(1)] if last > 1 else [strip_of(0), halo[2]]
     jobs = [
-        (({0: halo[0], 1: halo[1], 2: strip_of(0)}, b_mid), lambda part: last_ref[:, part], pl.ds(0, cols)),
-        (({0: halo[1]}, begun_ref[0]), lambda part: xs_ref[pl.ds(0, cols), part], pl.ds(cols, cols)),
-        (({2: halo[2]}, begun_ref[1]), lambda part: xs_ref[pl.ds(last * cols, cols), part], pl.ds(2 * cols, cols)),
+        ([halo[0], halo[1], strip_of(0)], lambda part: line[:, part], pl.ds(0, cols)),
+        ([halo[1], *below], lambda part: xs_ref[pl.ds(0, cols), part], pl.ds(cols, cols)),
+        ([strip_of(last - 1), strip_of(last), halo[2]], lambda part: xs_ref[pl.ds(last * cols, cols), part], pl.ds(2 * cols, cols)),
     ]
-    strip_blocks(jobs, ws_ref, ww_ref, b_wid, threes)
+    strip_blocks(jobs, ws_ref, ww_ref, b_mid, b_wid, threes)
     outs = [
         pltpu.make_async_copy(threes.at[pl.ds(cols, cols)], three_ref.at[pl.ds(0, cols)], sem.at[0]),
         pltpu.make_async_copy(threes.at[pl.ds(2 * cols, cols)], three_ref.at[pl.ds(last * cols, cols)], sem.at[1]),
@@ -312,6 +305,16 @@
     return near, far
 
 
+def odd_down(count):
+    if count < 8 or count % 4:
+        return [(i, (i + 1) % count) for i in range(count)]
+    pairs = {i: i + 1 for i in range(count - 1)}
+    for i in range(2, count - 4, 4):
+        pairs[i] = i - 3 if i > 2 else 0
+    pairs[count - 1] = count - 5
+    return sorted(pairs.items())
+
+
 def shards(scene_map, reduce_kernel, reduce_bias, spatial_kernel, spatial_bias, widen_kernel, widen_bias,
            entry_kernel, entry_bias, stride_kernel, stride_bias):
     count = lax.axis_size("rows")
@@ -332,12 +335,14 @@
         out_shape=pltpu.VMEM((cols, wide), BF16),
         in_specs=[hbm],
         out_specs=vmem,
-        scratch_shapes=[dma((4,))],
+        scratch_shapes=[dma],
         cost_estimate=work(2 * 10**9),
         compiler_params=limit(16),
         name="load",
     )(*pinned(scene))
-    last = lax.ppermute(last, "rows", [(i, (i + 1) % count) for i in range(count)])
+    near, far = swaps(lax.axis_size("groups"), count)
+    beside = lax.ppermute(last, ("groups", "rows"), near)
+    last = lax.ppermute(last, "rows", odd_down(count))
     w_reduce, b_reduce, mids, first, second = pl.pallas_call(
         reducing,
         out_shape=[
@@ -353,7 +358,6 @@
         compiler_params=limit(16),
         name="reduce",
     )(scene, reduce_kernel.transpose(1, 2, 0), reduce_bias[None])
-    near, far = swaps(lax.axis_size("groups"), count)
     first = lax.ppermute(first, ("groups", "rows"), far)
     second = lax.ppermute(second, ("groups", "rows"), near)
 
@@ -370,11 +374,10 @@
             pltpu.VMEM((1, s4), F32),
             pltpu.VMEM((1, s4), F32),
             pltpu.VMEM((s4, s4), BF16),
-            pltpu.VMEM((2, cols, mid), F32),
             pltpu.VMEM(((strips - 2) * half, 3 * s4), BF16),
         ],
         in_specs=[vmem] * 10,
-        out_specs=[hbm] + [vmem] * 11,
+        out_specs=[hbm] + [vmem] * 10,
         scratch_shapes=[
             pltpu.VMEM((mid, wide // ORIENT), F32),
             pltpu.VMEM((9 * mid, 128), F32),
@@ -387,7 +390,7 @@
         name="inner",
     )(scene, mids, spatial_bias[None], widen_bias[None], entry_bias[None], stride_bias[None], spatial_kernel, widen_kernel, entry_kernel.transpose(1, 2, 0), stride_kernel)
 
-    operands = [last, first, second, scene, w_reduce, b_reduce, mids, *kept, phases, three]
+    operands = [last, beside, first, second, scene, w_reduce, b_reduce, mids, *kept, phases, three]
     three, four = pl.pallas_call(
         edge_kernel,
         out_shape=[
@@ -399,6 +402,7 @@
         input_output_aliases={len(operands) - 1: 0},
         scratch_shapes=[
             pltpu.VMEM((3, cols, 3 * mid), BF16),
+            pltpu.VMEM((cols, wide), BF16),
             pltpu.VMEM((3 * cols, wide), BF16),
             pltpu.VMEM((s4 // 128, 3 * cols, 128), F32),
             pltpu.VMEM((3 * half, 3 * s4), BF16),

time: 14.6 us -> 13.7 us (0.938)
  Pallas kernels: 9.76 us -> 9.02 us
  waiting for transfers between devices: 0.44 us -> 0.01 us
  starting transfers between devices: 3.33 us -> 3.68 us
    pallas_call x1, Pallas kernels: 4.71 us -> 3.85 us  [shards(): pl.pallas_call(inner_kernel, out_shape=[jax.ShapeDtypeStruct((own, wide),...]
    ppermute x1, waiting for transfers between devices: 0.44 us -> 0.01 us  [shards(): first = lax.ppermute(first, ('groups', 'rows'), far)]
    ppermute x1, starting transfers between devices: 0.43 us -> 0.81 us  [shards(): second = lax.ppermute(second, ('groups', 'rows'), near)]
    ppermute x1 -> x2, starting transfers between devices: 2.65 us -> 2.74 us  [the longest x1 2.61 us: shards(): last = lax.ppermute(last, 'rows', odd_down(count))]
  transfers between devices with their start and end apart: 3 -> 4, of which waited for: 1 -> 0; matrix products, arithmetic and copies ran while one was open for 0% -> 0% of each run, Pallas kernels for 39% -> 35%
where the time goes in v6:
time: 13.7 us; the launch traced here: 13.6 us
  Pallas kernels  9.02 us (66%)
  starting transfers between devices  3.68 us (27%)
  between operations  0.81 us (6%)
    pallas_call x1, Pallas kernels, shards(): pl.pallas_call(inner_kernel, out_shape=[jax.ShapeDtypeStruct((own, wide),...  3.85 us
    pallas_call x1, Pallas kernels, shards(): pl.pallas_call(edge_kernel, out_shape=[jax.ShapeDtypeStruct((own, wide),...  3.18 us
    ppermute x1, starting transfers between devices, shards(): last = lax.ppermute(last, 'rows', odd_down(count))  2.61 us
    pallas_call x1, Pallas kernels, shards(): pl.pallas_call(load_kernel, out_shape=pltpu.VMEM((cols, wide), BF16), in_...  1.05 us
    pallas_call x1, Pallas kernels, shards(): pl.pallas_call(reducing, out_shape=[pltpu.VMEM((wide, mid), BF16), pltpu....  0.95 us
    ppermute x1, starting transfers between devices, shards(): second = lax.ppermute(second, ('groups', 'rows'), near)  0.81 us
  transfers between devices with their start and end apart: 4, of which 0 were waited for; matrix products, arithmetic and copies ran while one was open for 0% of the time, Pallas kernels for 35%

profile of v6, /device:TPU:1, one launch (start us, length us, event | category | flops | bytes accessed | tf_op | source)
XLA Modules:
  0.0 13.6 jit_solution(18245582041155469463)
XLA Ops:
  0.6 0.0 copy-start
  0.6 0.0 copy-start.9
  0.7 1.0 %load.1 = bf16[128,1024]{1,0:T(8,128)(2,1)S(1)} custom-call(bf16[512,1024]{1,0:T(8,128)(2,1)} %bitcast.10), custom_call_target="tpu_custom_call" | custom-call | flops 2000000000 | bytes 4194304 | tf_op jit(solution)/shard_map/load/pallas_call | solution.py:333
  1.7 0.1 collective-permute-start.1
  1.8 2.6 %collective-permute-start = (bf16[128,1024]{1,0:T(8,128)(2,1)S(1)}, bf16[128,1024]{1,0:T(8,128)(2,1)S(1)}, u32[]{:S(2)}, u32[]{:S(2)}) collective-permute-start(bf16[128,1024]{1,0:T(8,128)(2,1)S(1)} %load.1), channel_id=1, source_target_pairs={{0,1},{1,2},{2,0},{3,4},{4,5},{5,6},{6,3},{7,8},{8,9},{9,10},{10,7... | collective-permute-start | bytes 786440 | tf_op jit(solution)/shard_map/ppermute | solution.py:345
  4.5 0.0 copy-done.9
  4.5 0.0 copy-start.2
  4.5 0.0 copy-start.3
  4.5 0.0 copy-start.4
  4.5 0.0 copy-start.5
  4.5 0.0 copy-start.6
  4.5 0.0 copy-start.7
  4.5 0.0 copy-start.8
  4.6 0.9 %reduce.1 = (bf16[1024,256]{1,0:T(8,128)(2,1)S(1)}, f32[1,256]{1,0:T(1,128)S(1)}, bf16[512,768]{1,0:T(8,128)(2,1)S(1)}, bf16[128,256]{1,0:T(8,128)(2,1)S(1)}, bf16[128,256]{1,0:T(8,128)(2,1)S(1)}) custom-call(bf16[512,1024]{1,0:T(8,128)(2,1)S(1)} %bitcast.11, bf16[8,32,128]{2,1,0:T(8,128)(2,1)S(1)} %bitcast.19, f32[1,32]{1,0:T(1,128)S(1)} %bitcast.20), custom_call_target="tpu_custom_call" | custom-call | flops 2000000000 | bytes 4194304 | tf_op jit(solution)/shard_map/reduce/pallas_call | solution.py:346
  5.5 0.1 %collective-permute-start.2 = (bf16[128,256]{1,0:T(8,128)(2,1)S(1)}, bf16[128,256]{1,0:T(8,128)(2,1)S(1)}, u32[]{:S(2)}, u32[]{:S(2)}) collective-permute-start(bf16[128,256]{1,0:T(8,128)(2,1)S(1)} %get-tuple-element.20), channel_id=1, source_target_pairs={{0,16},{1,2},{2,1},{3,4},{4,3},{5,6},{6,5},{7,8},{8,7},{9,10},{10,... | collective-permute-start | bytes 196616 | tf_op jit(solution)/shard_map/ppermute | solution.py:361
  5.6 0.8 %collective-permute-start.3 = (bf16[128,256]{1,0:T(8,128)(2,1)S(1)}, bf16[128,256]{1,0:T(8,128)(2,1)S(1)}, u32[]{:S(2)}, u32[]{:S(2)}) collective-permute-start(bf16[128,256]{1,0:T(8,128)(2,1)S(1)} %get-tuple-element.21), channel_id=1, source_target_pairs={{0,1},{1,0},{2,3},{3,2},{4,5},{5,4},{6,7},{7,6},{8,9},{9,8},{10,11... | collective-permute-start | bytes 196616 | tf_op jit(solution)/shard_map/ppermute | solution.py:362
  6.5 0.0 copy-done.2
  6.5 0.0 copy-done.4
  6.5 3.9 %inner.1 = (bf16[512,1024]{1,0:T(8,128)(2,1)}, bf16[2304,256]{1,0:T(8,128)(2,1)S(1)}, bf16[256,1024]{1,0:T(8,128)(2,1)S(1)}, bf16[1024,512]{1,0:T(8,128)(2,1)S(1...) custom-call(bf16[512,1024]{1,0:T(8,128)(2,1)S(1)} %bitcast.12, ...), custom_call_target="tpu_custom_call" | custom-call | tf_op jit(solution)/shard_map/inner/pallas_call | solution.py:364
  10.4 0.0 collective-permute-done.2.first_ref
  10.4 0.0 collective-permute-done.3.second_ref
  10.4 0.0 collective-permute-done.1.beside_ref
  10.4 0.0 collective-permute-done.last_ref
  10.4 3.2 %edge.1 = (bf16[512,1024]{1,0:T(8,128)(2,1)}, bf16[128,512]{1,0:T(8,128)(2,1)}) custom-call(bf16[128,1024]{1,0:T(8,128)(2,1)S(1)} %collective-permute-done.last_ref, bf16[128,1024]{1,0:T(8,128)(2,1)S(1)} %collective-permute-done.1.beside_ref, bf16[128,256]{1,0:T(8,128)(2,1)S(1)} %collective-permute-done.2.first_ref, ...), custom_call_target="tpu_custom_call", output_to_operand_aliasing={{0}: (18, {})} | custom-call | tf_op jit(solution)/shard_map/edge/pallas_call | solution.py:394
  (10 shorter events, 0.0 us)
Async XLA Ops:
  0.6 3.8 %copy-start = (bf16[4,128,1024]{2,1,0:T(8,128)(2,1)S(1)}, bf16[4,128,1024]{2,1,0:T(8,128)(2,1)}, u32[]{:S(2)}) copy-start(bf16[4,128,1024]{2,1,0:T(8,128)(2,1)} %param.11) | copy-start | bytes 3145732
  0.6 3.8 %copy-start.9 = (bf16[128,8,32]{0,2,1:T(8,128)(2,1)S(1)}, bf16[128,8,32]{0,2,1:T(8,128)(2,1)}, u32[]{:S(2)}) copy-start(bf16[128,8,32]{0,2,1:T(8,128)(2,1)} %param.12) | copy-start | bytes 196612
  0.6 3.8 %copy-start.10 = (f32[32]{0:T(128)S(1)}, f32[32]{0:T(128)}, u32[]{:S(2)}) copy-start(f32[32]{0:T(128)} %param.13) | copy-start | bytes 388
  1.7 8.7 %collective-permute-start.1 = (bf16[128,1024]{1,0:T(8,128)(2,1)S(1)}, bf16[128,1024]{1,0:T(8,128)(2,1)S(1)}, u32[]{:S(2)}, u32[]{:S(2)}) collective-permute-start(bf16[128,1024]{1,0:T(8,128)(2,1)S(1)} %load.1), channel_id=1, source_target_pairs={{0,1},{1,0},{2,3},{3,2},{4,5},{5,4},{6,7},{7,6},{8,9},{9,8},{10,11... | collective-permute-start | bytes 786440 | tf_op jit(solution)/shard_map/ppermute | solution.py:344
  1.8 8.6 %collective-permute-start = (bf16[128,1024]{1,0:T(8,128)(2,1)S(1)}, bf16[128,1024]{1,0:T(8,128)(2,1)S(1)}, u32[]{:S(2)}, u32[]{:S(2)}) collective-permute-start(bf16[128,1024]{1,0:T(8,128)(2,1)S(1)} %load.1), channel_id=1, source_target_pairs={{0,1},{1,2},{2,0},{3,4},{4,5},{5,6},{6,3},{7,8},{8,9},{9,10},{10,7... | collective-permute-start | bytes 786440 | tf_op jit(solution)/shard_map/ppermute | solution.py:345
  4.5 2.0 %copy-start.1 = (bf16[9,64,8,64]{3,2,1,0:T(8,128)(2,1)S(1)}, bf16[9,64,8,64]{3,2,1,0:T(8,128)(2,1)}, u32[]{:S(2)}) copy-start(bf16[9,64,8,64]{3,2,1,0:T(8,128)(2,1)} %kt_v.1) | copy-start | bytes 1769476
  4.5 2.0 %copy-start.2 = (bf16[9,32,8,32]{3,2,1,0:T(8,128)(2,1)S(1)}, bf16[9,32,8,32]{3,2,1,0:T(8,128)(2,1)}, u32[]{:S(2)}) copy-start(bf16[9,32,8,32]{3,2,1,0:T(8,128)(2,1)} %ks_v.1) | copy-start | bytes 442372
  4.5 2.0 %copy-start.3 = (bf16[128,8,64]{0,2,1:T(8,128)(2,1)S(1)}, bf16[128,8,64]{0,2,1:T(8,128)(2,1)}, u32[]{:S(2)}) copy-start(bf16[128,8,64]{0,2,1:T(8,128)(2,1)} %param.18) | copy-start | bytes 393220
  4.5 2.0 %copy-start.4 = (bf16[32,8,128]{2,1,0:T(8,128)(2,1)S(1)}, bf16[32,8,128]{2,1,0:T(8,128)(2,1)}, u32[]{:S(2)}) copy-start(bf16[32,8,128]{2,1,0:T(8,128)(2,1)} %kw_ref.1) | copy-start | bytes 196612
  4.5 2.0 %copy-start.5 = (f32[32]{0:T(128)S(1)}, f32[32]{0:T(128)}, u32[]{:S(2)}) copy-start(f32[32]{0:T(128)} %param.15) | copy-start | bytes 388
  4.5 2.0 %copy-start.6 = (f32[128]{0:T(128)S(1)}, f32[128]{0:T(128)}, u32[]{:S(2)}) copy-start(f32[128]{0:T(128)} %param.17) | copy-start | bytes 1540
  4.5 2.0 %copy-start.7 = (f32[64]{0:T(128)S(1)}, f32[64]{0:T(128)}, u32[]{:S(2)}) copy-start(f32[64]{0:T(128)} %param.19) | copy-start | bytes 772
  4.5 2.0 %copy-start.8 = (f32[64]{0:T(128)S(1)}, f32[64]{0:T(128)}, u32[]{:S(2)}) copy-start(f32[64]{0:T(128)} %param.21) | copy-start | bytes 772
  5.5 4.9 %collective-permute-start.2 = (bf16[128,256]{1,0:T(8,128)(2,1)S(1)}, bf16[128,256]{1,0:T(8,128)(2,1)S(1)}, u32[]{:S(2)}, u32[]{:S(2)}) collective-permute-start(bf16[128,256]{1,0:T(8,128)(2,1)S(1)} %get-tuple-element.20), channel_id=1, source_target_pairs={{0,16},{1,2},{2,1},{3,4},{4,3},{5,6},{6,5},{7,8},{8,7},{9,10},{10,... | collective-permute-start | bytes 196616 | tf_op jit(solution)/shard_map/ppermute | solution.py:361
  5.6 4.7 %collective-permute-start.3 = (bf16[128,256]{1,0:T(8,128)(2,1)S(1)}, bf16[128,256]{1,0:T(8,128)(2,1)S(1)}, u32[]{:S(2)}, u32[]{:S(2)}) collective-permute-start(bf16[128,256]{1,0:T(8,128)(2,1)S(1)} %get-tuple-element.21), channel_id=1, source_target_pairs={{0,1},{1,0},{2,3},{3,2},{4,5},{5,4},{6,7},{7,6},{8,9},{9,8},{10,11... | collective-permute-start | bytes 196616 | tf_op jit(solution)/shard_map/ppermute | solution.py:362

commit v7 on v6

--- a/solution.py
+++ b/solution.py
@@ -52,13 +52,12 @@
     return blocks
 
 
-def unfold_in(kernel, fields, store):
+def unfold_in(tall_ref, kernel, fields, store):
     inputs = kernel.shape[1]
     base = jnp.concatenate([kernel[(-r) % ORIENT * fields:((-r) % ORIENT + 1) * fields] for r in range(ORIENT)], 0)
     base, other = base.T, rows_rolled(base, fields).T
     for first in range(0, inputs * ORIENT, 128):
-        lead = iota((128, inputs), 0) + first - ORIENT * iota((128, inputs), 1)
-        hot = jnp.where(lead & -ORIENT == 0, 1.0, 0.0).astype(BF16)
+        hot = tall_ref[pl.ds(first, 128), :]
         row = iota((128, fields * ORIENT), 0)
         block = jnp.where(row & 1 != 0, dot(hot, other), dot(hot, base))
         for bit in (2, 4):
@@ -100,21 +99,28 @@
     return copies
 
 
-def load_kernel(x_hbm, last_ref, sem):
+def load_kernel(x_hbm, last_ref, order_ref, tall_ref, flat_ref, sem):
     cols = last_ref.shape[0]
     copy = pltpu.make_async_copy(x_hbm.at[pl.ds(x_hbm.shape[0] - cols, cols)], last_ref, sem)
     copy.start()
+    s4 = order_ref.shape[0]
+    s4_f = s4 // ORIENT
+    a, b = iota((s4, s4), 0), iota((s4, s4), 1)
+    order_ref[...] = jnp.where(b == (a & (s4_f - 1)) * ORIENT + (a >> s4_f.bit_length() - 1), 1.0, 0.0).astype(BF16)
+    flat_ref[...] = spread(flat_ref.shape[0], 0, flat_ref.shape[1])
+    lead = iota(tall_ref.shape, 0) - ORIENT * iota(tall_ref.shape, 1)
+    tall_ref[...] = jnp.where(lead & -ORIENT == 0, 1.0, 0.0).astype(BF16)
     copy.wait()
 
 
-def reducing(xs_ref, kr_ref, br_ref, wr_ref, bias_ref, mids_ref, first_ref, second_ref):
+def reducing(tall_ref, xs_ref, kr_ref, br_ref, wr_ref, bias_ref, mids_ref, first_ref, second_ref):
     cols = first_ref.shape[0]
     strips = xs_ref.shape[0] // cols
     even = lax.axis_index("rows") % 2 == 0
     _, mid_f, in_f = kr_ref.shape
     def keep(at, block):
         wr_ref[at, :] = block
-    unfold_in(kr_ref[...].reshape(mid_f * ORIENT, in_f), mid_f, keep)
+    unfold_in(tall_ref, kr_ref[...].reshape(mid_f * ORIENT, in_f), mid_f, keep)
     bias = bias_lanes(br_ref[...], tile_hot(mid_f, mid_f * ORIENT))
     bias_ref[...] = bias
     y = jnp.maximum(dot(xs_ref[...], wr_ref[...]) + bias, 0.0)
@@ -165,8 +171,8 @@
                 phases[pl.ds(strip * half, half), pl.ds(n * s4 + g * 128, 128)] = value.astype(BF16)
 
 
-def inner_kernel(xs_ref, mids_ref, bs_ref, bw_ref, be_ref, bt_ref, ks_v, kw_ref, ke_ref, kt_v,
-                 three_ref, ws_ref, ww_ref, we_ref, k2_ref, b_mid_ref, b_wid_ref, b_ent_ref, b_str_ref, order_ref, phases_ref,
+def inner_kernel(tall_ref, flat_ref, xs_ref, mids_ref, bs_ref, bw_ref, be_ref, bt_ref, ks_v, kw_ref, ke_ref, kt_v,
+                 three_ref, ws_ref, ww_ref, we_ref, k2_ref, b_mid_ref, b_wid_ref, b_ent_ref, b_str_ref, phases_ref,
                  flat_w, flat_s, flat_t, threes, fours, sem):
     in_f, s4_f, mid_f = ke_ref.shape[2], ke_ref.shape[1], kw_ref.shape[0]
     wide, s4, mid = in_f * ORIENT, s4_f * ORIENT, mid_f * ORIENT
@@ -174,20 +180,17 @@
     strips = xs_ref.shape[0] // cols
     flat_w[...] = kw_ref[...].astype(F32).reshape(mid, in_f)
     kw = jnp.concatenate([flat_w[pl.ds(u, mid_f, stride=ORIENT), :] for u in range(ORIENT)], 0).astype(BF16)
-    shift = s4_f.bit_length() - 1
-    a, b = iota((s4, s4), 0), iota((s4, s4), 1)
-    order_ref[...] = jnp.where(b == (a & (s4_f - 1)) * ORIENT + (a >> shift), 1.0, 0.0).astype(BF16)
     hot_s4 = tile_hot(s4_f, s4)
     b_mid_ref[...] = bias_lanes(bs_ref[...], tile_hot(mid_f, mid))
     b_ent_ref[...] = bias_lanes(be_ref[...], hot_s4)
     b_str_ref[...] = bias_lanes(bt_ref[...], hot_s4)
     for first in range(0, wide, 256):
-        hot = spread(in_f, first, 256)
+        hot = flat_ref[:, pl.ds(first, 256)]
         ww_ref[:, pl.ds(first, 256)] = turned(dot(kw, hot), mid_f).astype(BF16)
         b_wid_ref[:, pl.ds(first, 256)] = bias_lanes(bw_ref[...], hot)
     def keep(at, block):
         we_ref[at, :] = block
-    unfold_in(ke_ref[...].reshape(s4, in_f), s4_f, keep)
+    unfold_in(tall_ref, ke_ref[...].reshape(s4, in_f), s4_f, keep)
 
     lane = iota((1, 128), 1)
     for tap in range(9):
@@ -226,8 +229,8 @@
     out.wait()
 
 
-def edge_kernel(last_ref, beside_ref, first_ref, second_ref, xs_ref, wr_ref, bias_ref, mids_ref, ws_ref, ww_ref, we_ref, k2_ref,
-                b_mid_ref, b_wid_ref, b_ent_ref, b_str_ref, order_ref, inner_ref, kept_ref,
+def edge_kernel(last_ref, beside_ref, first_ref, second_ref, xs_ref, wr_ref, bias_ref, order_ref, mids_ref, ws_ref, ww_ref, we_ref, k2_ref,
+                b_mid_ref, b_wid_ref, b_ent_ref, b_str_ref, inner_ref, kept_ref,
                 three_ref, four_ref, halo, line, threes, fours, phases, sem):
     place, count = lax.axis_index("rows"), lax.axis_size("rows")
     even = lax.axis_index("rows") % 2 == 0
@@ -330,11 +333,16 @@
     pinned = lambda *arrays: [pltpu.with_memory_space_constraint(a, pltpu.HBM) for a in arrays]
     scene = scene_map.reshape(own, wide)
     work = lambda flops: pl.CostEstimate(flops=flops, transcendentals=0, bytes_accessed=1 << 22)
-    last = pl.pallas_call(
+    last, order, tall, wide_hot = pl.pallas_call(
         load_kernel,
-        out_shape=pltpu.VMEM((cols, wide), BF16),
+        out_shape=[
+            pltpu.VMEM((cols, wide), BF16),
+            pltpu.VMEM((s4, s4), BF16),
+            pltpu.VMEM((wide, wide // ORIENT), BF16),
+            pltpu.VMEM((wide // ORIENT, wide), BF16),
+        ],
         in_specs=[hbm],
-        out_specs=vmem,
+        out_specs=[vmem] * 4,
         scratch_shapes=[dma],
         cost_estimate=work(2 * 10**9),
         compiler_params=limit(16),
@@ -352,12 +360,12 @@
             pltpu.VMEM((cols, mid), BF16),
             pltpu.VMEM((cols, mid), BF16),
         ],
-        in_specs=[vmem] * 3,
+        in_specs=[vmem] * 4,
         out_specs=[vmem] * 5,
         cost_estimate=work(2 * 10**9),
         compiler_params=limit(16),
         name="reduce",
-    )(scene, reduce_kernel.transpose(1, 2, 0), reduce_bias[None])
+    )(tall, scene, reduce_kernel.transpose(1, 2, 0), reduce_bias[None])
     first = lax.ppermute(first, ("groups", "rows"), far)
     second = lax.ppermute(second, ("groups", "rows"), near)
 
@@ -373,11 +381,10 @@
             pltpu.VMEM((1, wide), F32),
             pltpu.VMEM((1, s4), F32),
             pltpu.VMEM((1, s4), F32),
-            pltpu.VMEM((s4, s4), BF16),
             pltpu.VMEM(((strips - 2) * half, 3 * s4), BF16),
         ],
-        in_specs=[vmem] * 10,
-        out_specs=[hbm] + [vmem] * 10,
+        in_specs=[vmem] * 12,
+        out_specs=[hbm] + [vmem] * 9,
         scratch_shapes=[
             pltpu.VMEM((mid, wide // ORIENT), F32),
             pltpu.VMEM((9 * mid, 128), F32),
@@ -388,9 +395,9 @@
         ],
         compiler_params=limit(28),
         name="inner",
-    )(scene, mids, spatial_bias[None], widen_bias[None], entry_bias[None], stride_bias[None], spatial_kernel, widen_kernel, entry_kernel.transpose(1, 2, 0), stride_kernel)
-
-    operands = [last, beside, first, second, scene, w_reduce, b_reduce, mids, *kept, phases, three]
+    )(tall, wide_hot, scene, mids, spatial_bias[None], widen_bias[None], entry_bias[None], stride_bias[None], spatial_kernel, widen_kernel, entry_kernel.transpose(1, 2, 0), stride_kernel)
+
+    operands = [last, beside, first, second, scene, w_reduce, b_reduce, order, mids, *kept, phases, three]
     three, four = pl.pallas_call(
         edge_kernel,
         out_shape=[

time: 13.7 us -> 13.3 us (0.971)
  the two profiles are of different devices: /device:TPU:1 before, /device:TPU:17 now
where the time goes in v7:
time: 13.3 us; the launch traced here: 13.1 us
  Pallas kernels  8.4 us (63%)
  starting transfers between devices  3.53 us (27%)
  between operations  0.78 us (6%)
  waiting for transfers between devices  0.36 us (3%)
    pallas_call x1, Pallas kernels, shards(): pl.pallas_call(inner_kernel, out_shape=[jax.ShapeDtypeStruct((own, wide),...  3.26 us
    pallas_call x1, Pallas kernels, shards(): pl.pallas_call(edge_kernel, out_shape=[jax.ShapeDtypeStruct((own, wide),...  3.18 us
    ppermute x1, starting transfers between devices, shards(): last = lax.ppermute(last, 'rows', odd_down(count))  1.17 us
    ppermute x1, starting transfers between devices, shards(): second = lax.ppermute(second, ('groups', 'rows'), near)  1.06 us
    pallas_call x1, Pallas kernels, shards(): pl.pallas_call(load_kernel, out_shape=[pltpu.VMEM((cols, wide), BF16), pl...  1.05 us
    pallas_call x1, Pallas kernels, shards(): pl.pallas_call(reducing, out_shape=[pltpu.VMEM((wide, mid), BF16), pltpu....  0.91 us
    ppermute x1, starting transfers between devices, shards(): beside = lax.ppermute(last, ('groups', 'rows'), near)  0.74 us
    ppermute x1, starting transfers between devices, shards(): first = lax.ppermute(first, ('groups', 'rows'), far)  0.56 us
  transfers between devices with their start and end apart: 4, of which 1 were waited for; matrix products, arithmetic and copies ran while one was open for 0% of the time, Pallas kernels for 32%

profile of v7, /device:TPU:17, one launch (start us, length us, event | category | flops | bytes accessed | tf_op | source)
XLA Modules:
  0.0 13.1 jit_solution(12954741875796842611)
XLA Ops:
  0.6 0.0 copy-start
  0.6 0.0 copy-start.9
  0.6 0.0 copy-start.10
  0.7 1.0 %load.1 = (bf16[128,1024]{1,0:T(8,128)(2,1)S(1)}, bf16[512,512]{1,0:T(8,128)(2,1)S(1)}, bf16[1024,128]{1,0:T(8,128)(2,1)S(1)}, bf16[128,1024]{1,0:T(8,128)(2,1)S(1)}) custom-call(bf16[512,1024]{1,0:T(8,128)(2,1)} %bitcast.10), custom_call_target="tpu_custom_call" | custom-call | flops 2000000000 | bytes 4194304 | tf_op jit(solution)/shard_map/load/pallas_call | solution.py:336
  1.7 0.7 %collective-permute-start.1 = (bf16[128,1024]{1,0:T(8,128)(2,1)S(1)}, bf16[128,1024]{1,0:T(8,128)(2,1)S(1)}, u32[]{:S(2)}, u32[]{:S(2)}) collective-permute-start(bf16[128,1024]{1,0:T(8,128)(2,1)S(1)} %get-tuple-element.23), channel_id=1, source_target_pairs={{0,1},{1,0},{2,3},{3,2},{4,5},{5,4},{6,7},{7,6},{8,9},{9,8},{10,11... | collective-permute-start | bytes 786440 | tf_op jit(solution)/shard_map/ppermute | solution.py:352
  2.5 1.2 %collective-permute-start = (bf16[128,1024]{1,0:T(8,128)(2,1)S(1)}, bf16[128,1024]{1,0:T(8,128)(2,1)S(1)}, u32[]{:S(2)}, u32[]{:S(2)}) collective-permute-start(bf16[128,1024]{1,0:T(8,128)(2,1)S(1)} %get-tuple-element.23), channel_id=1, source_target_pairs={{0,1},{1,2},{2,0},{3,4},{4,5},{5,6},{6,3},{7,8},{8,9},{9,10},{10,7... | collective-permute-start | bytes 786440 | tf_op jit(solution)/shard_map/ppermute | solution.py:353
  3.6 0.0 copy-start.2
  3.7 0.0 copy-start.3
  3.7 0.0 copy-start.4
  3.7 0.0 copy-start.5
  3.7 0.0 copy-start.6
  3.7 0.0 copy-start.7
  3.7 0.0 copy-start.8
  3.7 0.9 %reduce.1 = (bf16[1024,256]{1,0:T(8,128)(2,1)S(1)}, f32[1,256]{1,0:T(1,128)S(1)}, bf16[512,768]{1,0:T(8,128)(2,1)S(1)}, bf16[128,256]{1,0:T(8,128)(2,1)S(1)}, bf16[128,256]{1,0:T(8,128)(2,1)S(1)}) custom-call(bf16[1024,128]{1,0:T(8,128)(2,1)S(1)} %get-tuple-element.24.tall_ref, bf16[512,1024]{1,0:T(8,128)(2,1)S(1)} %bitcast.11, ...), custom_call_target="tpu_custom_call" | custom-call | flops 2000000000 | bytes 4194304 | tf_op jit(solution)/shard_map/reduce/pallas_call | solution.py:354
  4.6 0.6 %collective-permute-start.2 = (bf16[128,256]{1,0:T(8,128)(2,1)S(1)}, bf16[128,256]{1,0:T(8,128)(2,1)S(1)}, u32[]{:S(2)}, u32[]{:S(2)}) collective-permute-start(bf16[128,256]{1,0:T(8,128)(2,1)S(1)} %get-tuple-element.25), channel_id=1, source_target_pairs={{0,16},{1,2},{2,1},{3,4},{4,3},{5,6},{6,5},{7,8},{8,7},{9,10},{10,... | collective-permute-start | bytes 196616 | tf_op jit(solution)/shard_map/ppermute | solution.py:369
  5.2 1.1 %collective-permute-start.3 = (bf16[128,256]{1,0:T(8,128)(2,1)S(1)}, bf16[128,256]{1,0:T(8,128)(2,1)S(1)}, u32[]{:S(2)}, u32[]{:S(2)}) collective-permute-start(bf16[128,256]{1,0:T(8,128)(2,1)S(1)} %get-tuple-element.26), channel_id=1, source_target_pairs={{0,1},{1,0},{2,3},{3,2},{4,5},{5,4},{6,7},{7,6},{8,9},{9,8},{10,11... | collective-permute-start | bytes 196616 | tf_op jit(solution)/shard_map/ppermute | solution.py:370
  6.3 0.0 copy-done.1
  6.3 0.0 copy-done.3
  6.3 3.3 %inner.1 = (bf16[512,1024]{1,0:T(8,128)(2,1)}, bf16[2304,256]{1,0:T(8,128)(2,1)S(1)}, bf16[256,1024]{1,0:T(8,128)(2,1)S(1)}, bf16[1024,512]{1,0:T(8,128)(2,1)S(1...) custom-call(bf16[1024,128]{1,0:T(8,128)(2,1)S(1)} %get-tuple-element, ...), custom_call_target="tpu_custom_call" | custom-call | tf_op jit(solution)/shard_map/inner/pallas_call | solution.py:372
  9.6 0.4 %collective-permute-done.2.first_ref = bf16[128,256]{1,0:T(8,128)(2,1)S(1)} collective-permute-done((bf16[128,256]{1,0:T(8,128)(2,1)S(1)}, bf16[128,256]{1,0:T(8,128)(2,1)S(1)}, u32[]{:S(2)}, u32[]{:S(2)}) %collective-permute-start.2) | collective-permute-done | bytes 65568 | tf_op jit(solution)/shard_map/ppermute | solution.py:369
  9.9 0.0 collective-permute-done.3.second_ref
  9.9 0.0 collective-permute-done.1.beside_ref
  9.9 0.0 collective-permute-done.last_ref
  10.0 3.2 %edge.1 = (bf16[512,1024]{1,0:T(8,128)(2,1)}, bf16[128,512]{1,0:T(8,128)(2,1)}) custom-call(bf16[128,1024]{1,0:T(8,128)(2,1)S(1)} %collective-permute-done.last_ref, bf16[128,1024]{1,0:T(8,128)(2,1)S(1)} %collective-permute-done.1.beside_ref, bf16[128,256]{1,0:T(8,128)(2,1)S(1)} %collective-permute-done.2.first_ref, ...), custom_call_target="tpu_custom_call", output_to_operand_aliasing={{0}: (18, {})} | custom-call | tf_op jit(solution)/shard_map/edge/pallas_call | solution.py:401
  (10 shorter events, 0.0 us)
Async XLA Ops:
  0.6 3.0 %copy-start = (bf16[4,128,1024]{2,1,0:T(8,128)(2,1)S(1)}, bf16[4,128,1024]{2,1,0:T(8,128)(2,1)}, u32[]{:S(2)}) copy-start(bf16[4,128,1024]{2,1,0:T(8,128)(2,1)} %param.11) | copy-start | bytes 3145732
  0.6 3.0 %copy-start.9 = (bf16[128,8,32]{0,2,1:T(8,128)(2,1)S(1)}, bf16[128,8,32]{0,2,1:T(8,128)(2,1)}, u32[]{:S(2)}) copy-start(bf16[128,8,32]{0,2,1:T(8,128)(2,1)} %param.12) | copy-start | bytes 196612
  0.6 3.0 %copy-start.10 = (f32[32]{0:T(128)S(1)}, f32[32]{0:T(128)}, u32[]{:S(2)}) copy-start(f32[32]{0:T(128)} %param.13) | copy-start | bytes 388
  1.7 8.2 %collective-permute-start.1 = (bf16[128,1024]{1,0:T(8,128)(2,1)S(1)}, bf16[128,1024]{1,0:T(8,128)(2,1)S(1)}, u32[]{:S(2)}, u32[]{:S(2)}) collective-permute-start(bf16[128,1024]{1,0:T(8,128)(2,1)S(1)} %get-tuple-element.23), channel_id=1, source_target_pairs={{0,1},{1,0},{2,3},{3,2},{4,5},{5,4},{6,7},{7,6},{8,9},{9,8},{10,11... | collective-permute-start | bytes 786440 | tf_op jit(solution)/shard_map/ppermute | solution.py:352
  2.5 7.5 %collective-permute-start = (bf16[128,1024]{1,0:T(8,128)(2,1)S(1)}, bf16[128,1024]{1,0:T(8,128)(2,1)S(1)}, u32[]{:S(2)}, u32[]{:S(2)}) collective-permute-start(bf16[128,1024]{1,0:T(8,128)(2,1)S(1)} %get-tuple-element.23), channel_id=1, source_target_pairs={{0,1},{1,2},{2,0},{3,4},{4,5},{5,6},{6,3},{7,8},{8,9},{9,10},{10,7... | collective-permute-start | bytes 786440 | tf_op jit(solution)/shard_map/ppermute | solution.py:353
  3.6 2.6 %copy-start.1 = (bf16[9,64,8,64]{3,2,1,0:T(8,128)(2,1)S(1)}, bf16[9,64,8,64]{3,2,1,0:T(8,128)(2,1)}, u32[]{:S(2)}) copy-start(bf16[9,64,8,64]{3,2,1,0:T(8,128)(2,1)} %kt_v.1) | copy-start | bytes 1769476
  3.6 2.6 %copy-start.2 = (bf16[9,32,8,32]{3,2,1,0:T(8,128)(2,1)S(1)}, bf16[9,32,8,32]{3,2,1,0:T(8,128)(2,1)}, u32[]{:S(2)}) copy-start(bf16[9,32,8,32]{3,2,1,0:T(8,128)(2,1)} %ks_v.1) | copy-start | bytes 442372
  3.7 2.6 %copy-start.3 = (bf16[128,8,64]{0,2,1:T(8,128)(2,1)S(1)}, bf16[128,8,64]{0,2,1:T(8,128)(2,1)}, u32[]{:S(2)}) copy-start(bf16[128,8,64]{0,2,1:T(8,128)(2,1)} %param.18) | copy-start | bytes 393220
  3.7 2.6 %copy-start.4 = (bf16[32,8,128]{2,1,0:T(8,128)(2,1)S(1)}, bf16[32,8,128]{2,1,0:T(8,128)(2,1)}, u32[]{:S(2)}) copy-start(bf16[32,8,128]{2,1,0:T(8,128)(2,1)} %kw_ref.1) | copy-start | bytes 196612
  3.7 2.6 %copy-start.5 = (f32[32]{0:T(128)S(1)}, f32[32]{0:T(128)}, u32[]{:S(2)}) copy-start(f32[32]{0:T(128)} %param.15) | copy-start | bytes 388
  3.7 2.6 %copy-start.6 = (f32[128]{0:T(128)S(1)}, f32[128]{0:T(128)}, u32[]{:S(2)}) copy-start(f32[128]{0:T(128)} %param.17) | copy-start | bytes 1540
  3.7 2.6 %copy-start.7 = (f32[64]{0:T(128)S(1)}, f32[64]{0:T(128)}, u32[]{:S(2)}) copy-start(f32[64]{0:T(128)} %param.19) | copy-start | bytes 772
  3.7 2.6 %copy-start.8 = (f32[64]{0:T(128)S(1)}, f32[64]{0:T(128)}, u32[]{:S(2)}) copy-start(f32[64]{0:T(128)} %param.21) | copy-start | bytes 772
  4.6 5.3 %collective-permute-start.2 = (bf16[128,256]{1,0:T(8,128)(2,1)S(1)}, bf16[128,256]{1,0:T(8,128)(2,1)S(1)}, u32[]{:S(2)}, u32[]{:S(2)}) collective-permute-start(bf16[128,256]{1,0:T(8,128)(2,1)S(1)} %get-tuple-element.25), channel_id=1, source_target_pairs={{0,16},{1,2},{2,1},{3,4},{4,3},{5,6},{6,5},{7,8},{8,7},{9,10},{10,... | collective-permute-start | bytes 196616 | tf_op jit(solution)/shard_map/ppermute | solution.py:369
  5.2 4.7 %collective-permute-start.3 = (bf16[128,256]{1,0:T(8,128)(2,1)S(1)}, bf16[128,256]{1,0:T(8,128)(2,1)S(1)}, u32[]{:S(2)}, u32[]{:S(2)}) collective-permute-start(bf16[128,256]{1,0:T(8,128)(2,1)S(1)} %get-tuple-element.26), channel_id=1, source_target_pairs={{0,1},{1,0},{2,3},{3,2},{4,5},{5,4},{6,7},{7,6},{8,9},{9,8},{10,11... | collective-permute-start | bytes 196616 | tf_op jit(solution)/shard_map/ppermute | solution.py:370
